TPU v7x, 32 devices: a whole 2x2x4 slice. The times are simulated.
32 devices in a mesh: groups: 2 (over x), ctx: 8 (over z, y), exp: 2 (over core).
Axes of the slice: x: 2, y: 2, z: 4, core: 2. Of those that a mesh axis runs over, the one named last changes fastest.
Arguments:
- x_in: bfloat16 [4096, 2048], P(('groups', 'ctx'), 'exp'), parts along dimension 0, may hold values from -6 to 6
- bc_in: bfloat16 [4096, 2, 512], P(('groups', 'ctx'), None, 'exp'), parts along dimension 0, may hold values from -6 to 6
- z_in: bfloat16 [4096, 2048], P(('groups', 'ctx'), 'exp'), parts along dimension 0, may hold values from -6 to 6
- time_step: float32 [4096, 32], P(('groups', 'ctx'), 'exp'), parts along dimension 0, may hold values from 0.002 to 0.02
- decay_log: float32 [4096, 32], P(('groups', 'ctx'), 'exp'), parts along dimension 0, may hold values from -1 to 0
- conv_inner: bfloat16 [4, 2048], P(None, 'exp'), may hold values from -3 to 3
- conv_bc: bfloat16 [4, 2, 512], P(None, None, 'exp'), may hold values from -3 to 3
- skip_gain: float32 [32], P('exp'), may hold values from 0.5 to 1.5
- start_state: bfloat16 [64, 64, 128], P(('groups', 'exp')), parts along dimension 0, may hold values from -3 to 3
- norm_gain: bfloat16 [2048], P('exp'), may hold values from 0.099609375 to 1.8984375
- out_proj: bfloat16 [2048, 2688], P('exp', 'ctx'), may hold values from -0.125 to 0.125
- residual: bfloat16 [4096, 2688], P(('groups', 'ctx', 'exp')), parts along dimension 0, may hold values from -40 to 40
- moe_gain: bfloat16 [2688], replicated, may hold values from 0.099609375 to 1.8984375
- routes: int32 [4096, 6], P(('groups', 'ctx', 'exp')), parts along dimension 0, may hold values from 0 to 15, all different within a row; in each aligned block of 128 rows (0 to 127, 128 to 255, ...) at most 64 rows name the same one
- gate_weight: float32 [4096, 6], P(('groups', 'ctx', 'exp')), parts along dimension 0, may hold values from 0.1 to 0.4
- up_weight: bfloat16 [16, 2688, 928], P(('ctx', 'exp')), may hold values from -0.125 to 0.125
- down_weight: bfloat16 [16, 928, 2688], P(('ctx', 'exp')), may hold values from -0.1875 to 0.1875
Outputs:
- layer_out: bfloat16 [4096, 2688], P(('groups', 'ctx', 'exp')), parts along dimension 0
There are 2 independent parts, one for each index of `groups`. A program takes and returns all parts, laid end to end along the dimension named above; an argument that names none is the same for every part. Nothing has to cross between parts.
Inputs may be any that keep to these rules, and one draw needn't show every extreme that they name: `routes`: each row names 6 different experts; among the rows of one device (aligned blocks of 128 rows) no expert is named more than 64 times.
All inputs are finite; a program needn't handle non-finite values.
Results may differ from a plain program's by a relative error of at most 0.0056.
Values may be sent and summed in bfloat16 or wider, within the bound.
No kernel may reach another device: no remote copies, remote signals or barrier semaphores. Data moves between devices by JAX's collectives and lax.ppermute only.
A program may use at most 128 MiB of HBM per device.

v0:
```python
import jax
import jax.numpy as jnp
from jax import lax
from jax.sharding import PartitionSpec as P

HEAD_DIM = 64
STATE = 128
KERNEL = 4


EPS = 1e-05
HIGH = lax.Precision.HIGHEST


def from_behind(array, axis, by):
    count = lax.axis_size(axis)
    pairs = [(i, i + by) for i in range(count) if 0 <= i + by < count]
    return lax.ppermute(array, axis, pairs)


def carried_in(array, axis, combine, identity):
    count, index = (lax.axis_size(axis), lax.axis_index(axis))
    everything = jax.tree.map(lambda part: lax.all_gather(part, axis), array)
    start = jax.tree.map(
        lambda part, zero: jnp.broadcast_to(jnp.asarray(zero, part.dtype), part.shape),
        array,
        identity,
    )

    def hop(k, before):
        reached = k < index
        new = combine(before, jax.tree.map(lambda part: part[k], everything))
        return jax.tree.map(lambda a, b: jnp.where(reached, a, b), new, before)

    return lax.fori_loop(0, count, hop, start)


def causal_conv(sequence, previous, taps):
    length = sequence.shape[0]
    padded = jnp.concatenate([previous, sequence], 0).astype(jnp.float32)
    summed = jnp.zeros(sequence.shape, jnp.float32)
    for offset in range(taps.shape[0]):
        summed = summed + taps[offset].astype(jnp.float32) * padded[offset : offset + length]
    return jax.nn.silu(summed).astype(jnp.bfloat16)


def chain_pair(earlier, later):
    return (earlier[0] * later[0], later[0][..., None, None] * earlier[1] + later[1])


def per_device(
    x_in,
    bc_in,
    z_in,
    time_step,
    decay_log,
    conv_inner,
    conv_bc,
    skip_gain,
    start_state,
    norm_gain,
    out_proj,
    residual,
    moe_gain,
    routes,
    gate_weight,
    up_weight,
    down_weight,
):
    block_len = x_in.shape[0]
    local_heads = time_step.shape[1]
    local_groups = bc_in.shape[2] // STATE
    per_group = local_heads // local_groups
    rim_rows = KERNEL - 1
    prev_inner, prev_bc = from_behind(
        (x_in[block_len - rim_rows :], bc_in[block_len - rim_rows :]), "ctx", 1
    )
    inner_act = causal_conv(x_in, prev_inner, conv_inner)
    bc_act = causal_conv(bc_in, prev_bc, conv_bc)
    values = inner_act.astype(jnp.float32).reshape(block_len, local_groups, per_group, HEAD_DIM)
    b_rows = bc_act[:, 0].astype(jnp.float32).reshape(block_len, local_groups, STATE)
    c_rows = bc_act[:, 1].astype(jnp.float32).reshape(block_len, local_groups, STATE)
    log_steps = decay_log.reshape(block_len, local_groups, per_group)
    step_sizes = time_step.reshape(block_len, local_groups, per_group)
    cumulative = jnp.cumsum(log_steps, axis=0)
    block_log = cumulative[block_len - 1]
    to_end = jnp.exp(block_log[None] - cumulative) * step_sizes
    end_state = jnp.einsum("tgrp,tgn->grpn", to_end[..., None] * values, b_rows, precision=HIGH)
    block_decay = jnp.exp(block_log)
    prior_decay, prior_state = carried_in(
        (block_decay, end_state),
        "ctx",
        chain_pair,
        (jnp.ones_like(block_decay), jnp.zeros_like(end_state)),
    )
    entering = (
        prior_decay[..., None, None]
        * start_state.astype(jnp.float32).reshape(local_groups, per_group, HEAD_DIM, STATE)
        + prior_state
    )
    carried = jnp.exp(cumulative)[..., None] * jnp.einsum(
        "tgn,grpn->tgrp", c_rows, entering, precision=HIGH
    )
    scores = jnp.einsum("tgn,sgn->tsg", c_rows, b_rows, precision=HIGH)
    position = jnp.arange(block_len)
    causal = (position[:, None] >= position[None, :])[:, :, None, None]
    spread_log = cumulative[:, None] - cumulative[None, :]
    decay_table = jnp.where(causal, jnp.exp(jnp.where(causal, spread_log, 0.0)), 0.0)
    mix_table = decay_table * step_sizes[None] * scores[..., None]
    local_part = jnp.einsum("tsgr,sgrp->tgrp", mix_table, values, precision=HIGH)
    outputs = (
        carried + local_part + skip_gain.reshape(local_groups, per_group)[None, :, :, None] * values
    )
    gated = outputs.reshape(block_len, local_groups, -1) * jax.nn.silu(
        z_in.astype(jnp.float32).reshape(block_len, local_groups, -1)
    )
    mean_square = jnp.mean(gated * gated, axis=-1, keepdims=True)
    normed = (
        (
            gated
            * lax.rsqrt(mean_square + EPS)
            * norm_gain.astype(jnp.float32).reshape(local_groups, -1)
        )
        .reshape(block_len, -1)
        .astype(jnp.bfloat16)
    )
    partial_out = jnp.dot(
        normed,
        lax.all_gather(out_proj, "ctx", axis=1, tiled=True),
        preferred_element_type=jnp.float32,
    )
    mixed = lax.psum_scatter(partial_out, "exp", scatter_dimension=0, tiled=True)
    hidden_f = (residual.astype(jnp.float32) + mixed).astype(jnp.bfloat16).astype(jnp.float32)
    expert_in = (
        hidden_f
        * lax.rsqrt(jnp.mean(hidden_f * hidden_f, axis=-1, keepdims=True) + EPS)
        * moe_gain.astype(jnp.float32)
    ).astype(jnp.bfloat16)
    tok_rows = routes.shape[0]
    top_count = routes.shape[1]
    model_width = expert_in.shape[1]
    ctx_count = lax.axis_size("ctx")
    exp_count = lax.axis_size("exp")
    experts = ctx_count * exp_count * up_weight.shape[0]
    capacity = max(2, 4 * tok_rows * top_count // (3 * experts))
    flat_ids = routes.reshape(-1)
    one_hot = (flat_ids[:, None] == jnp.arange(experts, dtype=jnp.int32)[None, :]).astype(jnp.int32)
    ranks = jnp.cumsum(one_hot, axis=0) - 1
    slots = jnp.sum(one_hot * ranks, axis=1)
    source_rows = jnp.repeat(jnp.arange(tok_rows, dtype=jnp.int32), top_count)
    send_buffer = (
        jnp.zeros((experts, capacity, model_width), jnp.bfloat16)
        .at[flat_ids, slots]
        .set(expert_in[source_rows])
    )
    arrived = lax.all_to_all(send_buffer, ("ctx", "exp"), split_axis=0, concat_axis=0, tiled=True)
    leading = arrived.shape[:-1]
    flat_rows = arrived.reshape(-1, arrived.shape[-1])
    inner = jnp.dot(flat_rows, up_weight[0], preferred_element_type=jnp.float32)
    inner = jnp.square(jax.nn.relu(inner)).astype(jnp.bfloat16)
    layer_answer = jnp.dot(inner, down_weight[0], preferred_element_type=jnp.float32).astype(
        jnp.bfloat16
    )
    finished = layer_answer.reshape(leading + (arrived.shape[-1],))
    returned = lax.all_to_all(finished, ("ctx", "exp"), split_axis=0, concat_axis=0, tiled=True)
    gathered = returned[flat_ids, slots].reshape(tok_rows, top_count, model_width)
    combined = jnp.sum(gate_weight[..., None] * gathered.astype(jnp.float32), axis=1)
    return (hidden_f + combined).astype(jnp.bfloat16)


def solution(mesh):
    in_specs = (
        P(("groups", "ctx"), "exp"),
        P(("groups", "ctx"), None, "exp"),
        P(("groups", "ctx"), "exp"),
        P(("groups", "ctx"), "exp"),
        P(("groups", "ctx"), "exp"),
        P(None, "exp"),
        P(None, None, "exp"),
        P("exp"),
        P(("groups", "exp"), None, None),
        P("exp"),
        P("exp", "ctx"),
        P(("groups", "ctx", "exp"), None),
        P(),
        P(("groups", "ctx", "exp"), None),
        P(("groups", "ctx", "exp"), None),
        P(("ctx", "exp"), None, None),
        P(("ctx", "exp"), None, None),
    )
    out_specs = P(("groups", "ctx", "exp"), None)
    return jax.shard_map(
        per_device, mesh=mesh, in_specs=in_specs, out_specs=out_specs, check_vma=False
    )
```

profile of v0, /device:TPU:13, one launch (start us, length us, event | category | flops | bytes accessed | tf_op | source)
XLA Modules:
  0.0 684.2 jit_solution(16131043887685088930)
XLA Ops:
  6.5 0.7 slice.88
  7.3 0.2 copy.97
  7.5 3.1 collective-permute-start.1
  10.6 0.7 slice.79
  11.4 3.1 collective-permute-start
  14.5 0.9 slice_convert_fusion.3
  15.4 1.2 reduce-window.14
  16.8 0.2 copy.118
  17.0 0.6 slice_bitcast_fusion
  17.6 0.9 copy.94
  18.5 0.3 bitcast_exponential_fusion
  18.8 0.7 bitcast_convert_fusion.3
  19.5 1.1 copy.98
  20.7 0.2 maximum_convert_fusion.1
  20.9 0.8 multiply_convert_fusion.4
  21.7 0.7 fusion.53
  22.4 0.1 maximum_convert_fusion
  22.6 0.6 multiply_convert_fusion.2
  23.2 0.2 copy.96
  23.4 1.5 fusion.29
  25.0 0.7 all-gather.4.cloned.1.call-update
  25.9 0.2 copy.107
  26.2 0.6 convert_element_type.82
  26.8 10.8 %all_gather.13 = f32[8,2,8]{2,1,0:T(2,128)S(1)} all-gather(f32[1,2,8]{2,1,0:T(2,128)S(1)} %copy-done.10), channel_id=1, replica_groups=mesh['groups'=2,'ctx'=8,'exp'=2] {'ctx'}, dimensions={0}, use_global_device_ids=true | all-gather | bytes 576 | tf_op jit(solution)/shard_map/all_gather | solution.py:23
  37.6 1.2 convolution_bitcast_fusion.1
  38.8 1.0 copy.105
  39.8 5.4 fusion.23
  45.2 51.4 %all-gather.6.cloned.1.call-done = f32[16,8,64,128]{3,2,1,0:T(8,128)} async-done(((f32[2,8,64,128]{3,2,1,0:T(8,128)}), f32[16,8,64,128]{3,2,1,0:T(8,128)}) %all-gather.6.cloned.1.call-update) | async-done | bytes 4194320 | tf_op jit(solution)/shard_map/all_gather | solution.py:23
  96.6 9.7 %while.16 = (s32[]{:T(128)}, f32[2,8]{1,0:T(2,128)S(1)}, f32[2,8,64,128]{3,2,1,0:T(8,128)S(1)}, s32[]{:T(128)}, f32[8,2,8]{2,1,0:T(2,128)S(1)}, /*index=5*/f32[8,2,8,64,128]{4,3,2,1,0:T(8,128)}, s32[]{:T(128)}, s32[]{:T(128)}) while((s32[]{:T(128)}, f32[2,8]{1,0:T(2,128)S(1)}, f32[2,8,64,128]{3,2,1,0:T(8,128)S(1)}, s32[]{:T(128)}, ...), condition=%wide.region_3.4_spmd.clone, body=%wide.region_2.3_spmd.clone.sunk | while | flops 524340 | bytes 1573299 | solution.py:35
  96.6 1.2 fusion.72
  97.8 1.2 fusion.72
  99.0 1.2 fusion.72
  100.2 1.2 fusion.72
  101.4 1.2 fusion.72
  102.7 1.2 fusion.72
  103.9 1.2 fusion.72
  105.1 1.2 fusion.72
  106.3 3.2 multiply_reduce_fusion.1
  109.5 0.1 copy.108
  109.7 0.3 mul.316
  110.0 0.2 copy.126
  110.2 1.6 copy.106
  111.8 74.2 %all-gather.4.cloned.1.call-done = bf16[1024,2688]{0,1:T(8,128)(2,1)} async-done(((bf16[1024,336]{0,1:T(8,128)(2,1)}), bf16[1024,2688]{0,1:T(8,128)(2,1)}) %all-gather.4.cloned.1.call-update) | async-done | bytes 5505040 | tf_op jit(solution)/shard_map/all_gather | solution.py:129
  186.0 6.1 fusion.33
  192.2 0.1 eq.29
  192.4 0.1 eq.25
  192.5 0.1 reshape.203
  192.7 0.1 reshape.205
  192.9 1.7 reduce-window.16
  194.6 0.3 slice_reduce_fusion
  195.0 9.6 %reduce-scatter.2.cloned.1.call-done = f32[128,2688]{1,0:T(8,128)} async-done(((f32[256,2688]{1,0:T(8,128)}), f32[128,2688]{1,0:T(8,128)}) %reduce-scatter.2.cloned.1.call-update) | async-done | bytes 1376272 | tf_op jit(solution)/shard_map/reduce_scatter | solution.py:132
  204.6 1.6 fusion.19
  206.3 0.2 fusion.21
  206.5 4.9 gather_fusion
  211.4 3.0 broadcast_in_dim.27
  214.3 158.4 %scatter_fusion = bf16[16,64,2688]{2,1,0:T(8,128)(2,1)} fusion(bf16[16,64,2688]{2,1,0:T(8,128)(2,1)} %broadcast_in_dim.27, s32[768]{0:T(1024)S(1)} %get-tuple-element.151, bf16[768,2688]{1,0:T(8,128)(2,1)} %gather_fusion), kind=kCustom, calls=%fused_computation.2 | custom fusion | bytes 12392448 | tf_op jit(solution)/shard_map/scatter | solution.py:154
  372.8 126.3 %all_to_all.10 = bf16[16,64,2688]{2,1,0:T(8,128)(2,1)} all-to-all(bf16[16,64,2688]{2,1,0:T(8,128)(2,1)} %scatter_fusion), channel_id=1, replica_groups=mesh['groups'=2,'ctx'=8,'exp'=2] {'ctx','exp'}, dimensions={0} | all-to-all | bytes 11010048 | tf_op jit(solution)/shard_map/all_to_all | solution.py:156
  499.0 18.8 %convolution_convert_fusion = bf16[1024,2688]{1,0:T(8,128)(2,1)} fusion(bf16[1,928,2688]{2,1,0:T(8,128)(2,1)} %param.35, bf16[1024,2688]{1,0:T(8,128)(2,1)} %bitcast.116, bf16[1,2688,928]{1,2,0:T(8,128)(2,1)} %param.34), kind=kOutput, calls=%fused_computation.8 | convolution fusion | flops 10222927872 | bytes 20987904 | tf_op jit(solution)/shard_map/dot_general | solution.py:161
  517.9 5.6 all-to-all-start.1
  523.6 120.5 %all-to-all-done.1 = bf16[16,64,2688]{2,1,0:T(8,128)(2,1)} async-done(((bf16[16,64,2688]{2,1,0:T(8,128)(2,1)}), bf16[16,64,2688]{2,1,0:T(8,128)(2,1)}, u32[]{:S(2)}, u32[]{:S(2)}) %all-to-all-start.1) | async-done | bytes 5505056 | tf_op jit(solution)/shard_map/all_to_all | solution.py:165
  644.1 16.6 %gather_fusion.1 = bf16[768,2688]{1,0:T(8,128)(2,1)} fusion(bf16[16,64,2688]{2,1,0:T(8,128)(2,1)} %all-to-all-done.1, s32[768]{0:T(1024)S(1)} %get-tuple-element.150), kind=kCustom, calls=%fused_computation.1 | custom fusion | bytes 8263680 | tf_op jit(solution)/shard_map/gather | solution.py:166
  660.7 7.9 %reshape.218 = f32[128,6,2688]{2,1,0:T(8,128)} reshape(bf16[768,2688]{1,0:T(8,128)(2,1)} %gather_fusion.1) | data formatting | bytes 12386304 | tf_op jit(solution)/shard_map/convert_element_type | solution.py:167
  668.6 8.1 %multiply_reduce_fusion = f32[128,2688]{1,0:T(8,128)S(1)} fusion(f32[128,6,2688]{2,1,0:T(8,128)} %reshape.218, f32[128,6]{1,0:T(8,128)S(1)} %copy.109), kind=kLoop, calls=%fused_computation.7 | loop fusion | flops 3784704 | bytes 9636864 | tf_op jit(solution)/shard_map/reduce_sum | solution.py:167
  676.7 1.0 fusion.22
  (71 shorter events, 1.5 us)
Async XLA Ops:
  6.5 8.8 %copy-start = (f32[256,16]{0,1:T(8,128)S(1)}, f32[256,16]{0,1:T(8,128)}, u32[]{:S(2)}) copy-start(f32[256,16]{0,1:T(8,128)} %param.23) | copy-start | bytes 49156
  6.5 15.8 %copy-start.3 = (bf16[256,1024]{1,0:T(8,128)(2,1)S(1)}, bf16[256,1024]{1,0:T(8,128)(2,1)}, u32[]{:S(2)}) copy-start(bf16[256,1024]{1,0:T(8,128)(2,1)} %param.19) | copy-start | bytes 1572868
  6.5 90.0 %all-gather.6.cloned.1.call-start = ((), (), s32[]{:S(2)}) async-start(), calls=%async_computation.5 | async-start | bytes 4718592 | tf_op jit(solution)/shard_map/all_gather | solution.py:23
  7.5 13.2 %collective-permute-start.1 = (bf16[3,2,256]{0,2,1:T(8,128)(2,1)S(1)}, bf16[3,2,256]{0,2,1:T(8,128)(2,1)S(1)}, u32[]{:S(2)}, u32[]{:S(2)}) collective-permute-start(bf16[3,2,256]{0,2,1:T(8,128)(2,1)S(1)} %copy.97), channel_id=1, source_target_pairs={{0,2},{2,4},{4,6},{6,8},{8,10},{10,12},{12,14},{1,3},{3,5},{5,7},{... | collective-permute-start | bytes 9224 | tf_op jit(solution)/shard_map/ppermute | solution.py:18
  11.4 11.0 %collective-permute-start = (bf16[3,1024]{1,0:T(4,128)(2,1)S(1)}, bf16[3,1024]{1,0:T(4,128)(2,1)S(1)}, u32[]{:S(2)}, u32[]{:S(2)}) collective-permute-start(bf16[3,1024]{1,0:T(4,128)(2,1)S(1)} %slice.79), channel_id=1, source_target_pairs={{0,2},{2,4},{4,6},{6,8},{8,10},{10,12},{12,14},{1,3},{3,5},{5,7},{... | collective-permute-start | bytes 18440 | tf_op jit(solution)/shard_map/ppermute | solution.py:18
  22.5 3.4 copy-start.4
  22.5 3.6 copy-start.14
  22.5 3.7 copy-start.12
  22.6 4.3 copy-start.10
  23.4 16.4 %copy-start.6 = (f32[256,16]{0,1:T(8,128)S(1)}, f32[256,16]{0,1:T(8,128)}, u32[]{:S(2)}) copy-start(f32[256,16]{0,1:T(8,128)} %param.22) | copy-start | bytes 49156
  24.9 161.1 %all-gather.4.cloned.1.call-start = ((), (), s32[]{:S(2)}) async-start(), calls=%async_computation.3 | async-start | bytes 6193152 | tf_op jit(solution)/shard_map/all_gather | solution.py:129
  25.7 178.9 %reduce-scatter.2.cloned.1.call-start = ((), (), s32[]{:S(2)}) async-start(), calls=%async_computation.4 | async-start | bytes 4128768 | tf_op jit(solution)/shard_map/reduce_scatter | solution.py:132
  45.2 61.1 %copy-start.5 = (bf16[256,1,256]{0,2,1:T(8,128)(2,1)S(1)}, bf16[256,1,256]{0,2,1:T(8,128)(2,1)}, u32[]{:S(2)}) copy-start(bf16[256,1,256]{0,2,1:T(8,128)(2,1)} %get-tuple-element.172) | copy-start | bytes 393220
  45.2 61.1 %copy-start.13 = (bf16[16,64,128]{2,1,0:T(8,128)(2,1)S(1)}, bf16[16,64,128]{2,1,0:T(8,128)(2,1)}, u32[]{:S(2)}) copy-start(bf16[16,64,128]{2,1,0:T(8,128)(2,1)} %param.27) | copy-start | bytes 786436
  109.5 76.5 %copy-start.11 = (f32[1024]{0:T(1024)S(1)}, f32[1024]{0:T(1024)}, u32[]{:S(2)}) copy-start(f32[1024]{0:T(1024)} %convert_element_type.82) | copy-start | bytes 12292
  186.0 6.1 copy-start.8
  186.0 6.7 copy-start.7
  186.0 18.6 %copy-start.2 = (bf16[128,2688]{1,0:T(8,128)(2,1)S(1)}, bf16[128,2688]{1,0:T(8,128)(2,1)}, u32[]{:S(2)}) copy-start(bf16[128,2688]{1,0:T(8,128)(2,1)} %param.30) | copy-start | bytes 2064388
  517.9 5.6 copy-start.9
  517.9 126.2 %all-to-all-start.1 = ((bf16[16,64,2688]{2,1,0:T(8,128)(2,1)}), bf16[16,64,2688]{2,1,0:T(8,128)(2,1)}, u32[]{:S(2)}, u32[]{:S(2)}) async-start(bf16[16,64,2688]{2,1,0:T(8,128)(2,1)} %bitcast.115), calls=%async_computation.2 | async-start | bytes 11010048 | tf_op jit(solution)/shard_map/all_to_all | solution.py:165
  668.6 9.1 %copy-start.1 = (f32[256,16]{0,1:T(8,128)S(1)}, f32[256,16]{0,1:T(8,128)}, u32[]{:S(2)}) copy-start(f32[256,16]{0,1:T(8,128)} %param.23) | copy-start | bytes 49156
Sparse Core Ops, SparseCore 0:
  25.0 71.4 all-gather.5
  98.7 87.2 all-gather.3
  192.2 12.3 reduce-scatter.1
where the time goes:
time: 688 us; the launch traced here: 684 us
  waiting for transfers between devices  256 us (37%)
  local copies, waits for them, and re-layouts  201 us (29%)
  blocking collectives  137 us (20%)
  matrix products  36.1 us (5%)
  other arithmetic  27.9 us (4%)
  between operations  13.5 us (2%)
  starting transfers between devices  12 us (2%)
    scatter x1, local copies, waits for them, and re-layouts, per_device(): send_buffer = jnp.zeros((experts, capacity, model_width), jnp.bfloat16).a...  158 us
    all_to_all x1, blocking collectives, per_device(): lax.all_to_all(send_buffer, ('ctx', 'exp'), split_axis=0, concat_axis=0,...  126 us
    all_to_all x1, waiting for transfers between devices, per_device(): lax.all_to_all(finished, ('ctx', 'exp'), split_axis=0, concat_axis=0, til...  120 us
    all_gather x1, waiting for transfers between devices, per_device(): lax.all_gather(out_proj, 'ctx', axis=1, tiled=True)  74.2 us
    all_gather x1, waiting for transfers between devices, carried_in(): everything = jax.tree.map(lambda part: lax.all_gather(part, axis), array)  51.4 us
    dot_general x1, matrix products, per_device(): jnp.dot(inner, down_weight[0], preferred_element_type=jnp.float32)  18.8 us
    gather x1, local copies, waits for them, and re-layouts, per_device(): returned[flat_ids, slots].reshape(tok_rows, top_count, model_width)  16.6 us
  transfers between devices with their start and end apart: 6, of which 4 were waited for; matrix products, arithmetic and copies ran while one was open for 5% of the time, Pallas kernels for 0%

commit v1 on v0

v1 whole, which is shorter than its diff:
```python
import functools

import jax
import jax.numpy as jnp
from jax import lax
from jax.experimental import pallas as pl
from jax.experimental.pallas import tpu as pltpu
from jax.sharding import PartitionSpec as P

HEAD_DIM = 64
STATE = 128
KERNEL = 4


EPS = 1e-05
HIGH = lax.Precision.HIGHEST
BF16 = jnp.bfloat16
F32 = jnp.float32


def from_behind(array, axis, by):
    count = lax.axis_size(axis)
    pairs = [(i, i + by) for i in range(count) if 0 <= i + by < count]
    return lax.ppermute(array, axis, pairs)


def entering_state(block_log, end_state, start_state):
    count, index = lax.axis_size("ctx"), lax.axis_index("ctx")
    logs = lax.all_gather(block_log, "ctx")
    earlier = (jnp.arange(count) < index).astype(F32)[:, None, None]
    masked = logs * earlier
    after = jnp.flip(jnp.cumsum(jnp.flip(masked, 0), axis=0), 0) - masked
    whole = jnp.sum(masked, axis=0)

    def spread(coefficient):
        return jnp.exp(coefficient)[..., None, None]

    partner = lax.ppermute(
        end_state.astype(BF16), "ctx", [(i, i ^ 1) for i in range(count)]
    ).astype(F32)
    odd = index % 2
    first_log = jnp.where(odd == 1, block_log, lax.dynamic_index_in_dim(logs, index ^ 1, 0, False))
    pair = jnp.where(
        odd == 1,
        spread(first_log) * partner + end_state,
        spread(first_log) * end_state + partner,
    ).astype(BF16)
    entering = spread(whole) * start_state + jnp.where(odd == 1, partner, 0.0)
    half = count // 2

    def after_pair(back):
        place = jnp.maximum((index // 2 - back) * 2 + 1, 0)
        return lax.dynamic_index_in_dim(after, place, 0, False)

    if half <= 4:
        for back in range(half - 1, 0, -1):
            entering = entering + spread(after_pair(back)) * from_behind(
                pair, "ctx", 2 * back
            ).astype(F32)
        return entering
    window = from_behind(pair, "ctx", 2).astype(F32)
    to_start = jnp.where(odd == 1, lax.dynamic_index_in_dim(logs, index ^ 1, 0, False), 0.0)
    back = 1
    while back < half - 1:
        step_log = after_pair(back + 1) - to_start
        window = window + spread(step_log) * from_behind(
            window.astype(BF16), "ctx", 2 * back
        ).astype(F32)
        back *= 2
    return entering + spread(to_start) * window


def causal_conv(sequence, previous, taps):
    length = sequence.shape[0]
    padded = jnp.concatenate([previous, sequence], 0).astype(F32)
    summed = jnp.zeros(sequence.shape, F32)
    for offset in range(taps.shape[0]):
        summed = summed + taps[offset].astype(F32) * padded[offset : offset + length]
    return jax.nn.silu(summed).astype(BF16)


def expert_kernel(cap, tok_rows, pairs, slot_ref, gate_ref, x_ref, up_ref, down_ref, out_ref, sel_ref, ans_ref):
    rows = 2 * cap
    toks = 2 * tok_rows
    def one_hot(i):
        slots = slot_ref[0, :, i * toks : (i + 1) * toks]
        place = lax.broadcasted_iota(jnp.int32, (rows, toks), 0)
        return (place == slots).astype(F32).astype(BF16)

    for i in range(pairs):
        sel_ref[i * rows : (i + 1) * rows, :] = jnp.dot(
            one_hot(i), x_ref[i * toks : (i + 1) * toks, :], preferred_element_type=F32
        ).astype(BF16)
    inner = jnp.dot(sel_ref[...], up_ref[0], preferred_element_type=F32)
    inner = jnp.square(jnp.maximum(inner, 0.0)).astype(BF16)
    ans_ref[...] = jnp.dot(inner, down_ref[0], preferred_element_type=F32).astype(BF16)
    for i in range(pairs):
        spread = lax.dot_general(
            one_hot(i),
            ans_ref[i * rows : (i + 1) * rows, :],
            (((0,), (0,)), ((), ())),
            preferred_element_type=F32,
        )
        out_ref[i * toks : (i + 1) * toks, :] = (
            spread * gate_ref[i * toks : (i + 1) * toks, :]
        ).astype(BF16)


def run_expert(tokens, slots, gates, up_weight, down_weight, cap):
    sources, tok_rows = slots.shape
    width, hidden = up_weight.shape[1:]
    pairs = 2 if cap >= 64 else 4
    step = 2 * pairs
    offset = (jnp.arange(sources, dtype=jnp.int32) % 2 * cap)[:, None]
    slots = jnp.where(slots >= 0, slots + offset, -1).reshape(sources // step, 1, step * tok_rows)
    total = sources * tok_rows
    block = step * tok_rows
    return pl.pallas_call(
        functools.partial(expert_kernel, cap, tok_rows, pairs),
        out_shape=jax.ShapeDtypeStruct((total, width), BF16),
        grid=(sources // step,),
        in_specs=[
            pl.BlockSpec((1, 1, block), lambda i: (i, 0, 0)),
            pl.BlockSpec((block, 1), lambda i: (i, 0)),
            pl.BlockSpec((block, width), lambda i: (i, 0)),
            pl.BlockSpec((1, width, hidden), lambda i: (0, 0, 0), pipeline_mode=pl.Buffered(1)),
            pl.BlockSpec((1, hidden, width), lambda i: (0, 0, 0), pipeline_mode=pl.Buffered(1)),
        ],
        out_specs=pl.BlockSpec((block, width), lambda i: (i, 0)),
        scratch_shapes=[
            pltpu.VMEM((step * cap, width), BF16),
            pltpu.VMEM((step * cap, width), BF16),
        ],
        compiler_params=pltpu.CompilerParams(
            dimension_semantics=("arbitrary",), vmem_limit_bytes=56 << 20
        ),
        cost_estimate=pl.CostEstimate(
            flops=4 * sources * cap * width * hidden,
            bytes_accessed=4 * total * width + 4 * width * hidden,
            transcendentals=0,
        ),
    )(slots, gates.reshape(total, 1), tokens, up_weight, down_weight)


def per_device(
    x_in,
    bc_in,
    z_in,
    time_step,
    decay_log,
    conv_inner,
    conv_bc,
    skip_gain,
    start_state,
    norm_gain,
    out_proj,
    residual,
    moe_gain,
    routes,
    gate_weight,
    up_weight,
    down_weight,
):
    ctx_count = lax.axis_size("ctx")
    exp_count = lax.axis_size("exp")
    exp_index = lax.axis_index("exp")
    block_len = x_in.shape[0]
    local_heads = time_step.shape[1]
    local_groups = bc_in.shape[2] // STATE
    per_group = local_heads // local_groups
    rim_rows = KERNEL - 1
    proj = lax.all_gather(out_proj.T, "ctx", axis=0, tiled=True)

    tok_rows = routes.shape[0]
    top_count = routes.shape[1]
    experts = ctx_count * exp_count * up_weight.shape[0]
    capacity = max(2, 4 * tok_rows * top_count // (3 * experts))
    chosen = routes[:, :, None] == jnp.arange(experts, dtype=jnp.int32)[None, None, :]
    dense_gate = jnp.sum(jnp.where(chosen, gate_weight[:, :, None], 0.0), axis=1)
    all_gates = lax.all_gather(dense_gate.T, ("ctx", "exp"), axis=0)
    me = lax.axis_index("ctx") * exp_count + exp_index
    gates = lax.dynamic_index_in_dim(all_gates, me, 1, False)
    member = gates > 0.0
    slots = jnp.where(member, jnp.cumsum(member.astype(jnp.int32), axis=1) - 1, -1)

    prev_inner, prev_bc = from_behind(
        (x_in[block_len - rim_rows :], bc_in[block_len - rim_rows :]), "ctx", 1
    )
    inner_act = causal_conv(x_in, prev_inner, conv_inner)
    bc_act = causal_conv(bc_in, prev_bc, conv_bc)
    values = inner_act.astype(F32).reshape(block_len, local_groups, per_group, HEAD_DIM)
    b_rows = bc_act[:, 0].astype(F32).reshape(block_len, local_groups, STATE)
    c_rows = bc_act[:, 1].astype(F32).reshape(block_len, local_groups, STATE)
    log_steps = decay_log.reshape(block_len, local_groups, per_group)
    step_sizes = time_step.reshape(block_len, local_groups, per_group)
    cumulative = jnp.cumsum(log_steps, axis=0)
    block_log = cumulative[block_len - 1]
    to_end = jnp.exp(block_log[None] - cumulative) * step_sizes
    end_state = jnp.einsum("tgrp,tgn->grpn", to_end[..., None] * values, b_rows, precision=HIGH)
    entering = entering_state(
        block_log,
        end_state,
        start_state.astype(F32).reshape(local_groups, per_group, HEAD_DIM, STATE),
    )
    carried = jnp.exp(cumulative)[..., None] * jnp.einsum(
        "tgn,grpn->tgrp", c_rows, entering, precision=HIGH
    )
    scores = jnp.einsum("tgn,sgn->tsg", c_rows, b_rows, precision=HIGH)
    position = jnp.arange(block_len)
    causal = (position[:, None] >= position[None, :])[:, :, None, None]
    spread_log = cumulative[:, None] - cumulative[None, :]
    decay_table = jnp.where(causal, jnp.exp(jnp.where(causal, spread_log, 0.0)), 0.0)
    mix_table = decay_table * step_sizes[None] * scores[..., None]
    local_part = jnp.einsum("tsgr,sgrp->tgrp", mix_table, values, precision=HIGH)
    outputs = (
        carried + local_part + skip_gain.reshape(local_groups, per_group)[None, :, :, None] * values
    )
    gated = outputs.reshape(block_len, local_groups, -1) * jax.nn.silu(
        z_in.astype(F32).reshape(block_len, local_groups, -1)
    )
    mean_square = jnp.mean(gated * gated, axis=-1, keepdims=True)
    normed = (
        (gated * lax.rsqrt(mean_square + EPS) * norm_gain.astype(F32).reshape(local_groups, -1))
        .reshape(block_len, -1)
        .astype(BF16)
    )

    def projected(part):
        rows = lax.dynamic_slice_in_dim(normed, part * tok_rows, tok_rows, 0)
        return lax.dot_general(rows, proj, (((1,), (1,)), ((), ())), preferred_element_type=F32)

    theirs = lax.ppermute(projected(1 - exp_index), "exp", [(0, 1), (1, 0)])
    mixed = projected(exp_index) + theirs
    hidden_f = (residual.astype(F32) + mixed).astype(BF16).astype(F32)
    expert_in = (
        hidden_f
        * lax.rsqrt(jnp.mean(hidden_f * hidden_f, axis=-1, keepdims=True) + EPS)
        * moe_gain.astype(F32)
    ).astype(BF16)
    tokens = lax.all_gather(expert_in, ("ctx", "exp"), axis=0, tiled=True)
    answers = run_expert(tokens, slots, gates, up_weight, down_weight, capacity)
    combined = lax.psum_scatter(answers, ("ctx", "exp"), scatter_dimension=0, tiled=True)
    return (hidden_f + combined.astype(F32)).astype(BF16)


def solution(mesh):
    in_specs = (
        P(("groups", "ctx"), "exp"),
        P(("groups", "ctx"), None, "exp"),
        P(("groups", "ctx"), "exp"),
        P(("groups", "ctx"), "exp"),
        P(("groups", "ctx"), "exp"),
        P(None, "exp"),
        P(None, None, "exp"),
        P("exp"),
        P(("groups", "exp"), None, None),
        P("exp"),
        P("exp", "ctx"),
        P(("groups", "ctx", "exp"), None),
        P(),
        P(("groups", "ctx", "exp"), None),
        P(("groups", "ctx", "exp"), None),
        P(("ctx", "exp"), None, None),
        P(("ctx", "exp"), None, None),
    )
    out_specs = P(("groups", "ctx", "exp"), None)
    return jax.shard_map(
        per_device, mesh=mesh, in_specs=in_specs, out_specs=out_specs, check_vma=False
    )
```

time: 688 us -> 375 us (0.55)
  local copies, waits for them, and re-layouts: 201 us -> 15.7 us
  blocking collectives: 137 us -> 28.9 us
  Pallas kernels: 0 us -> 23.7 us
  matrix products: 36.1 us -> 18.4 us
  other arithmetic: 27.9 us -> 11.2 us
  waiting for transfers between devices: 256 us -> 247 us
    scatter x1 -> x0, local copies, waits for them, and re-layouts: 158 us -> none  [per_device(): send_buffer = jnp.zeros((experts, capacity, model_width), jnp.bfloat16).a...]
    all_to_all x1 -> x0, blocking collectives: 126 us -> none  [per_device(): lax.all_to_all(send_buffer, ('ctx', 'exp'), split_axis=0, concat_axis=0,...]
    all_to_all x1 -> x0, waiting for transfers between devices: 120 us -> none  [per_device(): lax.all_to_all(finished, ('ctx', 'exp'), split_axis=0, concat_axis=0, til...]
    reduce_scatter x1, waiting for transfers between devices: 9.58 us -> 122 us  [per_device(): lax.psum_scatter(answers, ('ctx', 'exp'), scatter_dimension=0, tiled=True)]
    all_gather x2, waiting for transfers between devices: 126 us -> 101 us  [the longest x1 63.4 us: per_device(): tokens = lax.all_gather(expert_in, ('ctx', 'exp'), axis=0, tiled=True)]
    pallas_call x0 -> x1, Pallas kernels: none -> 23.7 us  [run_expert(): pl.pallas_call(functools.partial(expert_kernel, cap, tok_rows, pairs), ou...]
    gather x2 -> x0, local copies, waits for them, and re-layouts: 21.4 us -> none  [the longest x1 16.6 us: per_device(): returned[flat_ids, slots].reshape(tok_rows, top_count, model_width)]
    all_gather x1 -> x2, blocking collectives: 10.8 us -> 28.9 us  [the longest x1 17.5 us: per_device(): all_gates = lax.all_gather(dense_gate.T, ('ctx', 'exp'), axis=0)]
  transfers between devices with their start and end apart: 6 -> 10, of which waited for: 4 -> 6; matrix products, arithmetic and copies ran while one was open for 5% -> 9% of each run, Pallas kernels for 0% -> 0%
where the time goes in v1:
time: 375 us; the launch traced here: 372 us
  waiting for transfers between devices  247 us (66%)
  blocking collectives  28.9 us (8%)
  Pallas kernels  23.7 us (6%)
  matrix products  18.4 us (5%)
  local copies, waits for them, and re-layouts  15.7 us (4%)
  starting transfers between devices  14 us (4%)
  between operations  13.6 us (4%)
  other arithmetic  11.2 us (3%)
    reduce_scatter x1, waiting for transfers between devices, per_device(): lax.psum_scatter(answers, ('ctx', 'exp'), scatter_dimension=0, tiled=True)  122 us
    all_gather x1, waiting for transfers between devices, per_device(): tokens = lax.all_gather(expert_in, ('ctx', 'exp'), axis=0, tiled=True)  63.4 us
    all_gather x1, waiting for transfers between devices, per_device(): proj = lax.all_gather(out_proj.T, 'ctx', axis=0, tiled=True)  37.4 us
    pallas_call x1, Pallas kernels, run_expert(): pl.pallas_call(functools.partial(expert_kernel, cap, tok_rows, pairs), ou...  23.7 us
    all_gather x1, blocking collectives, per_device(): all_gates = lax.all_gather(dense_gate.T, ('ctx', 'exp'), axis=0)  17.5 us
    ppermute x5, waiting for transfers between devices, from_behind(): return lax.ppermute(array, axis, pairs)  17.1 us
    ppermute x5, starting transfers between devices, from_behind(): return lax.ppermute(array, axis, pairs)  12.2 us
    all_gather x1, blocking collectives, entering_state(): logs = lax.all_gather(block_log, 'ctx')  11.3 us
  transfers between devices with their start and end apart: 10, of which 6 were waited for; matrix products, arithmetic and copies ran while one was open for 9% of the time, Pallas kernels for 0%

profile of v1, /device:TPU:13, one launch (start us, length us, event | category | flops | bytes accessed | tf_op | source)
XLA Modules:
  0.0 372.4 jit_solution(17359947998062774112)
XLA Ops:
  6.5 0.7 all-gather.4.cloned.1.call-update
  7.3 0.0 all-gather.6.cloned.1.call-start
  7.3 0.7 slice.73
  8.0 3.1 collective-permute-start
  11.2 0.7 slice.82
  11.9 0.2 copy.93
  12.1 3.1 collective-permute-start.1
  15.3 1.2 reduce-window.6
  16.4 0.1 slice.92
  16.5 0.1 copy.88
  16.6 0.1 bitcast_bitcast_fusion
  16.7 0.2 fusion.74
  16.9 0.1 copy.91
  17.0 11.3 %all_gather.15 = f32[8,2,8]{2,1,0:T(2,128)S(1)} all-gather(f32[1,2,8]{2,1,0:T(2,128)S(1)} %copy.91), channel_id=1, replica_groups=mesh['groups'=2,'ctx'=8,'exp'=2] {'ctx'}, dimensions={0}, use_global_device_ids=true | all-gather | bytes 576 | tf_op jit(solution)/shard_map/all_gather | solution.py:29
  28.3 0.1 fusion.72
  28.4 0.7 bitcast_convert_fusion.3
  29.2 0.9 slice_convert_fusion.3
  30.0 0.8 fusion.70
  30.9 0.2 copy.94
  31.1 0.2 maximum_convert_fusion.1
  31.3 0.8 multiply_convert_fusion.3
  32.1 0.2 copy-done.3
  32.3 0.1 maximum_convert_fusion
  32.5 0.6 multiply_convert_fusion.2
  33.2 0.0 copy-start.2
  33.2 0.2 copy.92
  33.4 1.4 fusion.75
  34.8 1.2 collective-permute-start.2
  35.9 0.1 mul.353
  36.0 0.2 copy.101
  36.2 0.3 convolution_bitcast_fusion.1
  36.5 1.0 copy.99
  37.5 3.1 collective-permute-done.2
  40.6 1.1 fusion.33
  41.8 3.3 collective-permute-start.5
  45.1 1.8 collective-permute-start.4
  46.9 0.9 collective-permute-start.3
  47.7 4.5 %fusion.16 = f32[256,2,8,64]{0,3,2,1:T(8,128)S(1)} fusion(bf16[256,2,8,64]{0,3,2,1:T(8,128)(2,1)S(1)} %bitcast.105, f32[256,256,2]{1,0,2:T(8,128)} %copy.99, f32[256,2,8]{0,2,1:T(8,128)S(1)} %bitcast.124, f32[256,2,8]{0,2,1:T(8,128)S(1)} %bitcast_bitcast_fusion, pred[256,256]{1,0:T(8,128)(4,1)S(1)} %iota_compare_fusion), kind=kOutput, calls=%fused_computation.20 | convolution fusion | flops 810549248 | bytes 2195456 | tf_op jit(solution)/shard_map/tsgr,sgrp->tgrp/dot_general | solution.py:214
  52.2 17.1 %collective-permute-done.4 = bf16[2,8,64,128]{3,2,1,0:T(8,128)(2,1)S(1)} collective-permute-done((bf16[2,8,64,128]{3,2,1,0:T(8,128)(2,1)S(1)}, bf16[2,8,64,128]{3,2,1,0:T(8,128)(2,1)S(1)}, u32[]{:S(2)}, u32[]{:S(2)}) %collective-permute-start.4) | collective-permute-done | bytes 262176 | tf_op jit(solution)/shard_map/ppermute | solution.py:24
  69.3 3.1 multiply_reduce_fusion.1
  72.5 1.6 copy.100
  74.0 0.1 copy.102
  74.2 0.3 mul.361
  74.5 0.2 copy.116
  74.7 0.4 multiply_convert_fusion.1
  75.2 37.4 %all-gather.4.cloned.1.call-done = bf16[2688,1024]{1,0:T(8,128)(2,1)} async-done(((bf16[336,1024]{1,0:T(8,128)(2,1)}), bf16[2688,1024]{1,0:T(8,128)(2,1)}) %all-gather.4.cloned.1.call-update) | async-done | bytes 5505040 | tf_op jit(solution)/shard_map/all_gather | solution.py:172
  112.6 4.4 %fusion.44 = f32[128,2688]{1,0:T(8,128)S(1)} fusion(bf16[2688,1024]{1,0:T(8,128)(2,1)} %all-gather.4.cloned.1.call-done, bf16[256,1024]{1,0:T(8,128)(2,1)S(1)} %multiply_convert_fusion.1, s32[]{:T(128)S(6)} %select_n.109), kind=kOutput, calls=%fused_computation.67 | convolution fusion | flops 704643072 | bytes 7143428 | tf_op jit(solution)/shard_map/dot_general | solution.py:230
  117.0 0.5 collective-permute-start.6
  117.5 2.7 collective-permute-done.6
  120.2 4.8 %multiply_reduce_fusion = (f32[128]{0:T(128)S(1)}, f32[128,2688]{1,0:T(8,128)S(1)}) fusion(f32[128,2688]{1,0:T(8,128)S(1)} %collective-permute-done.6, bf16[2688,1024]{1,0:T(8,128)(2,1)} %all-gather.4.cloned.1.call-done, bf16[256,1024]{1,0:T(8,128)(2,1)S(1)} %multiply_convert_fusion.1, s32[]{:T(128)S(6)} %select_n.108, bf16[128,2688]{1,0:T(8,128)(2,1)} %param.28), kind=kOutput, calls=%fused_computation.19 | convolution fusion | flops 707051392 | bytes 9208324 | tf_op jit(solution)/shard_map/dot_general | solution.py:230
  125.1 1.0 multiply_convert_fusion
  126.1 0.0 all-gather.6.cloned.1.call-update
  126.1 0.0 reduce-scatter.2.cloned.1.call-start
  126.2 17.5 %all-gather = f32[256,128]{1,0:T(8,128)S(1)} all-gather(f32[16,128]{1,0:T(8,128)S(1)} %bitcast.116), channel_id=2, replica_groups=mesh['groups'=2,'ctx'=8,'exp'=2] {'ctx','exp'}, dimensions={0}, use_global_device_ids=true | all-gather | bytes 139264 | tf_op jit(solution)/shard_map/all_gather | solution.py:180
  143.8 0.3 reduce_window_sum.40
  144.1 1.4 copy.104.gate_ref
  145.4 8.1 %copy.105.up_ref = bf16[1,2688,928]{2,1,0:T(8,128)(2,1)} copy(bf16[1,2688,928]{1,2,0:T(8,128)(2,1)} %param.32) | data formatting | bytes 9977856 | tf_op args[15]
  153.5 0.1 add.197
  153.6 0.6 compare_select_fusion.slot_ref
  154.2 63.4 %all-gather.6.cloned.1.call-done.x_ref = bf16[2048,2688]{1,0:T(8,128)(2,1)} async-done(((bf16[128,2688]{1,0:T(8,128)(2,1)}), bf16[2048,2688]{1,0:T(8,128)(2,1)}) %all-gather.6.cloned.1.call-update) | async-done | bytes 11010064 | tf_op jit(solution)/shard_map/all_gather | solution.py:240
  217.6 23.7 %shard_map.163 = bf16[2048,2688]{1,0:T(8,128)(2,1)} custom-call(s32[4,1,512]{2,1,0:T(1,128)} %compare_select_fusion.slot_ref, f32[2048,1]{1,0:T(8,128)} %copy.104.gate_ref, bf16[2048,2688]{1,0:T(8,128)(2,1)} %all-gather.6.cloned.1.call-done.x_ref, bf16[1,2688,928]{2,1,0:T(8,128)(2,1)} %copy.105.up_ref, bf16[1,928,2688]{2,1,0:T(8,128)(2,1)} %down_ref.1), custom_call_target="tpu_custom_call" | custom-call | flops 10217324544 | bytes 31997952 | tf_op jit(solution)/shard_map/pallas_call | solution.py:118
  241.4 0.0 reduce-scatter.2.cloned.1.call-update
  241.4 122.4 %reduce-scatter.2.cloned.1.call-done = bf16[128,2688]{1,0:T(8,128)(2,1)} async-done(((bf16[2048,2688]{1,0:T(8,128)(2,1)}), bf16[128,2688]{1,0:T(8,128)(2,1)}) %reduce-scatter.2.cloned.1.call-update) | async-done | bytes 688144 | tf_op jit(solution)/shard_map/reduce_scatter | solution.py:242
  363.8 2.1 add_convert_fusion
  (49 shorter events, 0.3 us)
Async XLA Ops:
  6.5 8.7 %copy-start = (f32[256,16]{0,1:T(8,128)S(1)}, f32[256,16]{0,1:T(8,128)}, u32[]{:S(2)}) copy-start(f32[256,16]{0,1:T(8,128)} %param.21) | copy-start | bytes 49156
  6.5 24.3 %copy-start.4 = (bf16[256,2,256]{2,1,0:T(2,128)(2,1)S(1)}, bf16[256,2,256]{2,1,0:T(2,128)(2,1)}, u32[]{:S(2)}) copy-start(bf16[256,2,256]{2,1,0:T(2,128)(2,1)} %param.18) | copy-start | bytes 786436
  6.5 106.0 %all-gather.4.cloned.1.call-start = ((), (), s32[]{:S(2)}) async-start(), calls=%async_computation.1 | async-start | bytes 6193152 | tf_op jit(solution)/shard_map/all_gather | solution.py:172
  7.3 210.4 %all-gather.6.cloned.1.call-start = ((), (), s32[]{:S(2)}) async-start(), calls=%async_computation.2 | async-start | bytes 11698176 | tf_op jit(solution)/shard_map/all_gather | solution.py:240
  8.0 24.1 %collective-permute-start = (bf16[3,1024]{1,0:T(4,128)(2,1)S(1)}, bf16[3,1024]{1,0:T(4,128)(2,1)S(1)}, u32[]{:S(2)}, u32[]{:S(2)}) collective-permute-start(bf16[3,1024]{1,0:T(4,128)(2,1)S(1)} %slice.73), channel_id=1, source_target_pairs={{0,2},{2,4},{4,6},{6,8},{8,10},{10,12},{12,14},{1,3},{3,5},{5,7},{... | collective-permute-start | bytes 18440 | tf_op jit(solution)/shard_map/ppermute | solution.py:24
  12.1 19.0 %collective-permute-start.1 = (bf16[3,2,256]{0,2,1:T(8,128)(2,1)S(1)}, bf16[3,2,256]{0,2,1:T(8,128)(2,1)S(1)}, u32[]{:S(2)}, u32[]{:S(2)}) collective-permute-start(bf16[3,2,256]{0,2,1:T(8,128)(2,1)S(1)} %copy.93), channel_id=1, source_target_pairs={{0,2},{2,4},{4,6},{6,8},{8,10},{10,12},{12,14},{1,3},{3,5},{5,7},{... | collective-permute-start | bytes 9224 | tf_op jit(solution)/shard_map/ppermute | solution.py:24
  31.3 1.0 copy-start.3
  33.1 2.8 copy-start.11
  33.2 2.9 copy-start.9
  33.2 2.9 copy-start.2
  34.8 5.8 %collective-permute-start.2 = (bf16[2,8,64,128]{3,2,1,0:T(8,128)(2,1)}, bf16[2,8,64,128]{3,2,1,0:T(8,128)(2,1)}, u32[]{:S(2)}, u32[]{:S(2)}) collective-permute-start(bf16[2,8,64,128]{3,2,1,0:T(8,128)(2,1)} %get-tuple-element.26), channel_id=1, source_target_pairs={{0,2},{2,0},{4,6},{6,4},{8,10},{10,8},{12,14},{14,12},{1,3},{3,1},... | collective-permute-start | bytes 786440 | tf_op jit(solution)/shard_map/ppermute | solution.py:38
  36.2 11.5 %copy-start.5 = (f32[256,16]{0,1:T(8,128)S(1)}, f32[256,16]{0,1:T(8,128)}, u32[]{:S(2)}) copy-start(f32[256,16]{0,1:T(8,128)} %param.20) | copy-start | bytes 49156
  41.8 10.4 %collective-permute-start.5 = (bf16[2,8,64,128]{3,2,1,0:T(8,128)(2,1)S(1)}, bf16[2,8,64,128]{3,2,1,0:T(8,128)(2,1)S(1)}, u32[]{:S(2)}, u32[]{:S(2)}) collective-permute-start(bf16[2,8,64,128]{3,2,1,0:T(8,128)(2,1)S(1)} %fusion.33), channel_id=1, source_target_pairs={{0,4},{2,6},{4,8},{6,10},{8,12},{10,14},{1,5},{3,7},{5,9},{7,11},{... | collective-permute-start | bytes 786440 | tf_op jit(solution)/shard_map/ppermute | solution.py:24
  45.1 24.2 %collective-permute-start.4 = (bf16[2,8,64,128]{3,2,1,0:T(8,128)(2,1)S(1)}, bf16[2,8,64,128]{3,2,1,0:T(8,128)(2,1)S(1)}, u32[]{:S(2)}, u32[]{:S(2)}) collective-permute-start(bf16[2,8,64,128]{3,2,1,0:T(8,128)(2,1)S(1)} %fusion.33), channel_id=1, source_target_pairs={{0,8},{2,10},{4,12},{6,14},{1,9},{3,11},{5,13},{7,15},{16,24},{18,... | collective-permute-start | bytes 786440 | tf_op jit(solution)/shard_map/ppermute | solution.py:24
  46.9 22.5 %collective-permute-start.3 = (bf16[2,8,64,128]{3,2,1,0:T(8,128)(2,1)S(1)}, bf16[2,8,64,128]{3,2,1,0:T(8,128)(2,1)S(1)}, u32[]{:S(2)}, u32[]{:S(2)}) collective-permute-start(bf16[2,8,64,128]{3,2,1,0:T(8,128)(2,1)S(1)} %fusion.33), channel_id=1, source_target_pairs={{0,12},{2,14},{1,13},{3,15},{16,28},{18,30},{17,29},{19,31}} | collective-permute-start | bytes 786440 | tf_op jit(solution)/shard_map/ppermute | solution.py:24
  47.7 21.6 %copy-start.10 = (bf16[16,64,128]{2,1,0:T(8,128)(2,1)S(1)}, bf16[16,64,128]{2,1,0:T(8,128)(2,1)}, u32[]{:S(2)}) copy-start(bf16[16,64,128]{2,1,0:T(8,128)(2,1)} %param.25) | copy-start | bytes 786436
  75.1 42.3 %copy-start.6 = (bf16[2688]{0:T(1024)(128)(2,1)S(1)}, bf16[2688]{0:T(1024)(128)(2,1)}, u32[]{:S(2)}) copy-start(bf16[2688]{0:T(1024)(128)(2,1)} %param.29) | copy-start | bytes 16132
  117.0 3.2 collective-permute-start.6
  125.0 1.1 copy-start.7
  125.1 1.1 copy-start.8
  126.1 237.7 %reduce-scatter.2.cloned.1.call-start = ((), (), s32[]{:S(2)}) async-start(), calls=%async_computation.3 | async-start | bytes 11698176 | tf_op jit(solution)/shard_map/reduce_scatter | solution.py:242
  241.4 124.5 %copy-start.1 = (f32[256,16]{0,1:T(8,128)S(1)}, f32[256,16]{0,1:T(8,128)}, u32[]{:S(2)}) copy-start(f32[256,16]{0,1:T(8,128)} %param.21) | copy-start | bytes 49156
Sparse Core Ops, SparseCore 0:
  9.5 102.9 all-gather.3
  126.2 91.3 all-gather.5
  241.5 122.2 reduce-scatter.1

commit v2 on v1

--- a/solution.py
+++ b/solution.py
@@ -24,9 +24,8 @@
     return lax.ppermute(array, axis, pairs)
 
 
-def entering_state(block_log, end_state, start_state):
+def entering_state(block_log, logs, end_state, start_state):
     count, index = lax.axis_size("ctx"), lax.axis_index("ctx")
-    logs = lax.all_gather(block_log, "ctx")
     earlier = (jnp.arange(count) < index).astype(F32)[:, None, None]
     masked = logs * earlier
     after = jnp.flip(jnp.cumsum(jnp.flip(masked, 0), axis=0), 0) - masked
@@ -140,6 +139,306 @@
             transcendentals=0,
         ),
     )(slots, gates.reshape(total, 1), tokens, up_weight, down_weight)
+
+
+STEP = 4
+
+
+def pick(cap, slots):
+    place = lax.broadcasted_iota(jnp.int32, (cap, slots.shape[1]), 0)
+    return (place == slots).astype(F32).astype(BF16)
+
+
+def dot_t(a, b):
+    return lax.dot_general(a, b, (((1,), (1,)), ((), ())), preferred_element_type=F32)
+
+
+def spread_rows(one_hot, answers, gate):
+    rows = lax.dot_general(
+        one_hot, answers, (((0,), (0,)), ((), ())), preferred_element_type=F32
+    )
+    return (rows * gate).astype(BF16)
+
+
+def first_up_kernel(cap, toks, sources, *refs):
+    slot_ref, up_hbm = refs[:2]
+    blocks = refs[2 : 2 + sources]
+    out_ref, x_ref, up_ref, sel_ref, sems, up_sem = refs[2 + sources :]
+    width = x_ref.shape[2]
+    i = pl.program_id(0)
+
+    def block_copy(k):
+        return pltpu.make_async_copy(blocks[k], x_ref.at[k], sems.at[k])
+
+    up_copy = pltpu.make_async_copy(up_hbm.at[0, :, pl.ds(0, width)], up_ref, up_sem)
+
+    @pl.when(i == 0)
+    def _():
+        for k in range(sources):
+            block_copy(k).start()
+        up_copy.start()
+
+    for step in range(sources // STEP):
+        @pl.when(i == step)
+        def _():
+            for k in range(step * STEP, (step + 1) * STEP):
+                block_copy(k).wait()
+            if step == 0:
+                up_copy.wait()
+
+    for j in range(STEP):
+        one_hot = pick(cap, slot_ref[0, :, j * toks : (j + 1) * toks])
+        sel_ref[j * cap : (j + 1) * cap, :] = jnp.dot(
+            one_hot, x_ref[i * STEP + j], preferred_element_type=F32
+        ).astype(BF16)
+    out_ref[...] = dot_t(sel_ref[...], up_ref[...])
+
+
+def second_kernel(
+    cap, toks, split, order_ref, slot_ref, gate_ref, part_ref, up_hbm, down_hbm, *refs
+):
+    blocks = refs[:STEP]
+    inner_ref, out_hbm, up_ref, down_ref, sel_ref, ans_ref, buf_ref, w_sems, sems = refs[STEP:]
+    width = up_ref.shape[1]
+    i = pl.program_id(0)
+    last = pl.num_programs(0) - 1
+    now = lax.rem(i, 2)
+    up_copy = pltpu.make_async_copy(up_hbm.at[0, :, pl.ds(split, width)], up_ref, w_sems.at[0])
+    down_copy = pltpu.make_async_copy(
+        down_hbm.at[0, :, pl.ds(split, width)], down_ref, w_sems.at[1]
+    )
+
+    @pl.when(i == 0)
+    def _():
+        up_copy.start()
+        down_copy.start()
+
+    def out_copy(step, slot, j):
+        source = order_ref[step * STEP + j]
+        return pltpu.make_async_copy(
+            buf_ref.at[slot, j],
+            out_hbm.at[pl.ds(pl.multiple_of(source * toks, toks), toks), :],
+            sems.at[slot, j],
+        )
+
+    one_hots = []
+    for j in range(STEP):
+        one_hots.append(pick(cap, slot_ref[0, :, j * toks : (j + 1) * toks]))
+        sel_ref[j * cap : (j + 1) * cap, :] = jnp.dot(
+            one_hots[j], blocks[j][...], preferred_element_type=F32
+        ).astype(BF16)
+
+    @pl.when(i == 0)
+    def _():
+        up_copy.wait()
+
+    inner = part_ref[...] + dot_t(sel_ref[...], up_ref[...])
+    inner = jnp.square(jnp.maximum(inner, 0.0)).astype(BF16)
+    inner_ref[...] = inner
+
+    @pl.when(i == 0)
+    def _():
+        down_copy.wait()
+
+    ans_ref[...] = jnp.dot(inner, down_ref[...], preferred_element_type=F32).astype(BF16)
+
+    @pl.when(i >= 2)
+    def _():
+        for j in range(STEP):
+            out_copy(i - 2, now, j).wait()
+
+    for j in range(STEP):
+        buf_ref[now, j] = spread_rows(
+            one_hots[j],
+            ans_ref[j * cap : (j + 1) * cap, :],
+            gate_ref[j * toks : (j + 1) * toks, :],
+        )
+        out_copy(i, now, j).start()
+
+    @pl.when(i == last)
+    def _():
+        for j in range(STEP):
+            out_copy(i - 1, 1 - now, j).wait()
+            out_copy(i, now, j).wait()
+
+
+def third_kernel(cap, toks, half, slot_ref, gate_ref, inner_ref, down_ref, own_ref, other_ref, ans_ref):
+    ans_ref[...] = jnp.dot(inner_ref[...], down_ref[0], preferred_element_type=F32).astype(BF16)
+
+    def put(out_ref):
+        for j in range(STEP):
+            out_ref[j * toks : (j + 1) * toks, :] = spread_rows(
+                pick(cap, slot_ref[0, :, j * toks : (j + 1) * toks]),
+                ans_ref[j * cap : (j + 1) * cap, :],
+                gate_ref[j * toks : (j + 1) * toks, :],
+            )
+
+    i = pl.program_id(0)
+    pl.when(i < half)(lambda: put(own_ref))
+    pl.when(i >= half)(lambda: put(other_ref))
+
+
+def kernel_params():
+    return pltpu.CompilerParams(dimension_semantics=("arbitrary",), vmem_limit_bytes=56 << 20)
+
+
+def first_up(blocks, slots, up_t, cap):
+    sources, toks = len(blocks), blocks[0].shape[0]
+    width, hidden = blocks[0].shape[1], up_t.shape[1]
+    steps = sources // STEP
+    return pl.pallas_call(
+        functools.partial(first_up_kernel, cap, toks, sources),
+        out_shape=jax.ShapeDtypeStruct((sources * cap, hidden), F32),
+        grid=(steps,),
+        in_specs=[pl.BlockSpec((1, 1, STEP * toks), lambda i: (i, 0, 0))]
+        + [pl.BlockSpec(memory_space=pl.ANY)] * (1 + sources),
+        out_specs=pl.BlockSpec((STEP * cap, hidden), lambda i: (i, 0)),
+        scratch_shapes=[
+            pltpu.VMEM((sources, toks, width), BF16),
+            pltpu.VMEM((hidden, width), BF16),
+            pltpu.VMEM((STEP * cap, width), BF16),
+            pltpu.SemaphoreType.DMA((sources,)),
+            pltpu.SemaphoreType.DMA,
+        ],
+        compiler_params=kernel_params(),
+        cost_estimate=pl.CostEstimate(
+            flops=2 * sources * cap * width * hidden,
+            bytes_accessed=2 * width * (sources * toks + hidden) + 4 * sources * cap * hidden,
+            transcendentals=0,
+        ),
+    )(slots.reshape(steps, 1, STEP * toks), up_t, *blocks)
+
+
+def second_part(tokens, part, order, slots, gates, up_t, down, split, cap):
+    sources, toks = slots.shape
+    width, hidden = tokens.shape[1], up_t.shape[1]
+    steps = sources // STEP
+
+    def source_spec(j):
+        return pl.BlockSpec((toks, width), lambda i, order: (order[i * STEP + j], 0))
+
+    return pl.pallas_call(
+        functools.partial(second_kernel, cap, toks, split),
+        out_shape=(
+            jax.ShapeDtypeStruct((sources * cap, hidden), BF16),
+            jax.ShapeDtypeStruct((sources * toks, width), BF16),
+        ),
+        grid_spec=pltpu.PrefetchScalarGridSpec(
+            num_scalar_prefetch=1,
+            grid=(steps,),
+            in_specs=[
+                pl.BlockSpec((1, 1, STEP * toks), lambda i, order: (i, 0, 0)),
+                pl.BlockSpec((STEP * toks, 1), lambda i, order: (i, 0)),
+                pl.BlockSpec((STEP * cap, hidden), lambda i, order: (i, 0)),
+                pl.BlockSpec(memory_space=pl.ANY),
+                pl.BlockSpec(memory_space=pl.ANY),
+            ]
+            + [source_spec(j) for j in range(STEP)],
+            out_specs=[
+                pl.BlockSpec((STEP * cap, hidden), lambda i, order: (i, 0)),
+                pl.BlockSpec(memory_space=pl.ANY),
+            ],
+            scratch_shapes=[
+                pltpu.VMEM((hidden, width), BF16),
+                pltpu.VMEM((hidden, width), BF16),
+                pltpu.VMEM((STEP * cap, width), BF16),
+                pltpu.VMEM((STEP * cap, width), BF16),
+                pltpu.VMEM((2, STEP, toks, width), BF16),
+                pltpu.SemaphoreType.DMA((2,)),
+                pltpu.SemaphoreType.DMA((2, STEP)),
+            ],
+        ),
+        compiler_params=kernel_params(),
+        cost_estimate=pl.CostEstimate(
+            flops=4 * sources * cap * width * hidden,
+            bytes_accessed=4 * width * (sources * toks + hidden) + 6 * sources * cap * hidden,
+            transcendentals=0,
+        ),
+    )(
+        order,
+        slots.reshape(steps, 1, STEP * toks),
+        gates,
+        part,
+        up_t,
+        down,
+        *([tokens] * STEP),
+    )
+
+
+def third_part(inner, slots, gates, down, width, cap):
+    sources, toks = slots.shape
+    hidden = inner.shape[1]
+    steps = sources // STEP
+    half = steps // 2
+    shape = jax.ShapeDtypeStruct((sources * toks // 2, width), BF16)
+    return pl.pallas_call(
+        functools.partial(third_kernel, cap, toks, half),
+        out_shape=(shape, shape),
+        grid=(steps,),
+        in_specs=[
+            pl.BlockSpec((1, 1, STEP * toks), lambda i: (i, 0, 0)),
+            pl.BlockSpec((STEP * toks, 1), lambda i: (i, 0)),
+            pl.BlockSpec((STEP * cap, hidden), lambda i: (i, 0)),
+            pl.BlockSpec((1, hidden, width), lambda i: (0, 0, 0), pipeline_mode=pl.Buffered(1)),
+        ],
+        out_specs=[
+            pl.BlockSpec((STEP * toks, width), lambda i: (jnp.minimum(i, half - 1), 0)),
+            pl.BlockSpec((STEP * toks, width), lambda i: (jnp.maximum(i - half, 0), 0)),
+        ],
+        scratch_shapes=[pltpu.VMEM((STEP * cap, width), BF16)],
+        compiler_params=kernel_params(),
+        cost_estimate=pl.CostEstimate(
+            flops=2 * sources * cap * width * hidden,
+            bytes_accessed=2 * width * (sources * toks + hidden) + 2 * sources * cap * hidden,
+            transcendentals=0,
+        ),
+    )(slots.reshape(steps, 1, STEP * toks), gates, inner, down)
+
+
+def swap_axis(array, axis):
+    count = lax.axis_size(axis)
+    return lax.ppermute(array, axis, [(i, i ^ 1) for i in range(count)])
+
+
+def along_pairs(array, by):
+    half = lax.axis_size("ctx") // 2
+    pairs = [
+        (2 * i + r, (i + by) % half * 2 + r) for i in range(half) for r in range(2)
+    ]
+    return lax.ppermute(array, "ctx", pairs)
+
+
+def split_experts(expert_in, order, slots, gates, up_weight, down_weight, cap, split):
+    half = lax.axis_size("ctx") // 2
+    toks = expert_in.shape[0]
+    up_t = jnp.swapaxes(up_weight, 1, 2)
+    slots = slots[order]
+    gates = gates[order].reshape(-1, 1)
+    late = lax.all_gather(expert_in[:, split:], ("ctx", "exp"), axis=0, tiled=True)
+    here = [expert_in[:, :split]]
+    shifts = [half // 2] + [s for s in range(1, half) if s != half // 2]
+    come = {s: along_pairs(here[0], s) for s in shifts if s}
+    here += [come[s] for s in range(1, half)]
+    here += [swap_axis(block, "ctx") for block in here]
+    here += [swap_axis(block, "exp") for block in here]
+    part = first_up(here, slots, up_t, cap)
+    inner, answers = second_part(
+        late, part, order, slots, gates, up_t, down_weight, split, cap
+    )
+    late_sum = lax.psum_scatter(answers, ("ctx", "exp"), scatter_dimension=0, tiled=True)
+    own, other = third_part(inner, slots, gates, down_weight, split, cap)
+    mid = half * toks
+    far = own[mid:] + swap_axis(other[mid:], "exp")
+    near = own[:mid] + swap_axis(other[:mid], "exp")
+    total = None
+    for s in shifts + [0]:
+        rows = slice(s * toks, (s + 1) * toks)
+        block = near[rows] + swap_axis(far[rows], "ctx")
+        if s:
+            block = along_pairs(block, -s)
+        block = block.astype(F32)
+        total = block if total is None else total + block
+    return jnp.concatenate([total, late_sum.astype(F32)], axis=1)
 
 
 def per_device(
@@ -177,9 +476,22 @@
     capacity = max(2, 4 * tok_rows * top_count // (3 * experts))
     chosen = routes[:, :, None] == jnp.arange(experts, dtype=jnp.int32)[None, None, :]
     dense_gate = jnp.sum(jnp.where(chosen, gate_weight[:, :, None], 0.0), axis=1)
-    all_gates = lax.all_gather(dense_gate.T, ("ctx", "exp"), axis=0)
-    me = lax.axis_index("ctx") * exp_count + exp_index
-    gates = lax.dynamic_index_in_dim(all_gates, me, 1, False)
+    log_steps = decay_log.reshape(block_len, local_groups, per_group)
+    cumulative = jnp.cumsum(log_steps, axis=0)
+    block_log = cumulative[block_len - 1]
+    table = jnp.concatenate(
+        [dense_gate.T, jnp.pad(block_log.reshape(1, -1), ((0, 0), (0, tok_rows - local_heads)))], 0
+    )
+    tables = lax.all_gather(table, ("ctx", "exp"), axis=0)
+    ctx_index = lax.axis_index("ctx")
+    me = ctx_index * exp_count + exp_index
+    gates = lax.dynamic_index_in_dim(tables, me, 1, False)
+    logs = lax.dynamic_index_in_dim(
+        tables[:, experts, :local_heads].reshape(ctx_count, exp_count, local_groups, per_group),
+        exp_index,
+        1,
+        False,
+    )
     member = gates > 0.0
     slots = jnp.where(member, jnp.cumsum(member.astype(jnp.int32), axis=1) - 1, -1)
 
@@ -191,14 +503,12 @@
     values = inner_act.astype(F32).reshape(block_len, local_groups, per_group, HEAD_DIM)
     b_rows = bc_act[:, 0].astype(F32).reshape(block_len, local_groups, STATE)
     c_rows = bc_act[:, 1].astype(F32).reshape(block_len, local_groups, STATE)
-    log_steps = decay_log.reshape(block_len, local_groups, per_group)
     step_sizes = time_step.reshape(block_len, local_groups, per_group)
-    cumulative = jnp.cumsum(log_steps, axis=0)
-    block_log = cumulative[block_len - 1]
     to_end = jnp.exp(block_log[None] - cumulative) * step_sizes
     end_state = jnp.einsum("tgrp,tgn->grpn", to_end[..., None] * values, b_rows, precision=HIGH)
     entering = entering_state(
         block_log,
+        logs,
         end_state,
         start_state.astype(F32).reshape(local_groups, per_group, HEAD_DIM, STATE),
     )
@@ -237,9 +547,21 @@
         * lax.rsqrt(jnp.mean(hidden_f * hidden_f, axis=-1, keepdims=True) + EPS)
         * moe_gain.astype(F32)
     ).astype(BF16)
-    tokens = lax.all_gather(expert_in, ("ctx", "exp"), axis=0, tiled=True)
-    answers = run_expert(tokens, slots, gates, up_weight, down_weight, capacity)
-    combined = lax.psum_scatter(answers, ("ctx", "exp"), scatter_dimension=0, tiled=True)
+    half = ctx_count // 2
+    if ctx_count % 2 == 0 and 1 < half <= 4 and exp_count == 2:
+        place = jnp.arange(2 * ctx_count, dtype=jnp.int32)
+        back = ctx_index // 2 + half - place % half
+        order = back % half * 4 + (ctx_index + place // half) % 2 * 2 + (
+            exp_index + place // ctx_count
+        ) % 2
+        split = expert_in.shape[1] // 256 * 128
+        combined = split_experts(
+            expert_in, order, slots, gates, up_weight, down_weight, capacity, split
+        )
+    else:
+        tokens = lax.all_gather(expert_in, ("ctx", "exp"), axis=0, tiled=True)
+        answers = run_expert(tokens, slots, gates, up_weight, down_weight, capacity)
+        combined = lax.psum_scatter(answers, ("ctx", "exp"), scatter_dimension=0, tiled=True)
     return (hidden_f + combined.astype(F32)).astype(BF16)
 
 

time: 375 us -> 354 us (0.944)
  waiting for transfers between devices: 247 us -> 205 us
  starting transfers between devices: 14 us -> 35.6 us
  Pallas kernels: 23.7 us -> 36.9 us
  blocking collectives: 28.9 us -> 17.5 us
    ppermute x0 -> x24, waiting for transfers between devices: none -> 116 us  [the longest x6 61.3 us: along_pairs(): return lax.ppermute(array, 'ctx', pairs)]
    reduce_scatter x1, waiting for transfers between devices: 122 us -> 16.7 us  [split_experts(): lax.psum_scatter(answers, ('ctx', 'exp'), scatter_dimension=0, tiled=True)]
    all_gather x1, waiting for transfers between devices: 63.4 us -> 12.2 us  [split_experts(): lax.all_gather(expert_in[:, split:], ('ctx', 'exp'), axis=0, tiled=True)]
    all_gather x1, waiting for transfers between devices: 37.4 us -> 10.9 us  [per_device(): proj = lax.all_gather(out_proj.T, 'ctx', axis=0, tiled=True)]
    ppermute x5, waiting for transfers between devices: 17.1 us -> 41.3 us  [from_behind(): return lax.ppermute(array, axis, pairs)]
    ppermute x0 -> x24, starting transfers between devices: none -> 21.4 us  [the longest x18 13.7 us: swap_axis(): return lax.ppermute(array, axis, [(i, i ^ 1) for i in range(count)])]
    pallas_call x1 -> x3, Pallas kernels: 23.7 us -> 36.9 us  [the longest x1 17.9 us: second_part(): pl.pallas_call(functools.partial(second_kernel, cap, toks, split), out_sh...]
    all_gather x2 -> x1, blocking collectives: 28.9 us -> 17.5 us  [per_device(): tables = lax.all_gather(table, ('ctx', 'exp'), axis=0)]
  transfers between devices with their start and end apart: 10 -> 34, of which waited for: 6 -> 20; matrix products, arithmetic and copies ran while one was open for 9% -> 8% of each run, Pallas kernels for 0% -> 5%
where the time goes in v2:
time: 354 us; the launch traced here: 351 us
  waiting for transfers between devices  205 us (58%)
  Pallas kernels  36.9 us (10%)
  starting transfers between devices  35.6 us (10%)
  matrix products  18.4 us (5%)
  blocking collectives  17.5 us (5%)
  local copies, waits for them, and re-layouts  14.1 us (4%)
  between operations  13.7 us (4%)
  other arithmetic  9.31 us (3%)
    ppermute x6, waiting for transfers between devices, along_pairs(): return lax.ppermute(array, 'ctx', pairs)  61.3 us
    ppermute x18, waiting for transfers between devices, swap_axis(): return lax.ppermute(array, axis, [(i, i ^ 1) for i in range(count)])  54.4 us
    ppermute x5, waiting for transfers between devices, from_behind(): return lax.ppermute(array, axis, pairs)  41.3 us
    pallas_call x1, Pallas kernels, second_part(): pl.pallas_call(functools.partial(second_kernel, cap, toks, split), out_sh...  17.9 us
    all_gather x1, blocking collectives, per_device(): tables = lax.all_gather(table, ('ctx', 'exp'), axis=0)  17.5 us
    reduce_scatter x1, waiting for transfers between devices, split_experts(): lax.psum_scatter(answers, ('ctx', 'exp'), scatter_dimension=0, tiled=True)  16.7 us
    ppermute x18, starting transfers between devices, swap_axis(): return lax.ppermute(array, axis, [(i, i ^ 1) for i in range(count)])  13.7 us
    ppermute x5, starting transfers between devices, from_behind(): return lax.ppermute(array, axis, pairs)  12.4 us
  transfers between devices with their start and end apart: 34, of which 20 were waited for; matrix products, arithmetic and copies ran while one was open for 8% of the time, Pallas kernels for 5%

profile of v2, /device:TPU:13, one launch (start us, length us, event | category | flops | bytes accessed | tf_op | source)
XLA Modules:
  0.0 351.0 jit_solution(4767141542927267622)
XLA Ops:
  6.6 0.7 all-gather.5.cloned.1.call-update
  7.3 0.7 slice.119
  8.1 3.1 collective-permute-start
  11.2 0.7 slice.128
  12.1 3.1 collective-permute-start.1
  15.3 1.2 reduce-window.6
  17.0 0.7 select_reduce_fusion
  17.7 17.5 %all-gather.1 = f32[16,17,128]{2,1,0:T(8,128)S(1)} all-gather(f32[1,17,128]{2,1,0:T(8,128)S(1)} %fusion.54), channel_id=2, replica_groups=mesh['groups'=2,'ctx'=8,'exp'=2] {'ctx','exp'}, dimensions={0}, use_global_device_ids=true | all-gather | bytes 147968 | tf_op jit(solution)/shard_map/all_gather | solution.py:485
  35.2 0.7 copy-done.12
  36.8 0.8 multiply_convert_fusion.3
  38.0 0.6 multiply_convert_fusion.2
  38.8 1.4 fusion.92
  40.2 1.3 collective-permute-start.2
  42.1 1.0 copy.97
  43.1 5.2 %collective-permute-done.2 = bf16[2,8,64,128]{3,2,1,0:T(8,128)(2,1)} collective-permute-done((bf16[2,8,64,128]{3,2,1,0:T(8,128)(2,1)}, bf16[2,8,64,128]{3,2,1,0:T(8,128)(2,1)}, u32[]{:S(2)}, u32[]{:S(2)}) %collective-permute-start.2) | collective-permute-done | bytes 262176 | tf_op jit(solution)/shard_map/ppermute | solution.py:37
  48.3 1.1 fusion.34
  49.4 3.4 collective-permute-start.5
  52.8 1.8 collective-permute-start.4
  54.7 0.9 collective-permute-start.3
  55.5 4.5 %fusion.17 = f32[256,2,8,64]{0,3,2,1:T(8,128)S(1)} fusion(bf16[256,2,8,64]{0,3,2,1:T(8,128)(2,1)S(1)} %bitcast.107, f32[256,256,2]{1,0,2:T(8,128)} %copy.97, f32[256,2,8]{0,2,1:T(8,128)S(1)} %bitcast.126, f32[256,2,8]{0,2,1:T(8,128)S(1)} %bitcast_bitcast_fusion, pred[256,256]{1,0:T(8,128)(4,1)S(1)} %iota_compare_fusion), kind=kOutput, calls=%fused_computation.23 | convolution fusion | flops 810549248 | bytes 2195456 | tf_op jit(solution)/shard_map/tsgr,sgrp->tgrp/dot_general | solution.py:524
  60.0 8.5 %collective-permute-done.5 = bf16[2,8,64,128]{3,2,1,0:T(8,128)(2,1)S(1)} collective-permute-done((bf16[2,8,64,128]{3,2,1,0:T(8,128)(2,1)S(1)}, bf16[2,8,64,128]{3,2,1,0:T(8,128)(2,1)S(1)}, u32[]{:S(2)}, u32[]{:S(2)}) %collective-permute-start.5) | collective-permute-done | bytes 262176 | tf_op jit(solution)/shard_map/ppermute | solution.py:24
  68.5 32.8 %collective-permute-done.4 = bf16[2,8,64,128]{3,2,1,0:T(8,128)(2,1)S(1)} collective-permute-done((bf16[2,8,64,128]{3,2,1,0:T(8,128)(2,1)S(1)}, bf16[2,8,64,128]{3,2,1,0:T(8,128)(2,1)S(1)}, u32[]{:S(2)}, u32[]{:S(2)}) %collective-permute-start.4) | collective-permute-done | bytes 262176 | tf_op jit(solution)/shard_map/ppermute | solution.py:24
  101.3 3.1 multiply_reduce_fusion.1
  104.5 1.6 copy.98
  107.1 10.9 %all-gather.5.cloned.1.call-done = bf16[2688,1024]{1,0:T(8,128)(2,1)} async-done(((bf16[336,1024]{1,0:T(8,128)(2,1)}), bf16[2688,1024]{1,0:T(8,128)(2,1)}) %all-gather.5.cloned.1.call-update) | async-done | bytes 5505040 | tf_op jit(solution)/shard_map/all_gather | solution.py:471
  118.0 4.4 %fusion.45 = f32[128,2688]{1,0:T(8,128)S(1)} fusion(bf16[2688,1024]{1,0:T(8,128)(2,1)} %all-gather.5.cloned.1.call-done, bf16[256,1024]{1,0:T(8,128)(2,1)S(1)} %multiply_convert_fusion.1, s32[]{:T(128)S(6)} %select_n.186), kind=kOutput, calls=%fused_computation.77 | convolution fusion | flops 704643072 | bytes 7143428 | tf_op jit(solution)/shard_map/dot_general | solution.py:540
  123.0 2.7 collective-permute-done.6
  125.7 4.8 %multiply_reduce_fusion = (f32[128]{0:T(128)S(1)}, f32[128,2688]{1,0:T(8,128)S(1)}) fusion(f32[128,2688]{1,0:T(8,128)S(1)} %collective-permute-done.6, bf16[2688,1024]{1,0:T(8,128)(2,1)} %all-gather.5.cloned.1.call-done, bf16[256,1024]{1,0:T(8,128)(2,1)S(1)} %multiply_convert_fusion.1, s32[]{:T(128)S(6)} %select_n.185, bf16[128,2688]{1,0:T(8,128)(2,1)} %param.28), kind=kOutput, calls=%fused_computation.22 | convolution fusion | flops 707051392 | bytes 9208324 | tf_op jit(solution)/shard_map/dot_general | solution.py:540
  130.7 0.8 slice.171
  132.3 3.4 collective-permute-start.8
  135.7 2.6 collective-permute-start.7
  138.3 0.9 constant_dynamic-slice_fusion
  139.1 1.4 collective-permute-done.9.refs_5_
  140.6 2.0 collective-permute-start.17
  143.0 22.7 %collective-permute-done.8.refs_4_ = bf16[128,1280]{1,0:T(8,128)(2,1)S(1)} collective-permute-done((bf16[128,1280]{1,0:T(8,128)(2,1)S(1)}, bf16[128,1280]{1,0:T(8,128)(2,1)S(1)}, u32[]{:S(2)}, u32[]{:S(2)}) %collective-permute-start.8) | collective-permute-done | bytes 327712 | tf_op jit(solution)/shard_map/ppermute | solution.py:408
  165.7 0.9 collective-permute-start.12
  166.6 9.0 %collective-permute-done.7.refs_3_ = bf16[128,1280]{1,0:T(8,128)(2,1)S(1)} collective-permute-done((bf16[128,1280]{1,0:T(8,128)(2,1)S(1)}, bf16[128,1280]{1,0:T(8,128)(2,1)S(1)}, u32[]{:S(2)}, u32[]{:S(2)}) %collective-permute-start.7) | collective-permute-done | bytes 327712 | tf_op jit(solution)/shard_map/ppermute | solution.py:408
  175.6 0.7 collective-permute-start.11
  177.2 0.8 collective-permute-start.16
  178.6 8.5 %collective-permute-done.11.refs_7_ = bf16[128,1280]{1,0:T(8,128)(2,1)} collective-permute-done((bf16[128,1280]{1,0:T(8,128)(2,1)S(1)}, bf16[128,1280]{1,0:T(8,128)(2,1)}, u32[]{:S(2)}, u32[]{:S(2)}) %collective-permute-start.11) | collective-permute-done | bytes 327712 | tf_op jit(solution)/shard_map/ppermute | solution.py:400
  187.1 4.1 %collective-permute-start.19 = (bf16[128,1280]{1,0:T(8,128)(2,1)}, bf16[128,1280]{1,0:T(8,128)(2,1)}, u32[]{:S(2)}, u32[]{:S(2)}) collective-permute-start(bf16[128,1280]{1,0:T(8,128)(2,1)} %collective-permute-done.11.refs_7_), channel_id=1, source_target_pairs={{0,1},{1,0},{2,3},{3,2},{4,5},{5,4},{6,7},{7,6},{8,9},{9,8},{10,11... | collective-permute-start | bytes 983048 | tf_op jit(solution)/shard_map/ppermute | solution.py:400
  191.2 1.1 gather_fusion
  192.4 1.3 copy.102.gate_ref
  194.4 9.7 %shard_map.163.part_ref = f32[1024,928]{1,0:T(8,128)} custom-call(s32[4,1,512]{2,1,0:T(1,128)} %bitcast.117, bf16[1,928,2688]{2,1,0:T(8,128)(2,1)} %bitcast.102, bf16[128,1280]{1,0:T(8,128)(2,1)} %copy-done.4, bf16[128,1280]{1,0:T(8,128)(2,1)} %copy-done.10, bf16[128,1280]{1,0:T(8,128)(2,1)} %copy-done.9, bf16[128,1280]{1,0:T(8,128)(2,1)} %copy-done.6, ...), custom_call_target="tpu_custom_call" | custom-call | flops 2432696320 | bytes 11419648 | tf_op jit(solution)/shard_map/pallas_call | solution.py:289
  204.0 12.2 %all-gather.7.cloned.1.call-done.refs_0_.refs_1_.refs_2_.refs_3_ = bf16[2048,1408]{1,0:T(8,128)(2,1)} async-done(((bf16[128,1408]{1,0:T(8,128)(2,1)}), bf16[2048,1408]{1,0:T(8,128)(2,1)}) %all-gather.7.cloned.1.call-update) | async-done | bytes 5767184 | tf_op jit(solution)/shard_map/all_gather | solution.py:417
  216.3 17.9 %shard_map.164 = (bf16[1024,928]{1,0:T(8,128)(2,1)}, bf16[2048,1408]{1,0:T(8,128)(2,1)}) custom-call(s32[16]{0:T(128)} %fusion.64.order_ref, s32[4,1,512]{2,1,0:T(1,128)} %bitcast.118, f32[2048,1]{1,0:T(8,128)} %copy.102.gate_ref, f32[1024,928]{1,0:T(8,128)} %shard_map.163.part_ref, bf16[1,928,2688]{2,1,0:T(8,128)(2,1)} %bitcast.103, ...), custom_call_target="tpu_custom_call" | custom-call | flops 5351931904 | bytes 22462464 | tf_op jit(solution)/shard_map/pallas_call | solution.py:320
  234.2 9.4 %shard_map.165 = (bf16[1024,1280]{1,0:T(8,128)(2,1)}, bf16[1024,1280]{1,0:T(8,128)(2,1)}) custom-call(s32[4,1,512]{2,1,0:T(1,128)} %bitcast.119, f32[2048,1]{1,0:T(8,128)} %copy.102.gate_ref, bf16[1024,928]{1,0:T(8,128)(2,1)} %get-tuple-element.9.inner_ref, bf16[1,928,2688]{2,1,0:T(8,128)(2,1)} %down_ref.1), custom_call_target="tpu_custom_call" | custom-call | flops 2432696320 | bytes 9519104 | tf_op jit(solution)/shard_map/pallas_call | solution.py:374
  243.6 2.2 fusion.89
  246.4 2.9 collective-permute-done.22
  249.3 2.0 collective-permute-done.23
  251.7 0.6 collective-permute-start.28
  252.2 0.9 collective-permute-start.26
  253.7 0.9 collective-permute-start.30
  254.7 6.1 %collective-permute-done.28 = bf16[128,1280]{1,0:T(8,128)(2,1)S(1)} collective-permute-done((bf16[128,1280]{1,0:T(8,128)(2,1)S(1)}, bf16[128,1280]{1,0:T(8,128)(2,1)S(1)}, u32[]{:S(2)}, u32[]{:S(2)}) %collective-permute-start.28) | collective-permute-done | bytes 327712 | tf_op jit(solution)/shard_map/ppermute | solution.py:400
  260.8 8.4 %collective-permute-done.26 = bf16[128,1280]{1,0:T(8,128)(2,1)S(1)} collective-permute-done((bf16[128,1280]{1,0:T(8,128)(2,1)S(1)}, bf16[128,1280]{1,0:T(8,128)(2,1)S(1)}, u32[]{:S(2)}, u32[]{:S(2)}) %collective-permute-start.26) | collective-permute-done | bytes 327712 | tf_op jit(solution)/shard_map/ppermute | solution.py:400
  269.2 14.0 %collective-permute-done.24 = bf16[128,1280]{1,0:T(8,128)(2,1)S(1)} collective-permute-done((bf16[128,1280]{1,0:T(8,128)(2,1)S(1)}, bf16[128,1280]{1,0:T(8,128)(2,1)S(1)}, u32[]{:S(2)}, u32[]{:S(2)}) %collective-permute-start.24) | collective-permute-done | bytes 327712 | tf_op jit(solution)/shard_map/ppermute | solution.py:400
  283.5 1.4 collective-permute-start.27
  284.9 12.3 %collective-permute-done.30 = bf16[128,1280]{1,0:T(8,128)(2,1)S(1)} collective-permute-done((bf16[128,1280]{1,0:T(8,128)(2,1)S(1)}, bf16[128,1280]{1,0:T(8,128)(2,1)S(1)}, u32[]{:S(2)}, u32[]{:S(2)}) %collective-permute-start.30) | collective-permute-done | bytes 327712 | tf_op jit(solution)/shard_map/ppermute | solution.py:400
  297.3 10.2 %collective-permute-done.25 = bf16[128,1280]{1,0:T(8,128)(2,1)S(1)} collective-permute-done((bf16[128,1280]{1,0:T(8,128)(2,1)S(1)}, bf16[128,1280]{1,0:T(8,128)(2,1)S(1)}, u32[]{:S(2)}, u32[]{:S(2)}) %collective-permute-start.25) | collective-permute-done | bytes 327712 | tf_op jit(solution)/shard_map/ppermute | solution.py:408
  307.5 16.5 %collective-permute-done.29 = bf16[128,1280]{1,0:T(8,128)(2,1)S(1)} collective-permute-done((bf16[128,1280]{1,0:T(8,128)(2,1)S(1)}, bf16[128,1280]{1,0:T(8,128)(2,1)S(1)}, u32[]{:S(2)}, u32[]{:S(2)}) %collective-permute-start.29) | collective-permute-done | bytes 327712 | tf_op jit(solution)/shard_map/ppermute | solution.py:408
  323.9 1.5 collective-permute-done.27
  325.6 16.7 %reduce-scatter.2.cloned.1.call-done = bf16[128,1408]{1,0:T(8,128)(2,1)} async-done(((bf16[2048,1408]{1,0:T(8,128)(2,1)}), bf16[128,1408]{1,0:T(8,128)(2,1)}) %reduce-scatter.2.cloned.1.call-update) | async-done | bytes 360464 | tf_op jit(solution)/shard_map/reduce_scatter | solution.py:428
  342.4 1.0 convert_element_type.128
  343.4 1.0 fusion.16
  (128 shorter events, 9.8 us)
Async XLA Ops:
  6.5 8.7 %copy-start = (f32[256,16]{0,1:T(8,128)S(1)}, f32[256,16]{0,1:T(8,128)}, u32[]{:S(2)}) copy-start(f32[256,16]{0,1:T(8,128)} %param.21) | copy-start | bytes 49156
  6.5 29.7 %copy-start.11 = (bf16[256,2,256]{2,1,0:T(2,128)(2,1)S(1)}, bf16[256,2,256]{2,1,0:T(2,128)(2,1)}, u32[]{:S(2)}) copy-start(bf16[256,2,256]{2,1,0:T(2,128)(2,1)} %param.18) | copy-start | bytes 786436
  6.5 29.5 %copy-start.16 = (bf16[4,2,256]{2,1,0:T(2,128)(2,1)S(1)}, bf16[4,2,256]{2,1,0:T(2,128)(2,1)}, u32[]{:S(2)}) copy-start(bf16[4,2,256]{2,1,0:T(2,128)(2,1)} %param.23) | copy-start | bytes 12292
  6.5 29.6 %copy-start.13 = (bf16[4,1024]{1,0:T(4,128)(2,1)S(1)}, bf16[4,1024]{1,0:T(4,128)(2,1)}, u32[]{:S(2)}) copy-start(bf16[4,1024]{1,0:T(4,128)(2,1)} %param.22) | copy-start | bytes 24580
  6.5 29.6 %copy-start.14 = (f32[256,16]{0,1:T(8,128)S(1)}, f32[256,16]{0,1:T(8,128)}, u32[]{:S(2)}) copy-start(f32[256,16]{0,1:T(8,128)} %param.20) | copy-start | bytes 49156
  6.5 111.5 %all-gather.5.cloned.1.call-start = ((), (), s32[]{:S(2)}) async-start(), calls=%async_computation.1 | async-start | bytes 6193152 | tf_op jit(solution)/shard_map/all_gather | solution.py:471
  7.3 209.0 %all-gather.7.cloned.1.call-start = ((), (), s32[]{:S(2)}) async-start(), calls=%async_computation.2 | async-start | bytes 6127616 | tf_op jit(solution)/shard_map/all_gather | solution.py:417
  8.1 29.5 %collective-permute-start = (bf16[3,1024]{1,0:T(4,128)(2,1)S(1)}, bf16[3,1024]{1,0:T(4,128)(2,1)S(1)}, u32[]{:S(2)}, u32[]{:S(2)}) collective-permute-start(bf16[3,1024]{1,0:T(4,128)(2,1)S(1)} %slice.119), channel_id=1, source_target_pairs={{0,2},{2,4},{4,6},{6,8},{8,10},{10,12},{12,14},{1,3},{3,5},{5,7},{... | collective-permute-start | bytes 18440 | tf_op jit(solution)/shard_map/ppermute | solution.py:24
  12.1 24.5 %collective-permute-start.1 = (bf16[3,2,256]{0,2,1:T(8,128)(2,1)S(1)}, bf16[3,2,256]{0,2,1:T(8,128)(2,1)S(1)}, u32[]{:S(2)}, u32[]{:S(2)}) collective-permute-start(bf16[3,2,256]{0,2,1:T(8,128)(2,1)S(1)} %copy.91), channel_id=1, source_target_pairs={{0,2},{2,4},{4,6},{6,8},{8,10},{10,12},{12,14},{1,3},{3,5},{5,7},{... | collective-permute-start | bytes 9224 | tf_op jit(solution)/shard_map/ppermute | solution.py:24
  35.2 0.7 copy-start.12
  36.8 1.0 copy-start.5
  38.6 2.9 copy-start.19
  38.6 3.0 copy-start.17
  38.6 3.0 copy-start.3
  40.2 8.1 %collective-permute-start.2 = (bf16[2,8,64,128]{3,2,1,0:T(8,128)(2,1)}, bf16[2,8,64,128]{3,2,1,0:T(8,128)(2,1)}, u32[]{:S(2)}, u32[]{:S(2)}) collective-permute-start(bf16[2,8,64,128]{3,2,1,0:T(8,128)(2,1)} %get-tuple-element.43), channel_id=1, source_target_pairs={{0,2},{2,0},{4,6},{6,4},{8,10},{10,8},{12,14},{14,12},{1,3},{3,1},... | collective-permute-start | bytes 786440 | tf_op jit(solution)/shard_map/ppermute | solution.py:37
  49.4 19.1 %collective-permute-start.5 = (bf16[2,8,64,128]{3,2,1,0:T(8,128)(2,1)S(1)}, bf16[2,8,64,128]{3,2,1,0:T(8,128)(2,1)S(1)}, u32[]{:S(2)}, u32[]{:S(2)}) collective-permute-start(bf16[2,8,64,128]{3,2,1,0:T(8,128)(2,1)S(1)} %fusion.34), channel_id=1, source_target_pairs={{0,4},{2,6},{4,8},{6,10},{8,12},{10,14},{1,5},{3,7},{5,9},{7,11},{... | collective-permute-start | bytes 786440 | tf_op jit(solution)/shard_map/ppermute | solution.py:24
  52.8 48.5 %collective-permute-start.4 = (bf16[2,8,64,128]{3,2,1,0:T(8,128)(2,1)S(1)}, bf16[2,8,64,128]{3,2,1,0:T(8,128)(2,1)S(1)}, u32[]{:S(2)}, u32[]{:S(2)}) collective-permute-start(bf16[2,8,64,128]{3,2,1,0:T(8,128)(2,1)S(1)} %fusion.34), channel_id=1, source_target_pairs={{0,8},{2,10},{4,12},{6,14},{1,9},{3,11},{5,13},{7,15},{16,24},{18,... | collective-permute-start | bytes 786440 | tf_op jit(solution)/shard_map/ppermute | solution.py:24
  54.7 46.7 %collective-permute-start.3 = (bf16[2,8,64,128]{3,2,1,0:T(8,128)(2,1)S(1)}, bf16[2,8,64,128]{3,2,1,0:T(8,128)(2,1)S(1)}, u32[]{:S(2)}, u32[]{:S(2)}) collective-permute-start(bf16[2,8,64,128]{3,2,1,0:T(8,128)(2,1)S(1)} %fusion.34), channel_id=1, source_target_pairs={{0,12},{2,14},{1,13},{3,15},{16,28},{18,30},{17,29},{19,31}} | collective-permute-start | bytes 786440 | tf_op jit(solution)/shard_map/ppermute | solution.py:24
  55.5 45.8 %copy-start.18 = (bf16[16,64,128]{2,1,0:T(8,128)(2,1)S(1)}, bf16[16,64,128]{2,1,0:T(8,128)(2,1)}, u32[]{:S(2)}) copy-start(bf16[16,64,128]{2,1,0:T(8,128)(2,1)} %param.25) | copy-start | bytes 786436
  107.1 15.8 %copy-start.15 = (bf16[2688]{0:T(1024)(128)(2,1)S(1)}, bf16[2688]{0:T(1024)(128)(2,1)}, u32[]{:S(2)}) copy-start(bf16[2688]{0:T(1024)(128)(2,1)} %param.29) | copy-start | bytes 16132
  122.4 3.3 collective-permute-start.6
  131.5 210.9 %reduce-scatter.2.cloned.1.call-start = ((), (), s32[]{:S(2)}) async-start(), calls=%async_computation.3 | async-start | bytes 6127616 | tf_op jit(solution)/shard_map/reduce_scatter | solution.py:428
  131.6 62.7 %copy-start.4 = (bf16[128,1280]{1,0:T(8,128)(2,1)}, bf16[128,1280]{1,0:T(8,128)(2,1)S(1)}, u32[]{:S(2)}) copy-start(bf16[128,1280]{1,0:T(8,128)(2,1)S(1)} %slice.170.refs_2_) | copy-start | bytes 983044
  131.6 9.0 %collective-permute-start.9 = (bf16[128,1280]{1,0:T(8,128)(2,1)S(1)}, bf16[128,1280]{1,0:T(8,128)(2,1)S(1)}, u32[]{:S(2)}, u32[]{:S(2)}) collective-permute-start(bf16[128,1280]{1,0:T(8,128)(2,1)S(1)} %slice.170.refs_2_), channel_id=1, source_target_pairs={{0,12},{2,14},{4,0},{6,2},{8,4},{10,6},{12,8},{14,10},{1,13},{3,15... | collective-permute-start | bytes 983048 | tf_op jit(solution)/shard_map/ppermute | solution.py:408
  131.7 10.9 %collective-permute-start.14 = (bf16[128,1280]{1,0:T(8,128)(2,1)S(1)}, bf16[128,1280]{1,0:T(8,128)(2,1)S(1)}, u32[]{:S(2)}, u32[]{:S(2)}) collective-permute-start(bf16[128,1280]{1,0:T(8,128)(2,1)S(1)} %slice.170.refs_2_), channel_id=1, source_target_pairs={{0,1},{1,0},{2,3},{3,2},{4,5},{5,4},{6,7},{7,6},{8,9},{9,8},{10,11... | collective-permute-start | bytes 983048 | tf_op jit(solution)/shard_map/ppermute | solution.py:400
  132.1 10.5 %collective-permute-start.10 = (bf16[128,1280]{1,0:T(8,128)(2,1)S(1)}, bf16[128,1280]{1,0:T(8,128)(2,1)S(1)}, u32[]{:S(2)}, u32[]{:S(2)}) collective-permute-start(bf16[128,1280]{1,0:T(8,128)(2,1)S(1)} %slice.170.refs_2_), channel_id=1, source_target_pairs={{0,2},{2,0},{4,6},{6,4},{8,10},{10,8},{12,14},{14,12},{1,3},{3,1},... | collective-permute-start | bytes 983048 | tf_op jit(solution)/shard_map/ppermute | solution.py:400
  132.3 33.4 %collective-permute-start.8 = (bf16[128,1280]{1,0:T(8,128)(2,1)S(1)}, bf16[128,1280]{1,0:T(8,128)(2,1)S(1)}, u32[]{:S(2)}, u32[]{:S(2)}) collective-permute-start(bf16[128,1280]{1,0:T(8,128)(2,1)S(1)} %slice.170.refs_2_), channel_id=1, source_target_pairs={{0,8},{2,10},{4,12},{6,14},{8,0},{10,2},{12,4},{14,6},{1,9},{3,11}... | collective-permute-start | bytes 983048 | tf_op jit(solution)/shard_map/ppermute | solution.py:408
  135.7 39.9 %collective-permute-start.7 = (bf16[128,1280]{1,0:T(8,128)(2,1)S(1)}, bf16[128,1280]{1,0:T(8,128)(2,1)S(1)}, u32[]{:S(2)}, u32[]{:S(2)}) collective-permute-start(bf16[128,1280]{1,0:T(8,128)(2,1)S(1)} %slice.170.refs_2_), channel_id=1, source_target_pairs={{0,4},{2,6},{4,8},{6,10},{8,12},{10,14},{12,0},{14,2},{1,5},{3,7},... | collective-permute-start | bytes 983048 | tf_op jit(solution)/shard_map/ppermute | solution.py:408
  140.6 53.8 %copy-start.6 = (bf16[128,1280]{1,0:T(8,128)(2,1)}, bf16[128,1280]{1,0:T(8,128)(2,1)S(1)}, u32[]{:S(2)}) copy-start(bf16[128,1280]{1,0:T(8,128)(2,1)S(1)} %collective-permute-done.9.refs_5_) | copy-start | bytes 983044
  140.6 37.4 %collective-permute-start.17 = (bf16[128,1280]{1,0:T(8,128)(2,1)S(1)}, bf16[128,1280]{1,0:T(8,128)(2,1)}, u32[]{:S(2)}, u32[]{:S(2)}) collective-permute-start(bf16[128,1280]{1,0:T(8,128)(2,1)S(1)} %collective-permute-done.9.refs_5_), channel_id=1, source_target_pairs={{0,1},{1,0},{2,3},{3,2},{4,5},{5,4},{6,7},{7,6},{8,9},{9,8},{10,11... | collective-permute-start | bytes 983048 | tf_op jit(solution)/shard_map/ppermute | solution.py:400
  142.6 51.8 %copy-start.7 = (bf16[128,1280]{1,0:T(8,128)(2,1)}, bf16[128,1280]{1,0:T(8,128)(2,1)S(1)}, u32[]{:S(2)}) copy-start(bf16[128,1280]{1,0:T(8,128)(2,1)S(1)} %collective-permute-done.14.refs_10_) | copy-start | bytes 983044
  142.6 35.5 %collective-permute-start.13 = (bf16[128,1280]{1,0:T(8,128)(2,1)S(1)}, bf16[128,1280]{1,0:T(8,128)(2,1)}, u32[]{:S(2)}, u32[]{:S(2)}) collective-permute-start(bf16[128,1280]{1,0:T(8,128)(2,1)S(1)} %collective-permute-done.9.refs_5_), channel_id=1, source_target_pairs={{0,2},{2,0},{4,6},{6,4},{8,10},{10,8},{12,14},{14,12},{1,3},{3,1},... | collective-permute-start | bytes 983048 | tf_op jit(solution)/shard_map/ppermute | solution.py:400
  142.6 51.7 %copy-start.8 = (bf16[128,1280]{1,0:T(8,128)(2,1)}, bf16[128,1280]{1,0:T(8,128)(2,1)S(1)}, u32[]{:S(2)}) copy-start(bf16[128,1280]{1,0:T(8,128)(2,1)S(1)} %collective-permute-done.10.refs_6_) | copy-start | bytes 983044
  142.6 34.6 %collective-permute-start.18 = (bf16[128,1280]{1,0:T(8,128)(2,1)S(1)}, bf16[128,1280]{1,0:T(8,128)(2,1)}, u32[]{:S(2)}, u32[]{:S(2)}) collective-permute-start(bf16[128,1280]{1,0:T(8,128)(2,1)S(1)} %collective-permute-done.10.refs_6_), channel_id=1, source_target_pairs={{0,1},{1,0},{2,3},{3,2},{4,5},{5,4},{6,7},{7,6},{8,9},{9,8},{10,11... | collective-permute-start | bytes 983048 | tf_op jit(solution)/shard_map/ppermute | solution.py:400
  165.7 28.7 %copy-start.9 = (bf16[128,1280]{1,0:T(8,128)(2,1)}, bf16[128,1280]{1,0:T(8,128)(2,1)S(1)}, u32[]{:S(2)}) copy-start(bf16[128,1280]{1,0:T(8,128)(2,1)S(1)} %collective-permute-done.8.refs_4_) | copy-start | bytes 983044
  165.7 12.8 %collective-permute-start.12 = (bf16[128,1280]{1,0:T(8,128)(2,1)S(1)}, bf16[128,1280]{1,0:T(8,128)(2,1)}, u32[]{:S(2)}, u32[]{:S(2)}) collective-permute-start(bf16[128,1280]{1,0:T(8,128)(2,1)S(1)} %collective-permute-done.8.refs_4_), channel_id=1, source_target_pairs={{0,2},{2,0},{4,6},{6,4},{8,10},{10,8},{12,14},{14,12},{1,3},{3,1},... | collective-permute-start | bytes 983048 | tf_op jit(solution)/shard_map/ppermute | solution.py:400
  175.6 18.8 %copy-start.10 = (bf16[128,1280]{1,0:T(8,128)(2,1)}, bf16[128,1280]{1,0:T(8,128)(2,1)S(1)}, u32[]{:S(2)}) copy-start(bf16[128,1280]{1,0:T(8,128)(2,1)S(1)} %collective-permute-done.7.refs_3_) | copy-start | bytes 983044
  175.6 11.5 %collective-permute-start.11 = (bf16[128,1280]{1,0:T(8,128)(2,1)S(1)}, bf16[128,1280]{1,0:T(8,128)(2,1)}, u32[]{:S(2)}, u32[]{:S(2)}) collective-permute-start(bf16[128,1280]{1,0:T(8,128)(2,1)S(1)} %collective-permute-done.7.refs_3_), channel_id=1, source_target_pairs={{0,2},{2,0},{4,6},{6,4},{8,10},{10,8},{12,14},{14,12},{1,3},{3,1},... | collective-permute-start | bytes 983048 | tf_op jit(solution)/shard_map/ppermute | solution.py:400
  177.2 17.1 %collective-permute-start.16 = (bf16[128,1280]{1,0:T(8,128)(2,1)S(1)}, bf16[128,1280]{1,0:T(8,128)(2,1)}, u32[]{:S(2)}, u32[]{:S(2)}) collective-permute-start(bf16[128,1280]{1,0:T(8,128)(2,1)S(1)} %collective-permute-done.8.refs_4_), channel_id=1, source_target_pairs={{0,1},{1,0},{2,3},{3,2},{4,5},{5,4},{6,7},{7,6},{8,9},{9,8},{10,11... | collective-permute-start | bytes 983048 | tf_op jit(solution)/shard_map/ppermute | solution.py:400
  178.0 16.3 %collective-permute-start.15 = (bf16[128,1280]{1,0:T(8,128)(2,1)S(1)}, bf16[128,1280]{1,0:T(8,128)(2,1)}, u32[]{:S(2)}, u32[]{:S(2)}) collective-permute-start(bf16[128,1280]{1,0:T(8,128)(2,1)S(1)} %collective-permute-done.7.refs_3_), channel_id=1, source_target_pairs={{0,1},{1,0},{2,3},{3,2},{4,5},{5,4},{6,7},{7,6},{8,9},{9,8},{10,11... | collective-permute-start | bytes 983048 | tf_op jit(solution)/shard_map/ppermute | solution.py:400
  178.1 16.2 %collective-permute-start.21 = (bf16[128,1280]{1,0:T(8,128)(2,1)}, bf16[128,1280]{1,0:T(8,128)(2,1)}, u32[]{:S(2)}, u32[]{:S(2)}) collective-permute-start(bf16[128,1280]{1,0:T(8,128)(2,1)} %collective-permute-done.13.refs_9_), channel_id=1, source_target_pairs={{0,1},{1,0},{2,3},{3,2},{4,5},{5,4},{6,7},{7,6},{8,9},{9,8},{10,11... | collective-permute-start | bytes 983048 | tf_op jit(solution)/shard_map/ppermute | solution.py:400
  178.5 15.8 %collective-permute-start.20 = (bf16[128,1280]{1,0:T(8,128)(2,1)}, bf16[128,1280]{1,0:T(8,128)(2,1)}, u32[]{:S(2)}, u32[]{:S(2)}) collective-permute-start(bf16[128,1280]{1,0:T(8,128)(2,1)} %collective-permute-done.12.refs_8_), channel_id=1, source_target_pairs={{0,1},{1,0},{2,3},{3,2},{4,5},{5,4},{6,7},{7,6},{8,9},{9,8},{10,11... | collective-permute-start | bytes 983048 | tf_op jit(solution)/shard_map/ppermute | solution.py:400
  187.1 7.2 %collective-permute-start.19 = (bf16[128,1280]{1,0:T(8,128)(2,1)}, bf16[128,1280]{1,0:T(8,128)(2,1)}, u32[]{:S(2)}, u32[]{:S(2)}) collective-permute-start(bf16[128,1280]{1,0:T(8,128)(2,1)} %collective-permute-done.11.refs_7_), channel_id=1, source_target_pairs={{0,1},{1,0},{2,3},{3,2},{4,5},{5,4},{6,7},{7,6},{8,9},{9,8},{10,11... | collective-permute-start | bytes 983048 | tf_op jit(solution)/shard_map/ppermute | solution.py:400
  243.6 7.7 %copy-start.2 = (bf16[1024,1280]{1,0:T(8,128)(2,1)S(1)}, bf16[1024,1280]{1,0:T(8,128)(2,1)}, u32[]{:S(2)}) copy-start(bf16[1024,1280]{1,0:T(8,128)(2,1)} %get-tuple-element.10) | copy-start | bytes 7864324
  245.8 3.5 collective-permute-start.22
  246.1 5.2 %collective-permute-start.23 = (bf16[512,1280]{1,0:T(8,128)(2,1)S(1)}, bf16[512,1280]{1,0:T(8,128)(2,1)S(1)}, u32[]{:S(2)}, u32[]{:S(2)}) collective-permute-start(bf16[512,1280]{1,0:T(8,128)(2,1)S(1)} %get-tuple-element.20), channel_id=1, source_target_pairs={{0,1},{1,0},{2,3},{3,2},{4,5},{5,4},{6,7},{7,6},{8,9},{9,8},{10,11... | collective-permute-start | bytes 3932168 | tf_op jit(solution)/shard_map/ppermute | solution.py:400
  251.7 9.1 %collective-permute-start.28 = (bf16[128,1280]{1,0:T(8,128)(2,1)S(1)}, bf16[128,1280]{1,0:T(8,128)(2,1)S(1)}, u32[]{:S(2)}, u32[]{:S(2)}) collective-permute-start(bf16[128,1280]{1,0:T(8,128)(2,1)S(1)} %get-tuple-element.22), channel_id=1, source_target_pairs={{0,2},{2,0},{4,6},{6,4},{8,10},{10,8},{12,14},{14,12},{1,3},{3,1},... | collective-permute-start | bytes 983048 | tf_op jit(solution)/shard_map/ppermute | solution.py:400
  252.2 16.9 %collective-permute-start.26 = (bf16[128,1280]{1,0:T(8,128)(2,1)S(1)}, bf16[128,1280]{1,0:T(8,128)(2,1)S(1)}, u32[]{:S(2)}, u32[]{:S(2)}) collective-permute-start(bf16[128,1280]{1,0:T(8,128)(2,1)S(1)} %get-tuple-element.23), channel_id=1, source_target_pairs={{0,2},{2,0},{4,6},{6,4},{8,10},{10,8},{12,14},{14,12},{1,3},{3,1},... | collective-permute-start | bytes 983048 | tf_op jit(solution)/shard_map/ppermute | solution.py:400
  253.2 30.0 %collective-permute-start.24 = (bf16[128,1280]{1,0:T(8,128)(2,1)S(1)}, bf16[128,1280]{1,0:T(8,128)(2,1)S(1)}, u32[]{:S(2)}, u32[]{:S(2)}) collective-permute-start(bf16[128,1280]{1,0:T(8,128)(2,1)S(1)} %get-tuple-element.24), channel_id=1, source_target_pairs={{0,2},{2,0},{4,6},{6,4},{8,10},{10,8},{12,14},{14,12},{1,3},{3,1},... | collective-permute-start | bytes 983048 | tf_op jit(solution)/shard_map/ppermute | solution.py:400
  253.7 43.5 %collective-permute-start.30 = (bf16[128,1280]{1,0:T(8,128)(2,1)S(1)}, bf16[128,1280]{1,0:T(8,128)(2,1)S(1)}, u32[]{:S(2)}, u32[]{:S(2)}) collective-permute-start(bf16[128,1280]{1,0:T(8,128)(2,1)S(1)} %get-tuple-element.21), channel_id=1, source_target_pairs={{0,2},{2,0},{4,6},{6,4},{8,10},{10,8},{12,14},{14,12},{1,3},{3,1},... | collective-permute-start | bytes 983048 | tf_op jit(solution)/shard_map/ppermute | solution.py:400
  283.3 24.2 %collective-permute-start.25 = (bf16[128,1280]{1,0:T(8,128)(2,1)S(1)}, bf16[128,1280]{1,0:T(8,128)(2,1)S(1)}, u32[]{:S(2)}, u32[]{:S(2)}) collective-permute-start(bf16[128,1280]{1,0:T(8,128)(2,1)S(1)} %get-tuple-element.25), channel_id=1, source_target_pairs={{0,8},{2,10},{4,12},{6,14},{8,0},{10,2},{12,4},{14,6},{1,9},{3,11}... | collective-permute-start | bytes 983048 | tf_op jit(solution)/shard_map/ppermute | solution.py:408
  283.4 40.5 %collective-permute-start.29 = (bf16[128,1280]{1,0:T(8,128)(2,1)S(1)}, bf16[128,1280]{1,0:T(8,128)(2,1)S(1)}, u32[]{:S(2)}, u32[]{:S(2)}) collective-permute-start(bf16[128,1280]{1,0:T(8,128)(2,1)S(1)} %get-tuple-element.26), channel_id=1, source_target_pairs={{0,4},{2,6},{4,8},{6,10},{8,12},{10,14},{12,0},{14,2},{1,5},{3,7},... | collective-permute-start | bytes 983048 | tf_op jit(solution)/shard_map/ppermute | solution.py:408
  283.5 41.9 %collective-permute-start.27 = (bf16[128,1280]{1,0:T(8,128)(2,1)S(1)}, bf16[128,1280]{1,0:T(8,128)(2,1)S(1)}, u32[]{:S(2)}, u32[]{:S(2)}) collective-permute-start(bf16[128,1280]{1,0:T(8,128)(2,1)S(1)} %get-tuple-element.27), channel_id=1, source_target_pairs={{0,12},{2,14},{4,0},{6,2},{8,4},{10,6},{12,8},{14,10},{1,13},{3,15... | collective-permute-start | bytes 983048 | tf_op jit(solution)/shard_map/ppermute | solution.py:408
  342.4 2.1 copy-start.1
Sparse Core Ops, SparseCore 0:
  9.6 108.3 all-gather.4
  131.6 84.5 all-gather.6
  234.3 108.0 reduce-scatter.1

commit v3 on v1

--- a/solution.py
+++ b/solution.py
@@ -24,9 +24,8 @@
     return lax.ppermute(array, axis, pairs)
 
 
-def entering_state(block_log, end_state, start_state):
+def entering_state(block_log, logs, end_state, start_state):
     count, index = lax.axis_size("ctx"), lax.axis_index("ctx")
-    logs = lax.all_gather(block_log, "ctx")
     earlier = (jnp.arange(count) < index).astype(F32)[:, None, None]
     masked = logs * earlier
     after = jnp.flip(jnp.cumsum(jnp.flip(masked, 0), axis=0), 0) - masked
@@ -142,6 +141,100 @@
     )(slots, gates.reshape(total, 1), tokens, up_weight, down_weight)
 
 
+def dot_t(a, b):
+    return lax.dot_general(a, b, (((1,), (1,)), ((), ())), preferred_element_type=F32)
+
+
+def dense_kernel(toks, count, gate_ref, *refs):
+    blocks = refs[:count]
+    up_ref, down_ref = refs[count : count + 2]
+    outs = refs[count + 2 : 2 * count + 2]
+    x_ref, y_ref = refs[2 * count + 2 :]
+    for j in range(count):
+        x_ref[j * toks : (j + 1) * toks, :] = blocks[j][...]
+    size = 2 * toks
+
+    def part(n, carry):
+        rows = pl.ds(pl.multiple_of(n * size, size), size)
+        inner = dot_t(x_ref[rows, :], up_ref[0])
+        inner = jnp.square(jnp.maximum(inner, 0.0)).astype(BF16)
+        answers = jnp.dot(inner, down_ref[0], preferred_element_type=F32)
+        y_ref[rows, :] = (answers.astype(BF16).astype(F32) * gate_ref[rows, :]).astype(BF16)
+        return carry
+
+    lax.fori_loop(0, count // 2, part, 0)
+    for j in range(count):
+        outs[j][...] = y_ref[j * toks : (j + 1) * toks, :]
+
+
+def dense_expert(blocks, gates, up_t, down):
+    toks, width = blocks[0].shape
+    hidden = up_t.shape[1]
+    count = len(blocks)
+    whole = pl.BlockSpec(memory_space=pltpu.VMEM)
+    return pl.pallas_call(
+        functools.partial(dense_kernel, toks, count),
+        out_shape=(jax.ShapeDtypeStruct((toks, width), BF16),) * count,
+        in_specs=[whole] * (count + 3),
+        out_specs=(whole,) * count,
+        scratch_shapes=[
+            pltpu.VMEM((count * toks, width), BF16),
+            pltpu.VMEM((count * toks, width), BF16),
+        ],
+        compiler_params=pltpu.CompilerParams(vmem_limit_bytes=28 << 20),
+        cost_estimate=pl.CostEstimate(
+            flops=4 * count * toks * width, bytes_accessed=count * toks, transcendentals=0
+        ),
+    )(gates, *blocks, up_t, down)
+
+
+def swap_axis(array, axis):
+    count = lax.axis_size(axis)
+    return lax.ppermute(array, axis, [(i, i ^ 1) for i in range(count)])
+
+
+def along_pairs(array, by):
+    half = lax.axis_size("ctx") // 2
+    pairs = [
+        (2 * i + r, (i + by) % half * 2 + r) for i in range(half) for r in range(2)
+    ]
+    return lax.ppermute(array, "ctx", pairs)
+
+
+def barrier(*values):
+    return lax.optimization_barrier(values)
+
+
+def add(*parts):
+    return sum(part.astype(F32) for part in parts)
+
+
+def token_experts(expert_in, gates, up_weight, down_weight):
+    half = lax.axis_size("ctx") // 2
+    up_t = jnp.swapaxes(up_weight, 1, 2)
+    turns = [0] + [s for s in (2, 1, 3) if 0 < s < half]
+    turns = list(dict.fromkeys(turns))
+    come = {0: expert_in}
+    for s in turns[1:]:
+        come[s] = along_pairs(expert_in, s)
+    total = None
+    held, block = None, None
+    for s in turns:
+        same = come[s]
+        across = swap_axis(same, "ctx")
+        blocks = [same, across, swap_axis(same, "exp"), swap_axis(across, "exp")]
+        if held is not None:
+            *blocks, _ = barrier(*blocks, held)
+        near, far, near_out, far_out = dense_expert(blocks, gates[s], up_t, down_weight)
+        far = add(far, swap_axis(far_out, "exp")).astype(BF16)
+        held = far
+        block = add(near, swap_axis(near_out, "exp"), swap_axis(far, "ctx")).astype(BF16)
+        if s:
+            block = along_pairs(block, -s)
+        total = add(block) if total is None else add(total, block)
+    return total
+
+
 def per_device(
     x_in,
     bc_in,
@@ -177,9 +270,22 @@
     capacity = max(2, 4 * tok_rows * top_count // (3 * experts))
     chosen = routes[:, :, None] == jnp.arange(experts, dtype=jnp.int32)[None, None, :]
     dense_gate = jnp.sum(jnp.where(chosen, gate_weight[:, :, None], 0.0), axis=1)
-    all_gates = lax.all_gather(dense_gate.T, ("ctx", "exp"), axis=0)
-    me = lax.axis_index("ctx") * exp_count + exp_index
-    gates = lax.dynamic_index_in_dim(all_gates, me, 1, False)
+    log_steps = decay_log.reshape(block_len, local_groups, per_group)
+    cumulative = jnp.cumsum(log_steps, axis=0)
+    block_log = cumulative[block_len - 1]
+    table = jnp.concatenate(
+        [dense_gate.T, jnp.pad(block_log.reshape(1, -1), ((0, 0), (0, tok_rows - local_heads)))], 0
+    )
+    tables = lax.all_gather(table, ("ctx", "exp"), axis=0)
+    ctx_index = lax.axis_index("ctx")
+    me = ctx_index * exp_count + exp_index
+    gates = lax.dynamic_index_in_dim(tables, me, 1, False)
+    logs = lax.dynamic_index_in_dim(
+        tables[:, experts, :local_heads].reshape(ctx_count, exp_count, local_groups, per_group),
+        exp_index,
+        1,
+        False,
+    )
     member = gates > 0.0
     slots = jnp.where(member, jnp.cumsum(member.astype(jnp.int32), axis=1) - 1, -1)
 
@@ -191,14 +297,12 @@
     values = inner_act.astype(F32).reshape(block_len, local_groups, per_group, HEAD_DIM)
     b_rows = bc_act[:, 0].astype(F32).reshape(block_len, local_groups, STATE)
     c_rows = bc_act[:, 1].astype(F32).reshape(block_len, local_groups, STATE)
-    log_steps = decay_log.reshape(block_len, local_groups, per_group)
     step_sizes = time_step.reshape(block_len, local_groups, per_group)
-    cumulative = jnp.cumsum(log_steps, axis=0)
-    block_log = cumulative[block_len - 1]
     to_end = jnp.exp(block_log[None] - cumulative) * step_sizes
     end_state = jnp.einsum("tgrp,tgn->grpn", to_end[..., None] * values, b_rows, precision=HIGH)
     entering = entering_state(
         block_log,
+        logs,
         end_state,
         start_state.astype(F32).reshape(local_groups, per_group, HEAD_DIM, STATE),
     )
@@ -237,9 +341,21 @@
         * lax.rsqrt(jnp.mean(hidden_f * hidden_f, axis=-1, keepdims=True) + EPS)
         * moe_gain.astype(F32)
     ).astype(BF16)
-    tokens = lax.all_gather(expert_in, ("ctx", "exp"), axis=0, tiled=True)
-    answers = run_expert(tokens, slots, gates, up_weight, down_weight, capacity)
-    combined = lax.psum_scatter(answers, ("ctx", "exp"), scatter_dimension=0, tiled=True)
+    half = ctx_count // 2
+    if ctx_count % 2 == 0 and 1 < half <= 4 and exp_count == 2:
+        shift, place = jnp.arange(half)[:, None], jnp.arange(4)[None, :]
+        source = (
+            (ctx_index // 2 - shift) % half * 4
+            + (ctx_index + place) % 2 * 2
+            + (exp_index + place // 2) % 2
+        )
+        combined = token_experts(
+            expert_in, gates[source].reshape(half, -1, 1), up_weight, down_weight
+        )
+    else:
+        tokens = lax.all_gather(expert_in, ("ctx", "exp"), axis=0, tiled=True)
+        answers = run_expert(tokens, slots, gates, up_weight, down_weight, capacity)
+        combined = lax.psum_scatter(answers, ("ctx", "exp"), scatter_dimension=0, tiled=True)
     return (hidden_f + combined.astype(F32)).astype(BF16)
 
 

time: 375 us -> 332 us (0.89)
  waiting for transfers between devices: 247 us -> 146 us
  starting transfers between devices: 14 us -> 49.5 us
  local copies, waits for them, and re-layouts: 15.7 us -> 36.5 us
  blocking collectives: 28.9 us -> 17.5 us
  Pallas kernels: 23.7 us -> 34.2 us
    reduce_scatter x1 -> x0, waiting for transfers between devices: 122 us -> none  [per_device(): lax.psum_scatter(answers, ('ctx', 'exp'), scatter_dimension=0, tiled=True)]
    ppermute x0 -> x30, waiting for transfers between devices: none -> 83.4 us  [the longest x24 55 us: swap_axis(): return lax.ppermute(array, axis, [(i, i ^ 1) for i in range(count)])]
    all_gather x1 -> x0, waiting for transfers between devices: 63.4 us -> none  [per_device(): tokens = lax.all_gather(expert_in, ('ctx', 'exp'), axis=0, tiled=True)]
    ppermute x0 -> x30, starting transfers between devices: none -> 34.2 us  [the longest x6 19.6 us: along_pairs(): return lax.ppermute(array, 'ctx', pairs)]
    ppermute x5, waiting for transfers between devices: 17.1 us -> 43.1 us  [from_behind(): return lax.ppermute(array, axis, pairs)]
    all_gather x1, waiting for transfers between devices: 37.4 us -> 11.8 us  [per_device(): proj = lax.all_gather(out_proj.T, 'ctx', axis=0, tiled=True)]
    unnamed x27 -> x78, local copies, waits for them, and re-layouts: 8.71 us -> 28 us
    all_gather x2 -> x1, blocking collectives: 28.9 us -> 17.5 us  [per_device(): tables = lax.all_gather(table, ('ctx', 'exp'), axis=0)]
  transfers between devices with their start and end apart: 10 -> 38, of which waited for: 6 -> 15; matrix products, arithmetic and copies ran while one was open for 9% -> 8% of each run, Pallas kernels for 0% -> 10%
where the time goes in v3:
time: 332 us; the launch traced here: 328 us
  waiting for transfers between devices  146 us (44%)
  starting transfers between devices  49.5 us (15%)
  local copies, waits for them, and re-layouts  36.5 us (11%)
  Pallas kernels  34.2 us (10%)
  blocking collectives  17.5 us (5%)
  matrix products  16.6 us (5%)
  between operations  14.1 us (4%)
  other arithmetic  13.1 us (4%)
    ppermute x24, waiting for transfers between devices, swap_axis(): return lax.ppermute(array, axis, [(i, i ^ 1) for i in range(count)])  55 us
    ppermute x5, waiting for transfers between devices, from_behind(): return lax.ppermute(array, axis, pairs)  43.1 us
    pallas_call x4, Pallas kernels, dense_expert(): pl.pallas_call(functools.partial(dense_kernel, toks, count), out_shape=(j...  34.2 us
    ppermute x6, waiting for transfers between devices, along_pairs(): return lax.ppermute(array, 'ctx', pairs)  28.4 us
    unnamed x78, local copies, waits for them, and re-layouts  28 us
    ppermute x6, starting transfers between devices, along_pairs(): return lax.ppermute(array, 'ctx', pairs)  19.6 us
    all_gather x1, blocking collectives, per_device(): tables = lax.all_gather(table, ('ctx', 'exp'), axis=0)  17.5 us
    ppermute x24, starting transfers between devices, swap_axis(): return lax.ppermute(array, axis, [(i, i ^ 1) for i in range(count)])  14.6 us
  transfers between devices with their start and end apart: 38, of which 15 were waited for; matrix products, arithmetic and copies ran while one was open for 8% of the time, Pallas kernels for 10%

profile of v3, /device:TPU:13, one launch (start us, length us, event | category | flops | bytes accessed | tf_op | source)
XLA Modules:
  0.0 327.6 jit_solution(4916421138796002995)
XLA Ops:
  7.3 0.7 slice.93
  8.0 3.1 collective-permute-start
  12.0 3.1 collective-permute-start.1
  15.2 1.2 reduce-window.6
  17.7 17.5 %all-gather.1 = f32[16,17,128]{2,1,0:T(8,128)S(1)} all-gather(f32[1,17,128]{2,1,0:T(8,128)S(1)} %fusion.53), channel_id=2, replica_groups=mesh['groups'=2,'ctx'=8,'exp'=2] {'ctx','exp'}, dimensions={0}, use_global_device_ids=true | all-gather | bytes 147968 | tf_op jit(solution)/shard_map/all_gather | solution.py:279
  36.7 0.8 multiply_convert_fusion.3
  39.5 1.3 collective-permute-start.2
  40.8 1.2 copy.105
  43.1 4.2 %collective-permute-done.2 = bf16[2,8,64,128]{3,2,1,0:T(8,128)(2,1)S(1)} collective-permute-done((bf16[2,8,64,128]{3,2,1,0:T(8,128)(2,1)S(1)}, bf16[2,8,64,128]{3,2,1,0:T(8,128)(2,1)S(1)}, u32[]{:S(2)}, u32[]{:S(2)}) %collective-permute-start.2) | collective-permute-done | bytes 262176 | tf_op jit(solution)/shard_map/ppermute | solution.py:37
  48.2 4.5 %collective-permute-start.4 = (bf16[2,8,64,128]{3,2,1,0:T(8,128)(2,1)S(1)}, bf16[2,8,64,128]{3,2,1,0:T(8,128)(2,1)S(1)}, u32[]{:S(2)}, u32[]{:S(2)}) collective-permute-start(bf16[2,8,64,128]{3,2,1,0:T(8,128)(2,1)S(1)} %fusion.33), channel_id=1, source_target_pairs={{0,8},{2,10},{4,12},{6,14},{1,9},{3,11},{5,13},{7,15},{16,24},{18,... | collective-permute-start | bytes 786440 | tf_op jit(solution)/shard_map/ppermute | solution.py:24
  52.7 2.1 collective-permute-start.5
  54.8 3.4 %fusion.16 = f32[256,2,8,64]{0,3,2,1:T(8,128)S(1)} fusion(bf16[256,2,8,64]{0,3,2,1:T(8,128)(2,1)S(1)} %bitcast.111, f32[256,256,2]{1,0,2:T(8,128)S(1)} %copy.103, f32[256,2,8]{0,2,1:T(8,128)S(1)} %bitcast.125, f32[256,2,8]{0,2,1:T(8,128)S(1)} %bitcast_bitcast_fusion, pred[256,256]{1,0:T(8,128)(4,1)S(1)} %iota_compare_fusion), kind=kOutput, calls=%fused_computation.29 | convolution fusion | flops 810549248 | bytes 2195456 | tf_op jit(solution)/shard_map/tsgr,sgrp->tgrp/dot_general | solution.py:318
  58.2 24.0 %collective-permute-done.4 = bf16[2,8,64,128]{3,2,1,0:T(8,128)(2,1)S(1)} collective-permute-done((bf16[2,8,64,128]{3,2,1,0:T(8,128)(2,1)S(1)}, bf16[2,8,64,128]{3,2,1,0:T(8,128)(2,1)S(1)}, u32[]{:S(2)}, u32[]{:S(2)}) %collective-permute-start.4) | collective-permute-done | bytes 262176 | tf_op jit(solution)/shard_map/ppermute | solution.py:24
  82.2 19.0 %collective-permute-done.5 = bf16[2,8,64,128]{3,2,1,0:T(8,128)(2,1)S(1)} collective-permute-done((bf16[2,8,64,128]{3,2,1,0:T(8,128)(2,1)S(1)}, bf16[2,8,64,128]{3,2,1,0:T(8,128)(2,1)S(1)}, u32[]{:S(2)}, u32[]{:S(2)}) %collective-permute-start.5) | collective-permute-done | bytes 262176 | tf_op jit(solution)/shard_map/ppermute | solution.py:24
  101.3 2.2 multiply_reduce_fusion.1
  104.2 1.6 copy.104
  106.2 11.8 %all-gather.4.cloned.1.call-done = bf16[2688,1024]{1,0:T(8,128)(2,1)} async-done(((bf16[336,1024]{1,0:T(8,128)(2,1)}), bf16[2688,1024]{1,0:T(8,128)(2,1)}) %all-gather.4.cloned.1.call-update) | async-done | bytes 5505040 | tf_op jit(solution)/shard_map/all_gather | solution.py:265
  117.9 5.5 %fusion.44 = f32[128,2688]{1,0:T(8,128)} fusion(bf16[2688,1024]{1,0:T(8,128)(2,1)} %all-gather.4.cloned.1.call-done, bf16[256,1024]{1,0:T(8,128)(2,1)S(1)} %multiply_convert_fusion.1, s32[]{:T(128)S(6)} %select_n.142), kind=kOutput, calls=%fused_computation.76 | convolution fusion | flops 704643072 | bytes 7143428 | tf_op jit(solution)/shard_map/dot_general | solution.py:334
  123.9 3.0 collective-permute-done.6
  126.9 4.6 %multiply_reduce_fusion = (f32[128]{0:T(128)S(1)}, f32[128,2688]{1,0:T(8,128)S(1)}) fusion(f32[128,2688]{1,0:T(8,128)S(1)} %collective-permute-done.6, bf16[2688,1024]{1,0:T(8,128)(2,1)} %all-gather.4.cloned.1.call-done, bf16[256,1024]{1,0:T(8,128)(2,1)S(1)} %multiply_convert_fusion.1, s32[]{:T(128)S(6)} %select_n.141, bf16[128,2688]{1,0:T(8,128)(2,1)S(1)} %copy-done.26), kind=kOutput, calls=%fused_computation.28 | convolution fusion | flops 707051392 | bytes 9208324 | tf_op jit(solution)/shard_map/dot_general | solution.py:334
  132.6 3.4 %collective-permute-start.13 = (bf16[128,2688]{1,0:T(8,128)(2,1)S(1)}, bf16[128,2688]{1,0:T(8,128)(2,1)S(1)}, u32[]{:S(2)}, u32[]{:S(2)}) collective-permute-start(bf16[128,2688]{1,0:T(8,128)(2,1)S(1)} %multiply_convert_fusion.refs_0_), channel_id=1, source_target_pairs={{0,8},{2,10},{4,12},{6,14},{8,0},{10,2},{12,4},{14,6},{1,9},{3,11}... | collective-permute-start | bytes 2064392 | tf_op jit(solution)/shard_map/ppermute | solution.py:201
  136.0 12.4 %collective-permute-done.7.refs_1_ = bf16[128,2688]{1,0:T(8,128)(2,1)S(1)} collective-permute-done((bf16[128,2688]{1,0:T(8,128)(2,1)S(1)}, bf16[128,2688]{1,0:T(8,128)(2,1)S(1)}, u32[]{:S(2)}, u32[]{:S(2)}) %collective-permute-start.7) | collective-permute-done | bytes 688160 | tf_op jit(solution)/shard_map/ppermute | solution.py:193
  148.4 1.2 collective-permute-start.9
  149.6 0.9 copy-done.13
  150.7 0.8 constant_dynamic-slice_fusion
  152.3 9.1 %collective-permute-done.13.refs_0_ = bf16[128,2688]{1,0:T(8,128)(2,1)S(1)} collective-permute-done((bf16[128,2688]{1,0:T(8,128)(2,1)S(1)}, bf16[128,2688]{1,0:T(8,128)(2,1)S(1)}, u32[]{:S(2)}, u32[]{:S(2)}) %collective-permute-start.13) | collective-permute-done | bytes 688160 | tf_op jit(solution)/shard_map/ppermute | solution.py:201
  161.4 1.5 collective-permute-start.14
  162.9 0.9 copy-done.15
  163.8 2.4 copy-done.2
  166.2 2.4 copy-done.6
  168.6 1.1 copy-done.14
  169.7 1.1 copy-done.16
  170.8 8.6 %shard_map.163 = (bf16[128,2688]{1,0:T(8,128)(2,1)S(1)}, bf16[128,2688]{1,0:T(8,128)(2,1)S(1)}, bf16[128,2688]{1,0:T(8,128)(2,1)S(1)}, bf16[128,2688]{1,0:T(8,128)(2,1)}) custom-call(f32[512,1]{1,0:T(8,128)S(1)} %copy.107.gate_ref, bf16[128,2688]{1,0:T(8,128)(2,1)S(1)} %multiply_convert_fusion.refs_0_, bf16[128,2688]{1,0:T(8,128)(2,1)S(1)} %copy-done.14, ...), custom_call_target="tpu_custom_call" | custom-call | flops 5505024 | bytes 512 | tf_op jit(solution)/shard_map/pallas_call | solution.py:175
  179.5 0.9 copy-done.17
  180.3 0.8 collective-permute-start.11
  181.2 15.9 %collective-permute-start.29 = (bf16[128,2688]{1,0:T(8,128)(2,1)S(1)}, bf16[128,2688]{1,0:T(8,128)(2,1)}, u32[]{:S(2)}, u32[]{:S(2)}) collective-permute-start(bf16[128,2688]{1,0:T(8,128)(2,1)S(1)} %multiply_convert_fusion.refs_0_), channel_id=1, source_target_pairs={{0,12},{2,14},{4,0},{6,2},{8,4},{10,6},{12,8},{14,10},{1,13},{3,15... | collective-permute-start | bytes 2064392 | tf_op jit(solution)/shard_map/ppermute | solution.py:201
  198.0 2.1 add_convert_fusion.8
  200.5 2.4 copy-done.3
  202.9 2.4 copy-done.7
  205.4 8.6 %shard_map.164 = (bf16[128,2688]{1,0:T(8,128)(2,1)S(1)}, bf16[128,2688]{1,0:T(8,128)(2,1)S(1)}, bf16[128,2688]{1,0:T(8,128)(2,1)S(1)}, bf16[128,2688]{1,0:T(8,128)(2,1)}) custom-call(f32[512,1]{1,0:T(8,128)S(1)} %copy.108.gate_ref, bf16[128,2688]{1,0:T(8,128)(2,1)S(1)} %copy-done.12, bf16[128,2688]{1,0:T(8,128)(2,1)} %collective-permute-done.14.refs_1_, ...), custom_call_target="tpu_custom_call" | custom-call | flops 5505024 | bytes 512 | tf_op jit(solution)/shard_map/pallas_call | solution.py:175
  214.0 0.9 copy-done.18
  215.6 1.1 collective-permute-start.30
  217.3 2.1 add_convert_fusion.6
  219.5 2.4 copy-done.4
  221.9 2.4 copy-done.8
  224.3 8.8 %shard_map.165 = (bf16[128,2688]{1,0:T(8,128)(2,1)S(1)}, bf16[128,2688]{1,0:T(8,128)(2,1)S(1)}, bf16[128,2688]{1,0:T(8,128)(2,1)S(1)}, bf16[128,2688]{1,0:T(8,128)(2,1)}) custom-call(f32[512,1]{1,0:T(8,128)S(1)} %copy.109.gate_ref, bf16[128,2688]{1,0:T(8,128)(2,1)} %collective-permute-done.21.refs_0_, bf16[128,2688]{1,0:T(8,128)(2,1)} %collective-permute-done.22.refs_1_, ...), custom_call_target="tpu_custom_call" | custom-call | flops 5505024 | bytes 512 | tf_op jit(solution)/shard_map/pallas_call | solution.py:175
  233.1 0.8 copy-done.10
  234.0 0.8 copy-done.19
  236.4 0.9 collective-permute-done.26
  237.3 1.1 collective-permute-start.19
  238.4 1.5 add_convert_fusion.4
  240.3 0.8 collective-permute-start.25
  241.2 2.4 copy-done.5
  243.6 2.4 copy-done.9
  246.0 8.1 %shard_map.166 = (bf16[128,2688]{1,0:T(8,128)(2,1)S(1)}, bf16[128,2688]{1,0:T(8,128)(2,1)S(1)}, bf16[128,2688]{1,0:T(8,128)(2,1)S(1)}, bf16[128,2688]{1,0:T(8,128)(2,1)S(1)}) custom-call(f32[512,1]{1,0:T(8,128)S(1)} %copy.110.gate_ref, bf16[128,2688]{1,0:T(8,128)(2,1)} %collective-permute-done.29.refs_0_, bf16[128,2688]{1,0:T(8,128)(2,1)} %collective-permute-done.30.refs_1_, ...), custom_call_target="tpu_custom_call" | custom-call | flops 5505024 | bytes 512 | tf_op jit(solution)/shard_map/pallas_call | solution.py:175
  254.1 1.1 collective-permute-start.27
  255.2 0.9 collective-permute-start.34
  256.3 1.5 collective-permute-done.34
  258.5 25.3 %collective-permute-done.27 = bf16[128,2688]{1,0:T(8,128)(2,1)S(1)} collective-permute-done((bf16[128,2688]{1,0:T(8,128)(2,1)S(1)}, bf16[128,2688]{1,0:T(8,128)(2,1)S(1)}, u32[]{:S(2)}, u32[]{:S(2)}) %collective-permute-start.27) | collective-permute-done | bytes 688160 | tf_op jit(solution)/shard_map/ppermute | solution.py:193
  283.7 1.2 collective-permute-start.35
  285.3 14.3 %collective-permute-done.35 = bf16[128,2688]{1,0:T(8,128)(2,1)S(1)} collective-permute-done((bf16[128,2688]{1,0:T(8,128)(2,1)S(1)}, bf16[128,2688]{1,0:T(8,128)(2,1)S(1)}, u32[]{:S(2)}, u32[]{:S(2)}) %collective-permute-start.35) | collective-permute-done | bytes 688160 | tf_op jit(solution)/shard_map/ppermute | solution.py:193
  299.9 2.4 collective-permute-done.20
  302.3 16.9 %collective-permute-done.28 = bf16[128,2688]{1,0:T(8,128)(2,1)S(1)} collective-permute-done((bf16[128,2688]{1,0:T(8,128)(2,1)S(1)}, bf16[128,2688]{1,0:T(8,128)(2,1)S(1)}, u32[]{:S(2)}, u32[]{:S(2)}) %collective-permute-start.28) | collective-permute-done | bytes 688160 | tf_op jit(solution)/shard_map/ppermute | solution.py:201
  319.2 1.5 add_convert_fusion
  (172 shorter events, 18.1 us)
Async XLA Ops:
  6.5 8.7 %copy-start = (f32[256,16]{0,1:T(8,128)S(1)}, f32[256,16]{0,1:T(8,128)}, u32[]{:S(2)}) copy-start(f32[256,16]{0,1:T(8,128)} %param.21) | copy-start | bytes 49156
  6.5 29.7 %copy-start.28 = (bf16[256,2,256]{2,1,0:T(2,128)(2,1)S(1)}, bf16[256,2,256]{2,1,0:T(2,128)(2,1)}, u32[]{:S(2)}) copy-start(bf16[256,2,256]{2,1,0:T(2,128)(2,1)} %param.18) | copy-start | bytes 786436
  6.5 29.4 %copy-start.33 = (bf16[4,2,256]{2,1,0:T(2,128)(2,1)S(1)}, bf16[4,2,256]{2,1,0:T(2,128)(2,1)}, u32[]{:S(2)}) copy-start(bf16[4,2,256]{2,1,0:T(2,128)(2,1)} %param.23) | copy-start | bytes 12292
  6.5 29.6 %copy-start.30 = (bf16[4,1024]{1,0:T(4,128)(2,1)S(1)}, bf16[4,1024]{1,0:T(4,128)(2,1)}, u32[]{:S(2)}) copy-start(bf16[4,1024]{1,0:T(4,128)(2,1)} %param.22) | copy-start | bytes 24580
  6.5 29.6 %copy-start.31 = (f32[256,16]{0,1:T(8,128)S(1)}, f32[256,16]{0,1:T(8,128)}, u32[]{:S(2)}) copy-start(f32[256,16]{0,1:T(8,128)} %param.20) | copy-start | bytes 49156
  6.5 111.4 %all-gather.4.cloned.1.call-start = ((), (), s32[]{:S(2)}) async-start(), calls=%async_computation | async-start | bytes 6193152 | tf_op jit(solution)/shard_map/all_gather | solution.py:265
  8.0 29.5 %collective-permute-start = (bf16[3,1024]{1,0:T(4,128)(2,1)S(1)}, bf16[3,1024]{1,0:T(4,128)(2,1)S(1)}, u32[]{:S(2)}, u32[]{:S(2)}) collective-permute-start(bf16[3,1024]{1,0:T(4,128)(2,1)S(1)} %slice.93), channel_id=1, source_target_pairs={{0,2},{2,4},{4,6},{6,8},{8,10},{10,12},{12,14},{1,3},{3,5},{5,7},{... | collective-permute-start | bytes 18440 | tf_op jit(solution)/shard_map/ppermute | solution.py:24
  12.0 24.5 %collective-permute-start.1 = (bf16[3,2,256]{0,2,1:T(8,128)(2,1)S(1)}, bf16[3,2,256]{0,2,1:T(8,128)(2,1)S(1)}, u32[]{:S(2)}, u32[]{:S(2)}) collective-permute-start(bf16[3,2,256]{0,2,1:T(8,128)(2,1)S(1)} %copy.97), channel_id=1, source_target_pairs={{0,2},{2,4},{4,6},{6,8},{8,10},{10,12},{12,14},{1,3},{3,5},{5,7},{... | collective-permute-start | bytes 9224 | tf_op jit(solution)/shard_map/ppermute | solution.py:24
  38.8 3.2 copy-start.36
  38.8 3.8 %copy-start.34 = (bf16[1024]{0:T(1024)(128)(2,1)S(1)}, bf16[1024]{0:T(1024)(128)(2,1)}, u32[]{:S(2)}) copy-start(bf16[1024]{0:T(1024)(128)(2,1)} %param.26) | copy-start | bytes 6148
  39.5 7.8 %collective-permute-start.2 = (bf16[2,8,64,128]{3,2,1,0:T(8,128)(2,1)S(1)}, bf16[2,8,64,128]{3,2,1,0:T(8,128)(2,1)S(1)}, u32[]{:S(2)}, u32[]{:S(2)}) collective-permute-start(bf16[2,8,64,128]{3,2,1,0:T(8,128)(2,1)S(1)} %get-tuple-element.82), channel_id=1, source_target_pairs={{0,2},{2,0},{4,6},{6,4},{8,10},{10,8},{12,14},{14,12},{1,3},{3,1},... | collective-permute-start | bytes 786440 | tf_op jit(solution)/shard_map/ppermute | solution.py:37
  47.5 10.7 %collective-permute-start.3 = (bf16[2,8,64,128]{3,2,1,0:T(8,128)(2,1)S(1)}, bf16[2,8,64,128]{3,2,1,0:T(8,128)(2,1)S(1)}, u32[]{:S(2)}, u32[]{:S(2)}) collective-permute-start(bf16[2,8,64,128]{3,2,1,0:T(8,128)(2,1)S(1)} %fusion.33), channel_id=1, source_target_pairs={{0,12},{2,14},{1,13},{3,15},{16,28},{18,30},{17,29},{19,31}} | collective-permute-start | bytes 786440 | tf_op jit(solution)/shard_map/ppermute | solution.py:24
  48.2 34.0 %collective-permute-start.4 = (bf16[2,8,64,128]{3,2,1,0:T(8,128)(2,1)S(1)}, bf16[2,8,64,128]{3,2,1,0:T(8,128)(2,1)S(1)}, u32[]{:S(2)}, u32[]{:S(2)}) collective-permute-start(bf16[2,8,64,128]{3,2,1,0:T(8,128)(2,1)S(1)} %fusion.33), channel_id=1, source_target_pairs={{0,8},{2,10},{4,12},{6,14},{1,9},{3,11},{5,13},{7,15},{16,24},{18,... | collective-permute-start | bytes 786440 | tf_op jit(solution)/shard_map/ppermute | solution.py:24
  52.7 48.6 %collective-permute-start.5 = (bf16[2,8,64,128]{3,2,1,0:T(8,128)(2,1)S(1)}, bf16[2,8,64,128]{3,2,1,0:T(8,128)(2,1)S(1)}, u32[]{:S(2)}, u32[]{:S(2)}) collective-permute-start(bf16[2,8,64,128]{3,2,1,0:T(8,128)(2,1)S(1)} %fusion.33), channel_id=1, source_target_pairs={{0,4},{2,6},{4,8},{6,10},{8,12},{10,14},{1,5},{3,7},{5,9},{7,11},{... | collective-permute-start | bytes 786440 | tf_op jit(solution)/shard_map/ppermute | solution.py:24
  54.8 46.5 %copy-start.24 = (f32[256,1024]{0,1:T(8,128)S(1)}, f32[256,1024]{0,1:T(8,128)}, u32[]{:S(2)}) copy-start(f32[256,1024]{0,1:T(8,128)} %copy.105) | copy-start | bytes 3145732
  54.8 46.5 %copy-start.35 = (bf16[16,64,128]{2,1,0:T(8,128)(2,1)S(1)}, bf16[16,64,128]{2,1,0:T(8,128)(2,1)}, u32[]{:S(2)}) copy-start(bf16[16,64,128]{2,1,0:T(8,128)(2,1)} %param.25) | copy-start | bytes 786436
  54.8 46.5 %copy-start.37 = (f32[2,8]{1,0:T(2,128)S(1)}, f32[2,8]{1,0:T(2,128)}, u32[]{:S(2)}) copy-start(f32[2,8]{1,0:T(2,128)} %mul.362) | copy-start | bytes 196
  106.1 17.8 %copy-start.32 = (bf16[2688]{0:T(1024)(128)(2,1)S(1)}, bf16[2688]{0:T(1024)(128)(2,1)}, u32[]{:S(2)}) copy-start(bf16[2688]{0:T(1024)(128)(2,1)} %param.29) | copy-start | bytes 16132
  106.2 20.7 %copy-start.26 = (bf16[128,2688]{1,0:T(8,128)(2,1)S(1)}, bf16[128,2688]{1,0:T(8,128)(2,1)}, u32[]{:S(2)}) copy-start(bf16[128,2688]{1,0:T(8,128)(2,1)} %param.28) | copy-start | bytes 2064388
  123.5 3.4 %collective-permute-start.6 = (f32[128,2688]{1,0:T(8,128)}, f32[128,2688]{1,0:T(8,128)S(1)}, u32[]{:S(2)}, u32[]{:S(2)}) collective-permute-start(f32[128,2688]{1,0:T(8,128)} %fusion.44), channel_id=1, source_target_pairs={{0,1},{1,0},{2,3},{3,2},{4,5},{5,4},{6,7},{7,6},{8,9},{9,8},{10,11... | collective-permute-start | bytes 4128776 | tf_op jit(solution)/shard_map/ppermute | solution.py:336
  131.5 18.1 %copy-start.21 = (f32[128,2688]{1,0:T(8,128)}, f32[128,2688]{1,0:T(8,128)S(1)}, u32[]{:S(2)}) copy-start(f32[128,2688]{1,0:T(8,128)S(1)} %get-tuple-element.87) | copy-start | bytes 4128772
  131.7 16.7 %collective-permute-start.7 = (bf16[128,2688]{1,0:T(8,128)(2,1)S(1)}, bf16[128,2688]{1,0:T(8,128)(2,1)S(1)}, u32[]{:S(2)}, u32[]{:S(2)}) collective-permute-start(bf16[128,2688]{1,0:T(8,128)(2,1)S(1)} %multiply_convert_fusion.refs_0_), channel_id=1, source_target_pairs={{0,2},{2,0},{4,6},{6,4},{8,10},{10,8},{12,14},{14,12},{1,3},{3,1},... | collective-permute-start | bytes 2064392 | tf_op jit(solution)/shard_map/ppermute | solution.py:193
  131.9 31.0 %collective-permute-start.8 = (bf16[128,2688]{1,0:T(8,128)(2,1)S(1)}, bf16[128,2688]{1,0:T(8,128)(2,1)S(1)}, u32[]{:S(2)}, u32[]{:S(2)}) collective-permute-start(bf16[128,2688]{1,0:T(8,128)(2,1)S(1)} %multiply_convert_fusion.refs_0_), channel_id=1, source_target_pairs={{0,1},{1,0},{2,3},{3,2},{4,5},{5,4},{6,7},{7,6},{8,9},{9,8},{10,11... | collective-permute-start | bytes 2064392 | tf_op jit(solution)/shard_map/ppermute | solution.py:193
  132.6 28.8 %collective-permute-start.13 = (bf16[128,2688]{1,0:T(8,128)(2,1)S(1)}, bf16[128,2688]{1,0:T(8,128)(2,1)S(1)}, u32[]{:S(2)}, u32[]{:S(2)}) collective-permute-start(bf16[128,2688]{1,0:T(8,128)(2,1)S(1)} %multiply_convert_fusion.refs_0_), channel_id=1, source_target_pairs={{0,8},{2,10},{4,12},{6,14},{8,0},{10,2},{12,4},{14,6},{1,9},{3,11}... | collective-permute-start | bytes 2064392 | tf_op jit(solution)/shard_map/ppermute | solution.py:201
  148.4 15.4 %collective-permute-start.9 = (bf16[128,2688]{1,0:T(8,128)(2,1)S(1)}, bf16[128,2688]{1,0:T(8,128)(2,1)}, u32[]{:S(2)}, u32[]{:S(2)}) collective-permute-start(bf16[128,2688]{1,0:T(8,128)(2,1)S(1)} %collective-permute-done.7.refs_1_), channel_id=1, source_target_pairs={{0,1},{1,0},{2,3},{3,2},{4,5},{5,4},{6,7},{7,6},{8,9},{9,8},{10,11... | collective-permute-start | bytes 2064392 | tf_op jit(solution)/shard_map/ppermute | solution.py:193
  152.3 45.2 %collective-permute-start.21 = (bf16[128,2688]{1,0:T(8,128)(2,1)S(1)}, bf16[128,2688]{1,0:T(8,128)(2,1)}, u32[]{:S(2)}, u32[]{:S(2)}) collective-permute-start(bf16[128,2688]{1,0:T(8,128)(2,1)S(1)} %multiply_convert_fusion.refs_0_), channel_id=1, source_target_pairs={{0,4},{2,6},{4,8},{6,10},{8,12},{10,14},{12,0},{14,2},{1,5},{3,7},... | collective-permute-start | bytes 2064392 | tf_op jit(solution)/shard_map/ppermute | solution.py:201
  161.4 35.8 %copy-start.11 = (bf16[128,2688]{1,0:T(8,128)(2,1)}, bf16[128,2688]{1,0:T(8,128)(2,1)S(1)}, u32[]{:S(2)}) copy-start(bf16[128,2688]{1,0:T(8,128)(2,1)S(1)} %collective-permute-done.13.refs_0_) | copy-start | bytes 2064388
  161.4 36.1 %collective-permute-start.14 = (bf16[128,2688]{1,0:T(8,128)(2,1)S(1)}, bf16[128,2688]{1,0:T(8,128)(2,1)}, u32[]{:S(2)}, u32[]{:S(2)}) collective-permute-start(bf16[128,2688]{1,0:T(8,128)(2,1)S(1)} %collective-permute-done.13.refs_0_), channel_id=1, source_target_pairs={{0,2},{2,0},{4,6},{6,4},{8,10},{10,8},{12,14},{14,12},{1,3},{3,1},... | collective-permute-start | bytes 2064392 | tf_op jit(solution)/shard_map/ppermute | solution.py:193
  163.8 2.4 copy-start.2
  166.2 2.4 copy-start.6
  180.3 17.6 %collective-permute-start.11 = (bf16[128,2688]{1,0:T(8,128)(2,1)}, bf16[128,2688]{1,0:T(8,128)(2,1)}, u32[]{:S(2)}, u32[]{:S(2)}) collective-permute-start(bf16[128,2688]{1,0:T(8,128)(2,1)} %get-tuple-element.36), channel_id=1, source_target_pairs={{0,1},{1,0},{2,3},{3,2},{4,5},{5,4},{6,7},{7,6},{8,9},{9,8},{10,11... | collective-permute-start | bytes 2064392 | tf_op jit(solution)/shard_map/ppermute | solution.py:193
  181.2 34.3 %collective-permute-start.29 = (bf16[128,2688]{1,0:T(8,128)(2,1)S(1)}, bf16[128,2688]{1,0:T(8,128)(2,1)}, u32[]{:S(2)}, u32[]{:S(2)}) collective-permute-start(bf16[128,2688]{1,0:T(8,128)(2,1)S(1)} %multiply_convert_fusion.refs_0_), channel_id=1, source_target_pairs={{0,12},{2,14},{4,0},{6,2},{8,4},{10,6},{12,8},{14,10},{1,13},{3,15... | collective-permute-start | bytes 2064392 | tf_op jit(solution)/shard_map/ppermute | solution.py:201
  197.2 2.9 collective-permute-start.15
  197.5 3.1 copy-start.12
  197.5 19.2 %collective-permute-start.22 = (bf16[128,2688]{1,0:T(8,128)(2,1)}, bf16[128,2688]{1,0:T(8,128)(2,1)}, u32[]{:S(2)}, u32[]{:S(2)}) collective-permute-start(bf16[128,2688]{1,0:T(8,128)(2,1)} %collective-permute-done.21.refs_0_), channel_id=1, source_target_pairs={{0,2},{2,0},{4,6},{6,4},{8,10},{10,8},{12,14},{14,12},{1,3},{3,1},... | collective-permute-start | bytes 2064392 | tf_op jit(solution)/shard_map/ppermute | solution.py:193
  197.5 3.0 collective-permute-start.16
  200.5 2.4 copy-start.3
  202.9 2.4 copy-start.7
  214.8 2.5 collective-permute-start.18
  215.3 4.2 %collective-permute-start.23 = (bf16[128,2688]{1,0:T(8,128)(2,1)}, bf16[128,2688]{1,0:T(8,128)(2,1)S(1)}, u32[]{:S(2)}, u32[]{:S(2)}) collective-permute-start(bf16[128,2688]{1,0:T(8,128)(2,1)} %collective-permute-done.21.refs_0_), channel_id=1, source_target_pairs={{0,1},{1,0},{2,3},{3,2},{4,5},{5,4},{6,7},{7,6},{8,9},{9,8},{10,11... | collective-permute-start | bytes 2064392 | tf_op jit(solution)/shard_map/ppermute | solution.py:193
  215.6 20.3 %collective-permute-start.30 = (bf16[128,2688]{1,0:T(8,128)(2,1)}, bf16[128,2688]{1,0:T(8,128)(2,1)}, u32[]{:S(2)}, u32[]{:S(2)}) collective-permute-start(bf16[128,2688]{1,0:T(8,128)(2,1)} %collective-permute-done.29.refs_0_), channel_id=1, source_target_pairs={{0,2},{2,0},{4,6},{6,4},{8,10},{10,8},{12,14},{14,12},{1,3},{3,1},... | collective-permute-start | bytes 2064392 | tf_op jit(solution)/shard_map/ppermute | solution.py:193
  216.7 2.8 collective-permute-start.24
  219.5 2.4 copy-start.4
  221.9 2.4 copy-start.8
  234.8 5.5 %copy-start.20 = (bf16[128,2688]{1,0:T(8,128)(2,1)S(1)}, bf16[128,2688]{1,0:T(8,128)(2,1)}, u32[]{:S(2)}) copy-start(bf16[128,2688]{1,0:T(8,128)(2,1)} %copy-done.19) | copy-start | bytes 2064388
  234.8 2.5 collective-permute-start.26
  235.3 4.6 %copy-start.25 = (bf16[128,2688]{1,0:T(8,128)(2,1)S(1)}, bf16[128,2688]{1,0:T(8,128)(2,1)}, u32[]{:S(2)}) copy-start(bf16[128,2688]{1,0:T(8,128)(2,1)} %add_convert_fusion.8) | copy-start | bytes 2064388
  235.3 4.6 %collective-permute-start.31 = (bf16[128,2688]{1,0:T(8,128)(2,1)}, bf16[128,2688]{1,0:T(8,128)(2,1)S(1)}, u32[]{:S(2)}, u32[]{:S(2)}) collective-permute-start(bf16[128,2688]{1,0:T(8,128)(2,1)} %collective-permute-done.29.refs_0_), channel_id=1, source_target_pairs={{0,1},{1,0},{2,3},{3,2},{4,5},{5,4},{6,7},{7,6},{8,9},{9,8},{10,11... | collective-permute-start | bytes 2064392 | tf_op jit(solution)/shard_map/ppermute | solution.py:193
  235.6 64.4 %collective-permute-start.10 = (bf16[128,2688]{1,0:T(8,128)(2,1)}, bf16[128,2688]{1,0:T(8,128)(2,1)S(1)}, u32[]{:S(2)}, u32[]{:S(2)}) collective-permute-start(bf16[128,2688]{1,0:T(8,128)(2,1)} %copy-done.17), channel_id=1, source_target_pairs={{0,1},{1,0},{2,3},{3,2},{4,5},{5,4},{6,7},{7,6},{8,9},{9,8},{10,11... | collective-permute-start | bytes 2064392 | tf_op jit(solution)/shard_map/ppermute | solution.py:193
  235.8 4.5 %collective-permute-start.32 = (bf16[128,2688]{1,0:T(8,128)(2,1)}, bf16[128,2688]{1,0:T(8,128)(2,1)S(1)}, u32[]{:S(2)}, u32[]{:S(2)}) collective-permute-start(bf16[128,2688]{1,0:T(8,128)(2,1)} %collective-permute-done.30.refs_1_), channel_id=1, source_target_pairs={{0,1},{1,0},{2,3},{3,2},{4,5},{5,4},{6,7},{7,6},{8,9},{9,8},{10,11... | collective-permute-start | bytes 2064392 | tf_op jit(solution)/shard_map/ppermute | solution.py:193
  236.1 18.0 %collective-permute-start.17 = (bf16[128,2688]{1,0:T(8,128)(2,1)}, bf16[128,2688]{1,0:T(8,128)(2,1)S(1)}, u32[]{:S(2)}, u32[]{:S(2)}) collective-permute-start(bf16[128,2688]{1,0:T(8,128)(2,1)} %copy-done.18), channel_id=1, source_target_pairs={{0,1},{1,0},{2,3},{3,2},{4,5},{5,4},{6,7},{7,6},{8,9},{9,8},{10,11... | collective-permute-start | bytes 2064392 | tf_op jit(solution)/shard_map/ppermute | solution.py:193
  237.3 17.9 %collective-permute-start.19 = (bf16[128,2688]{1,0:T(8,128)(2,1)}, bf16[128,2688]{1,0:T(8,128)(2,1)S(1)}, u32[]{:S(2)}, u32[]{:S(2)}) collective-permute-start(bf16[128,2688]{1,0:T(8,128)(2,1)} %add_convert_fusion.6), channel_id=1, source_target_pairs={{0,2},{2,0},{4,6},{6,4},{8,10},{10,8},{12,14},{14,12},{1,3},{3,1},... | collective-permute-start | bytes 2064392 | tf_op jit(solution)/shard_map/ppermute | solution.py:193
  239.9 60.1 %collective-permute-start.12 = (bf16[128,2688]{1,0:T(8,128)(2,1)S(1)}, bf16[128,2688]{1,0:T(8,128)(2,1)S(1)}, u32[]{:S(2)}, u32[]{:S(2)}) collective-permute-start(bf16[128,2688]{1,0:T(8,128)(2,1)S(1)} %copy-done.25), channel_id=1, source_target_pairs={{0,2},{2,0},{4,6},{6,4},{8,10},{10,8},{12,14},{14,12},{1,3},{3,1},... | collective-permute-start | bytes 2064392 | tf_op jit(solution)/shard_map/ppermute | solution.py:193
  240.3 17.7 %collective-permute-start.25 = (bf16[128,2688]{1,0:T(8,128)(2,1)S(1)}, bf16[128,2688]{1,0:T(8,128)(2,1)S(1)}, u32[]{:S(2)}, u32[]{:S(2)}) collective-permute-start(bf16[128,2688]{1,0:T(8,128)(2,1)S(1)} %copy-done.20), channel_id=1, source_target_pairs={{0,1},{1,0},{2,3},{3,2},{4,5},{5,4},{6,7},{7,6},{8,9},{9,8},{10,11... | collective-permute-start | bytes 2064392 | tf_op jit(solution)/shard_map/ppermute | solution.py:193
  241.2 2.4 copy-start.5
  243.6 2.4 copy-start.9
  254.1 29.7 %collective-permute-start.27 = (bf16[128,2688]{1,0:T(8,128)(2,1)S(1)}, bf16[128,2688]{1,0:T(8,128)(2,1)S(1)}, u32[]{:S(2)}, u32[]{:S(2)}) collective-permute-start(bf16[128,2688]{1,0:T(8,128)(2,1)S(1)} %add_convert_fusion.4), channel_id=1, source_target_pairs={{0,2},{2,0},{4,6},{6,4},{8,10},{10,8},{12,14},{14,12},{1,3},{3,1},... | collective-permute-start | bytes 2064392 | tf_op jit(solution)/shard_map/ppermute | solution.py:193
  255.2 2.7 collective-permute-start.34
  257.8 44.5 %collective-permute-start.20 = (bf16[128,2688]{1,0:T(8,128)(2,1)S(1)}, bf16[128,2688]{1,0:T(8,128)(2,1)S(1)}, u32[]{:S(2)}, u32[]{:S(2)}) collective-permute-start(bf16[128,2688]{1,0:T(8,128)(2,1)S(1)} %add_convert_fusion.5), channel_id=1, source_target_pairs={{0,8},{2,10},{4,12},{6,14},{8,0},{10,2},{12,4},{14,6},{1,9},{3,11}... | collective-permute-start | bytes 2064392 | tf_op jit(solution)/shard_map/ppermute | solution.py:201
  258.0 27.1 %collective-permute-start.33 = (bf16[128,2688]{1,0:T(8,128)(2,1)S(1)}, bf16[128,2688]{1,0:T(8,128)(2,1)S(1)}, u32[]{:S(2)}, u32[]{:S(2)}) collective-permute-start(bf16[128,2688]{1,0:T(8,128)(2,1)S(1)} %get-tuple-element.58), channel_id=1, source_target_pairs={{0,1},{1,0},{2,3},{3,2},{4,5},{5,4},{6,7},{7,6},{8,9},{9,8},{10,11... | collective-permute-start | bytes 2064392 | tf_op jit(solution)/shard_map/ppermute | solution.py:193
  283.7 15.8 %collective-permute-start.35 = (bf16[128,2688]{1,0:T(8,128)(2,1)S(1)}, bf16[128,2688]{1,0:T(8,128)(2,1)S(1)}, u32[]{:S(2)}, u32[]{:S(2)}) collective-permute-start(bf16[128,2688]{1,0:T(8,128)(2,1)S(1)} %add_convert_fusion.2), channel_id=1, source_target_pairs={{0,2},{2,0},{4,6},{6,4},{8,10},{10,8},{12,14},{14,12},{1,3},{3,1},... | collective-permute-start | bytes 2064392 | tf_op jit(solution)/shard_map/ppermute | solution.py:193
  285.2 34.0 %collective-permute-start.28 = (bf16[128,2688]{1,0:T(8,128)(2,1)S(1)}, bf16[128,2688]{1,0:T(8,128)(2,1)S(1)}, u32[]{:S(2)}, u32[]{:S(2)}) collective-permute-start(bf16[128,2688]{1,0:T(8,128)(2,1)S(1)} %add_convert_fusion.3), channel_id=1, source_target_pairs={{0,12},{2,14},{4,0},{6,2},{8,4},{10,6},{12,8},{14,10},{1,13},{3,15... | collective-permute-start | bytes 2064392 | tf_op jit(solution)/shard_map/ppermute | solution.py:201
  299.6 19.7 %copy-start.22 = (f32[128,2688]{1,0:T(8,128)S(1)}, f32[128,2688]{1,0:T(8,128)}, u32[]{:S(2)}) copy-start(f32[128,2688]{1,0:T(8,128)} %copy-done.21) | copy-start | bytes 4128772
  299.9 19.4 %collective-permute-start.36 = (bf16[128,2688]{1,0:T(8,128)(2,1)S(1)}, bf16[128,2688]{1,0:T(8,128)(2,1)S(1)}, u32[]{:S(2)}, u32[]{:S(2)}) collective-permute-start(bf16[128,2688]{1,0:T(8,128)(2,1)S(1)} %add_convert_fusion.1), channel_id=1, source_target_pairs={{0,4},{2,6},{4,8},{6,10},{8,12},{10,14},{12,0},{14,2},{1,5},{3,7},... | collective-permute-start | bytes 2064392 | tf_op jit(solution)/shard_map/ppermute | solution.py:201
  (12 other events, 12.8 us)
Sparse Core Ops, SparseCore 0:
  9.6 108.3 all-gather.3

commit v4 on v3

--- a/solution.py
+++ b/solution.py
@@ -212,7 +212,7 @@
 def token_experts(expert_in, gates, up_weight, down_weight):
     half = lax.axis_size("ctx") // 2
     up_t = jnp.swapaxes(up_weight, 1, 2)
-    turns = [0] + [s for s in (2, 1, 3) if 0 < s < half]
+    turns = [0] + [s for s in (1, 3, 2) if 0 < s < half]
     turns = list(dict.fromkeys(turns))
     come = {0: expert_in}
     for s in turns[1:]:
@@ -228,11 +228,16 @@
         near, far, near_out, far_out = dense_expert(blocks, gates[s], up_t, down_weight)
         far = add(far, swap_axis(far_out, "exp")).astype(BF16)
         held = far
-        block = add(near, swap_axis(near_out, "exp"), swap_axis(far, "ctx")).astype(BF16)
-        if s:
-            block = along_pairs(block, -s)
+        near = add(near, swap_axis(near_out, "exp"))
+        if s == 0:
+            home = near.astype(BF16), far
+            continue
+        block = add(near, swap_axis(far, "ctx")).astype(BF16)
+        last = block
+        block = along_pairs(block, -s)
         total = add(block) if total is None else add(total, block)
-    return total
+    near, far, _ = barrier(*home, last)
+    return add(total, near, swap_axis(far, "ctx"))
 
 
 def per_device(

time: 332 us -> 331 us (level)
  waiting for transfers between devices: 146 us -> 164 us
  starting transfers between devices: 49.5 us -> 38.3 us
  local copies, waits for them, and re-layouts: 36.5 us -> 31 us
    ppermute x6, waiting for transfers between devices: 28.4 us -> 42.3 us  [along_pairs(): return lax.ppermute(array, 'ctx', pairs)]
    ppermute x6, starting transfers between devices: 19.6 us -> 6.88 us  [along_pairs(): return lax.ppermute(array, 'ctx', pairs)]
    unnamed x78 -> x70, local copies, waits for them, and re-layouts: 28 us -> 22.4 us
    ppermute x24, waiting for transfers between devices: 55 us -> 59.2 us  [swap_axis(): return lax.ppermute(array, axis, [(i, i ^ 1) for i in range(count)])]
  transfers between devices with their start and end apart: 38 -> 38, of which waited for: 15 -> 16; matrix products, arithmetic and copies ran while one was open for 8% -> 8% of each run, Pallas kernels for 10% -> 10%
where the time goes in v4:
time: 331 us; the launch traced here: 326 us
  waiting for transfers between devices  164 us (50%)
  starting transfers between devices  38.3 us (12%)
  Pallas kernels  33.6 us (10%)
  local copies, waits for them, and re-layouts  31 us (9%)
  blocking collectives  17.5 us (5%)
  matrix products  16.7 us (5%)
  between operations  14.1 us (4%)
  other arithmetic  10.8 us (3%)
    ppermute x24, waiting for transfers between devices, swap_axis(): return lax.ppermute(array, axis, [(i, i ^ 1) for i in range(count)])  59.2 us
    ppermute x5, waiting for transfers between devices, from_behind(): return lax.ppermute(array, axis, pairs)  43.1 us
    ppermute x6, waiting for transfers between devices, along_pairs(): return lax.ppermute(array, 'ctx', pairs)  42.3 us
    pallas_call x4, Pallas kernels, dense_expert(): pl.pallas_call(functools.partial(dense_kernel, toks, count), out_shape=(j...  33.6 us
    unnamed x70, local copies, waits for them, and re-layouts  22.4 us
    all_gather x1, blocking collectives, per_device(): tables = lax.all_gather(table, ('ctx', 'exp'), axis=0)  17.5 us
    ppermute x24, starting transfers between devices, swap_axis(): return lax.ppermute(array, axis, [(i, i ^ 1) for i in range(count)])  16.2 us
    ppermute x5, starting transfers between devices, from_behind(): return lax.ppermute(array, axis, pairs)  13.5 us
  transfers between devices with their start and end apart: 38, of which 16 were waited for; matrix products, arithmetic and copies ran while one was open for 8% of the time, Pallas kernels for 10%

profile of v4, /device:TPU:13, one launch (start us, length us, event | category | flops | bytes accessed | tf_op | source)
XLA Modules:
  0.0 326.1 jit_solution(16769551028675634452)
XLA Ops:
  6.6 0.7 all-gather.4.cloned.1.call-update
  7.3 0.7 slice.93
  8.0 3.1 collective-permute-start
  11.2 0.7 slice.102
  12.0 3.1 collective-permute-start.1
  15.2 1.2 reduce-window.6
  16.9 0.7 select_reduce_fusion
  17.7 17.5 %all-gather.1 = f32[16,17,128]{2,1,0:T(8,128)S(1)} all-gather(f32[1,17,128]{2,1,0:T(8,128)S(1)} %fusion.53), channel_id=2, replica_groups=mesh['groups'=2,'ctx'=8,'exp'=2] {'ctx','exp'}, dimensions={0}, use_global_device_ids=true | all-gather | bytes 147968 | tf_op jit(solution)/shard_map/all_gather | solution.py:284
  36.7 0.8 multiply_convert_fusion.3
  39.5 1.3 collective-permute-start.2
  40.8 1.2 copy.105
  43.2 4.1 %collective-permute-done.2 = bf16[2,8,64,128]{3,2,1,0:T(8,128)(2,1)S(1)} collective-permute-done((bf16[2,8,64,128]{3,2,1,0:T(8,128)(2,1)S(1)}, bf16[2,8,64,128]{3,2,1,0:T(8,128)(2,1)S(1)}, u32[]{:S(2)}, u32[]{:S(2)}) %collective-permute-start.2) | collective-permute-done | bytes 262176 | tf_op jit(solution)/shard_map/ppermute | solution.py:37
  48.2 4.5 %collective-permute-start.4 = (bf16[2,8,64,128]{3,2,1,0:T(8,128)(2,1)S(1)}, bf16[2,8,64,128]{3,2,1,0:T(8,128)(2,1)S(1)}, u32[]{:S(2)}, u32[]{:S(2)}) collective-permute-start(bf16[2,8,64,128]{3,2,1,0:T(8,128)(2,1)S(1)} %fusion.33), channel_id=1, source_target_pairs={{0,8},{2,10},{4,12},{6,14},{1,9},{3,11},{5,13},{7,15},{16,24},{18,... | collective-permute-start | bytes 786440 | tf_op jit(solution)/shard_map/ppermute | solution.py:24
  52.7 2.1 collective-permute-start.5
  54.8 3.4 %fusion.16 = f32[256,2,8,64]{0,3,2,1:T(8,128)S(1)} fusion(bf16[256,2,8,64]{0,3,2,1:T(8,128)(2,1)S(1)} %bitcast.111, f32[256,256,2]{1,0,2:T(8,128)S(1)} %copy.103, f32[256,2,8]{0,2,1:T(8,128)S(1)} %bitcast.125, f32[256,2,8]{0,2,1:T(8,128)S(1)} %bitcast_bitcast_fusion, pred[256,256]{1,0:T(8,128)(4,1)S(1)} %iota_compare_fusion), kind=kOutput, calls=%fused_computation.29 | convolution fusion | flops 810549248 | bytes 2195456 | tf_op jit(solution)/shard_map/tsgr,sgrp->tgrp/dot_general | solution.py:323
  58.2 24.0 %collective-permute-done.4 = bf16[2,8,64,128]{3,2,1,0:T(8,128)(2,1)S(1)} collective-permute-done((bf16[2,8,64,128]{3,2,1,0:T(8,128)(2,1)S(1)}, bf16[2,8,64,128]{3,2,1,0:T(8,128)(2,1)S(1)}, u32[]{:S(2)}, u32[]{:S(2)}) %collective-permute-start.4) | collective-permute-done | bytes 262176 | tf_op jit(solution)/shard_map/ppermute | solution.py:24
  82.2 19.1 %collective-permute-done.5 = bf16[2,8,64,128]{3,2,1,0:T(8,128)(2,1)S(1)} collective-permute-done((bf16[2,8,64,128]{3,2,1,0:T(8,128)(2,1)S(1)}, bf16[2,8,64,128]{3,2,1,0:T(8,128)(2,1)S(1)}, u32[]{:S(2)}, u32[]{:S(2)}) %collective-permute-start.5) | collective-permute-done | bytes 262176 | tf_op jit(solution)/shard_map/ppermute | solution.py:24
  101.3 2.2 multiply_reduce_fusion.1
  104.2 1.6 copy.104
  106.2 11.7 %all-gather.4.cloned.1.call-done = bf16[2688,1024]{1,0:T(8,128)(2,1)} async-done(((bf16[336,1024]{1,0:T(8,128)(2,1)}), bf16[2688,1024]{1,0:T(8,128)(2,1)}) %all-gather.4.cloned.1.call-update) | async-done | bytes 5505040 | tf_op jit(solution)/shard_map/all_gather | solution.py:270
  117.9 5.5 %fusion.44 = f32[128,2688]{1,0:T(8,128)} fusion(bf16[2688,1024]{1,0:T(8,128)(2,1)} %all-gather.4.cloned.1.call-done, bf16[256,1024]{1,0:T(8,128)(2,1)S(1)} %multiply_convert_fusion.1, s32[]{:T(128)S(6)} %select_n.142), kind=kOutput, calls=%fused_computation.76 | convolution fusion | flops 704643072 | bytes 7143428 | tf_op jit(solution)/shard_map/dot_general | solution.py:339
  123.9 3.0 collective-permute-done.6
  126.9 4.6 %multiply_reduce_fusion = (f32[128]{0:T(128)S(1)}, f32[128,2688]{1,0:T(8,128)S(1)}) fusion(f32[128,2688]{1,0:T(8,128)S(1)} %collective-permute-done.6, bf16[2688,1024]{1,0:T(8,128)(2,1)} %all-gather.4.cloned.1.call-done, bf16[256,1024]{1,0:T(8,128)(2,1)S(1)} %multiply_convert_fusion.1, s32[]{:T(128)S(6)} %select_n.141, bf16[128,2688]{1,0:T(8,128)(2,1)S(1)} %copy-done.22), kind=kOutput, calls=%fused_computation.28 | convolution fusion | flops 707051392 | bytes 9208324 | tf_op jit(solution)/shard_map/dot_general | solution.py:339
  131.9 0.7 collective-permute-start.12
  132.6 15.8 %collective-permute-done.11.refs_1_ = bf16[128,2688]{1,0:T(8,128)(2,1)S(1)} collective-permute-done((bf16[128,2688]{1,0:T(8,128)(2,1)S(1)}, bf16[128,2688]{1,0:T(8,128)(2,1)S(1)}, u32[]{:S(2)}, u32[]{:S(2)}) %collective-permute-start.11) | collective-permute-done | bytes 688160 | tf_op jit(solution)/shard_map/ppermute | solution.py:193
  148.4 1.2 collective-permute-start.13
  149.6 0.8 copy-done.10
  150.7 0.8 constant_dynamic-slice_fusion
  152.3 3.5 %collective-permute-start.27 = (bf16[128,2688]{1,0:T(8,128)(2,1)S(1)}, bf16[128,2688]{1,0:T(8,128)(2,1)}, u32[]{:S(2)}, u32[]{:S(2)}) collective-permute-start(bf16[128,2688]{1,0:T(8,128)(2,1)S(1)} %multiply_convert_fusion.refs_0_), channel_id=1, source_target_pairs={{0,8},{2,10},{4,12},{6,14},{8,0},{10,2},{12,4},{14,6},{1,9},{3,11}... | collective-permute-start | bytes 2064392 | tf_op jit(solution)/shard_map/ppermute | solution.py:201
  155.9 0.9 copy-done.12
  156.8 2.4 copy-done.2
  159.2 2.4 copy-done.5
  161.7 1.1 copy-done.11
  162.8 1.1 copy-done.13
  163.9 8.8 %shard_map.163 = (bf16[128,2688]{1,0:T(8,128)(2,1)S(1)}, bf16[128,2688]{1,0:T(8,128)(2,1)S(1)}, bf16[128,2688]{1,0:T(8,128)(2,1)S(1)}, bf16[128,2688]{1,0:T(8,128)(2,1)}) custom-call(f32[512,1]{1,0:T(8,128)S(1)} %copy.107.gate_ref, bf16[128,2688]{1,0:T(8,128)(2,1)S(1)} %multiply_convert_fusion.refs_0_, bf16[128,2688]{1,0:T(8,128)(2,1)S(1)} %copy-done.11, ...), custom_call_target="tpu_custom_call" | custom-call | flops 5505024 | bytes 512 | tf_op jit(solution)/shard_map/pallas_call | solution.py:175
  172.7 0.9 copy-done.14
  174.3 1.5 collective-permute-start.20
  175.8 24.4 %collective-permute-done.27.refs_0_ = bf16[128,2688]{1,0:T(8,128)(2,1)} collective-permute-done((bf16[128,2688]{1,0:T(8,128)(2,1)S(1)}, bf16[128,2688]{1,0:T(8,128)(2,1)}, u32[]{:S(2)}, u32[]{:S(2)}) %collective-permute-start.27) | collective-permute-done | bytes 688160 | tf_op jit(solution)/shard_map/ppermute | solution.py:201
  200.3 1.1 collective-permute-start.10
  201.3 2.1 add_convert_fusion.8
  203.4 2.4 copy-done.3
  205.9 2.4 copy-done.6
  208.3 8.6 %shard_map.164 = (bf16[128,2688]{1,0:T(8,128)(2,1)S(1)}, bf16[128,2688]{1,0:T(8,128)(2,1)S(1)}, bf16[128,2688]{1,0:T(8,128)(2,1)S(1)}, bf16[128,2688]{1,0:T(8,128)(2,1)}) custom-call(f32[512,1]{1,0:T(8,128)S(1)} %copy.108.gate_ref, bf16[128,2688]{1,0:T(8,128)(2,1)S(1)} %copy-done.9, bf16[128,2688]{1,0:T(8,128)(2,1)} %collective-permute-done.8.refs_1_, ...), custom_call_target="tpu_custom_call" | custom-call | flops 5505024 | bytes 512 | tf_op jit(solution)/shard_map/pallas_call | solution.py:175
  216.9 0.9 copy-done.15
  219.4 0.8 collective-permute-done.16
  220.5 1.3 add_convert_fusion.7
  222.1 1.9 collective-permute-done.22.refs_3_
  224.1 2.4 copy-done.4
  226.5 2.4 copy-done.7
  228.9 8.1 %shard_map.165 = (bf16[128,2688]{1,0:T(8,128)(2,1)S(1)}, bf16[128,2688]{1,0:T(8,128)(2,1)S(1)}, bf16[128,2688]{1,0:T(8,128)(2,1)S(1)}, bf16[128,2688]{1,0:T(8,128)(2,1)S(1)}) custom-call(f32[512,1]{1,0:T(8,128)S(1)} %copy.109.gate_ref, bf16[128,2688]{1,0:T(8,128)(2,1)} %collective-permute-done.19.refs_0_, bf16[128,2688]{1,0:T(8,128)(2,1)} %collective-permute-done.20.refs_1_, ...), custom_call_target="tpu_custom_call" | custom-call | flops 5505024 | bytes 512 | tf_op jit(solution)/shard_map/pallas_call | solution.py:175
  237.4 1.5 collective-permute-start.17
  239.6 1.4 collective-permute-start.25
  241.0 8.1 %shard_map.166 = (bf16[128,2688]{1,0:T(8,128)(2,1)S(1)}, bf16[128,2688]{1,0:T(8,128)(2,1)S(1)}, bf16[128,2688]{1,0:T(8,128)(2,1)S(1)}, bf16[128,2688]{1,0:T(8,128)(2,1)S(1)}) custom-call(f32[512,1]{1,0:T(8,128)S(1)} %copy.110.gate_ref, bf16[128,2688]{1,0:T(8,128)(2,1)} %collective-permute-done.27.refs_0_, bf16[128,2688]{1,0:T(8,128)(2,1)} %collective-permute-done.28.refs_1_, ...), custom_call_target="tpu_custom_call" | custom-call | flops 5505024 | bytes 512 | tf_op jit(solution)/shard_map/pallas_call | solution.py:175
  249.8 4.5 %collective-permute-done.17 = bf16[128,2688]{1,0:T(8,128)(2,1)S(1)} collective-permute-done((bf16[128,2688]{1,0:T(8,128)(2,1)S(1)}, bf16[128,2688]{1,0:T(8,128)(2,1)S(1)}, u32[]{:S(2)}, u32[]{:S(2)}) %collective-permute-start.17) | collective-permute-done | bytes 688160 | tf_op jit(solution)/shard_map/ppermute | solution.py:193
  254.6 2.0 collective-permute-start.31
  256.8 1.4 collective-permute-start.33
  258.2 10.8 %collective-permute-done.25 = bf16[128,2688]{1,0:T(8,128)(2,1)S(1)} collective-permute-done((bf16[128,2688]{1,0:T(8,128)(2,1)S(1)}, bf16[128,2688]{1,0:T(8,128)(2,1)S(1)}, u32[]{:S(2)}, u32[]{:S(2)}) %collective-permute-start.25) | collective-permute-done | bytes 688160 | tf_op jit(solution)/shard_map/ppermute | solution.py:193
  269.3 14.4 %collective-permute-done.33 = bf16[128,2688]{1,0:T(8,128)(2,1)S(1)} collective-permute-done((bf16[128,2688]{1,0:T(8,128)(2,1)S(1)}, bf16[128,2688]{1,0:T(8,128)(2,1)S(1)}, u32[]{:S(2)}, u32[]{:S(2)}) %collective-permute-start.33) | collective-permute-done | bytes 688160 | tf_op jit(solution)/shard_map/ppermute | solution.py:193
  284.0 0.8 copy-done.21
  284.8 1.4 collective-permute-start.36
  286.2 3.2 collective-permute-start.34
  290.1 10.6 %collective-permute-done.36 = bf16[128,2688]{1,0:T(8,128)(2,1)S(1)} collective-permute-done((bf16[128,2688]{1,0:T(8,128)(2,1)S(1)}, bf16[128,2688]{1,0:T(8,128)(2,1)S(1)}, u32[]{:S(2)}, u32[]{:S(2)}) %collective-permute-start.36) | collective-permute-done | bytes 688160 | tf_op jit(solution)/shard_map/ppermute | solution.py:193
  300.7 17.3 %collective-permute-done.34 = bf16[128,2688]{1,0:T(8,128)(2,1)S(1)} collective-permute-done((bf16[128,2688]{1,0:T(8,128)(2,1)S(1)}, bf16[128,2688]{1,0:T(8,128)(2,1)S(1)}, u32[]{:S(2)}, u32[]{:S(2)}) %collective-permute-start.34) | collective-permute-done | bytes 688160 | tf_op jit(solution)/shard_map/ppermute | solution.py:201
  318.0 1.3 add_convert_fusion
  (165 shorter events, 15.6 us)
Async XLA Ops:
  6.5 8.7 %copy-start = (f32[256,16]{0,1:T(8,128)S(1)}, f32[256,16]{0,1:T(8,128)}, u32[]{:S(2)}) copy-start(f32[256,16]{0,1:T(8,128)} %param.21) | copy-start | bytes 49156
  6.5 29.7 %copy-start.24 = (bf16[256,2,256]{2,1,0:T(2,128)(2,1)S(1)}, bf16[256,2,256]{2,1,0:T(2,128)(2,1)}, u32[]{:S(2)}) copy-start(bf16[256,2,256]{2,1,0:T(2,128)(2,1)} %param.18) | copy-start | bytes 786436
  6.5 29.5 %copy-start.29 = (bf16[4,2,256]{2,1,0:T(2,128)(2,1)S(1)}, bf16[4,2,256]{2,1,0:T(2,128)(2,1)}, u32[]{:S(2)}) copy-start(bf16[4,2,256]{2,1,0:T(2,128)(2,1)} %param.23) | copy-start | bytes 12292
  6.5 29.6 %copy-start.26 = (bf16[4,1024]{1,0:T(4,128)(2,1)S(1)}, bf16[4,1024]{1,0:T(4,128)(2,1)}, u32[]{:S(2)}) copy-start(bf16[4,1024]{1,0:T(4,128)(2,1)} %param.22) | copy-start | bytes 24580
  6.5 29.6 %copy-start.27 = (f32[256,16]{0,1:T(8,128)S(1)}, f32[256,16]{0,1:T(8,128)}, u32[]{:S(2)}) copy-start(f32[256,16]{0,1:T(8,128)} %param.20) | copy-start | bytes 49156
  6.5 111.4 %all-gather.4.cloned.1.call-start = ((), (), s32[]{:S(2)}) async-start(), calls=%async_computation | async-start | bytes 6193152 | tf_op jit(solution)/shard_map/all_gather | solution.py:270
  8.0 29.6 %collective-permute-start = (bf16[3,1024]{1,0:T(4,128)(2,1)S(1)}, bf16[3,1024]{1,0:T(4,128)(2,1)S(1)}, u32[]{:S(2)}, u32[]{:S(2)}) collective-permute-start(bf16[3,1024]{1,0:T(4,128)(2,1)S(1)} %slice.93), channel_id=1, source_target_pairs={{0,2},{2,4},{4,6},{6,8},{8,10},{10,12},{12,14},{1,3},{3,5},{5,7},{... | collective-permute-start | bytes 18440 | tf_op jit(solution)/shard_map/ppermute | solution.py:24
  12.0 24.5 %collective-permute-start.1 = (bf16[3,2,256]{0,2,1:T(8,128)(2,1)S(1)}, bf16[3,2,256]{0,2,1:T(8,128)(2,1)S(1)}, u32[]{:S(2)}, u32[]{:S(2)}) collective-permute-start(bf16[3,2,256]{0,2,1:T(8,128)(2,1)S(1)} %copy.97), channel_id=1, source_target_pairs={{0,2},{2,4},{4,6},{6,8},{8,10},{10,12},{12,14},{1,3},{3,5},{5,7},{... | collective-permute-start | bytes 9224 | tf_op jit(solution)/shard_map/ppermute | solution.py:24
  38.6 2.2 copy-start.19
  38.8 3.2 copy-start.32
  38.8 3.9 %copy-start.30 = (bf16[1024]{0:T(1024)(128)(2,1)S(1)}, bf16[1024]{0:T(1024)(128)(2,1)}, u32[]{:S(2)}) copy-start(bf16[1024]{0:T(1024)(128)(2,1)} %param.26) | copy-start | bytes 6148
  39.5 7.8 %collective-permute-start.2 = (bf16[2,8,64,128]{3,2,1,0:T(8,128)(2,1)S(1)}, bf16[2,8,64,128]{3,2,1,0:T(8,128)(2,1)S(1)}, u32[]{:S(2)}, u32[]{:S(2)}) collective-permute-start(bf16[2,8,64,128]{3,2,1,0:T(8,128)(2,1)S(1)} %get-tuple-element.86), channel_id=1, source_target_pairs={{0,2},{2,0},{4,6},{6,4},{8,10},{10,8},{12,14},{14,12},{1,3},{3,1},... | collective-permute-start | bytes 786440 | tf_op jit(solution)/shard_map/ppermute | solution.py:37
  47.5 10.7 %collective-permute-start.3 = (bf16[2,8,64,128]{3,2,1,0:T(8,128)(2,1)S(1)}, bf16[2,8,64,128]{3,2,1,0:T(8,128)(2,1)S(1)}, u32[]{:S(2)}, u32[]{:S(2)}) collective-permute-start(bf16[2,8,64,128]{3,2,1,0:T(8,128)(2,1)S(1)} %fusion.33), channel_id=1, source_target_pairs={{0,12},{2,14},{1,13},{3,15},{16,28},{18,30},{17,29},{19,31}} | collective-permute-start | bytes 786440 | tf_op jit(solution)/shard_map/ppermute | solution.py:24
  48.2 34.0 %collective-permute-start.4 = (bf16[2,8,64,128]{3,2,1,0:T(8,128)(2,1)S(1)}, bf16[2,8,64,128]{3,2,1,0:T(8,128)(2,1)S(1)}, u32[]{:S(2)}, u32[]{:S(2)}) collective-permute-start(bf16[2,8,64,128]{3,2,1,0:T(8,128)(2,1)S(1)} %fusion.33), channel_id=1, source_target_pairs={{0,8},{2,10},{4,12},{6,14},{1,9},{3,11},{5,13},{7,15},{16,24},{18,... | collective-permute-start | bytes 786440 | tf_op jit(solution)/shard_map/ppermute | solution.py:24
  52.7 48.6 %collective-permute-start.5 = (bf16[2,8,64,128]{3,2,1,0:T(8,128)(2,1)S(1)}, bf16[2,8,64,128]{3,2,1,0:T(8,128)(2,1)S(1)}, u32[]{:S(2)}, u32[]{:S(2)}) collective-permute-start(bf16[2,8,64,128]{3,2,1,0:T(8,128)(2,1)S(1)} %fusion.33), channel_id=1, source_target_pairs={{0,4},{2,6},{4,8},{6,10},{8,12},{10,14},{1,5},{3,7},{5,9},{7,11},{... | collective-permute-start | bytes 786440 | tf_op jit(solution)/shard_map/ppermute | solution.py:24
  54.8 46.5 %copy-start.20 = (f32[256,1024]{0,1:T(8,128)S(1)}, f32[256,1024]{0,1:T(8,128)}, u32[]{:S(2)}) copy-start(f32[256,1024]{0,1:T(8,128)} %copy.105) | copy-start | bytes 3145732
  54.8 46.5 %copy-start.31 = (bf16[16,64,128]{2,1,0:T(8,128)(2,1)S(1)}, bf16[16,64,128]{2,1,0:T(8,128)(2,1)}, u32[]{:S(2)}) copy-start(bf16[16,64,128]{2,1,0:T(8,128)(2,1)} %param.25) | copy-start | bytes 786436
  54.8 46.5 %copy-start.33 = (f32[2,8]{1,0:T(2,128)S(1)}, f32[2,8]{1,0:T(2,128)}, u32[]{:S(2)}) copy-start(f32[2,8]{1,0:T(2,128)} %mul.362) | copy-start | bytes 196
  106.2 17.7 %copy-start.28 = (bf16[2688]{0:T(1024)(128)(2,1)S(1)}, bf16[2688]{0:T(1024)(128)(2,1)}, u32[]{:S(2)}) copy-start(bf16[2688]{0:T(1024)(128)(2,1)} %param.29) | copy-start | bytes 16132
  106.2 20.7 %copy-start.22 = (bf16[128,2688]{1,0:T(8,128)(2,1)S(1)}, bf16[128,2688]{1,0:T(8,128)(2,1)}, u32[]{:S(2)}) copy-start(bf16[128,2688]{1,0:T(8,128)(2,1)} %param.28) | copy-start | bytes 2064388
  123.5 3.4 %collective-permute-start.6 = (f32[128,2688]{1,0:T(8,128)}, f32[128,2688]{1,0:T(8,128)S(1)}, u32[]{:S(2)}, u32[]{:S(2)}) collective-permute-start(f32[128,2688]{1,0:T(8,128)} %fusion.44), channel_id=1, source_target_pairs={{0,1},{1,0},{2,3},{3,2},{4,5},{5,4},{6,7},{7,6},{8,9},{9,8},{10,11... | collective-permute-start | bytes 4128776 | tf_op jit(solution)/shard_map/ppermute | solution.py:341
  131.5 18.1 %copy-start.17 = (f32[128,2688]{1,0:T(8,128)}, f32[128,2688]{1,0:T(8,128)S(1)}, u32[]{:S(2)}) copy-start(f32[128,2688]{1,0:T(8,128)S(1)} %get-tuple-element.91) | copy-start | bytes 4128772
  131.7 16.7 %collective-permute-start.11 = (bf16[128,2688]{1,0:T(8,128)(2,1)S(1)}, bf16[128,2688]{1,0:T(8,128)(2,1)S(1)}, u32[]{:S(2)}, u32[]{:S(2)}) collective-permute-start(bf16[128,2688]{1,0:T(8,128)(2,1)S(1)} %multiply_convert_fusion.refs_0_), channel_id=1, source_target_pairs={{0,2},{2,0},{4,6},{6,4},{8,10},{10,8},{12,14},{14,12},{1,3},{3,1},... | collective-permute-start | bytes 2064392 | tf_op jit(solution)/shard_map/ppermute | solution.py:193
  131.9 24.0 %collective-permute-start.12 = (bf16[128,2688]{1,0:T(8,128)(2,1)S(1)}, bf16[128,2688]{1,0:T(8,128)(2,1)S(1)}, u32[]{:S(2)}, u32[]{:S(2)}) collective-permute-start(bf16[128,2688]{1,0:T(8,128)(2,1)S(1)} %multiply_convert_fusion.refs_0_), channel_id=1, source_target_pairs={{0,1},{1,0},{2,3},{3,2},{4,5},{5,4},{6,7},{7,6},{8,9},{9,8},{10,11... | collective-permute-start | bytes 2064392 | tf_op jit(solution)/shard_map/ppermute | solution.py:193
  132.6 23.2 %collective-permute-start.7 = (bf16[128,2688]{1,0:T(8,128)(2,1)S(1)}, bf16[128,2688]{1,0:T(8,128)(2,1)S(1)}, u32[]{:S(2)}, u32[]{:S(2)}) collective-permute-start(bf16[128,2688]{1,0:T(8,128)(2,1)S(1)} %multiply_convert_fusion.refs_0_), channel_id=1, source_target_pairs={{0,4},{2,6},{4,8},{6,10},{8,12},{10,14},{12,0},{14,2},{1,5},{3,7},... | collective-permute-start | bytes 2064392 | tf_op jit(solution)/shard_map/ppermute | solution.py:201
  148.4 8.4 %collective-permute-start.13 = (bf16[128,2688]{1,0:T(8,128)(2,1)S(1)}, bf16[128,2688]{1,0:T(8,128)(2,1)}, u32[]{:S(2)}, u32[]{:S(2)}) collective-permute-start(bf16[128,2688]{1,0:T(8,128)(2,1)S(1)} %collective-permute-done.11.refs_1_), channel_id=1, source_target_pairs={{0,1},{1,0},{2,3},{3,2},{4,5},{5,4},{6,7},{7,6},{8,9},{9,8},{10,11... | collective-permute-start | bytes 2064392 | tf_op jit(solution)/shard_map/ppermute | solution.py:193
  152.2 22.0 %collective-permute-start.19 = (bf16[128,2688]{1,0:T(8,128)(2,1)S(1)}, bf16[128,2688]{1,0:T(8,128)(2,1)}, u32[]{:S(2)}, u32[]{:S(2)}) collective-permute-start(bf16[128,2688]{1,0:T(8,128)(2,1)S(1)} %multiply_convert_fusion.refs_0_), channel_id=1, source_target_pairs={{0,12},{2,14},{4,0},{6,2},{8,4},{10,6},{12,8},{14,10},{1,13},{3,15... | collective-permute-start | bytes 2064392 | tf_op jit(solution)/shard_map/ppermute | solution.py:201
  152.3 47.9 %collective-permute-start.27 = (bf16[128,2688]{1,0:T(8,128)(2,1)S(1)}, bf16[128,2688]{1,0:T(8,128)(2,1)}, u32[]{:S(2)}, u32[]{:S(2)}) collective-permute-start(bf16[128,2688]{1,0:T(8,128)(2,1)S(1)} %multiply_convert_fusion.refs_0_), channel_id=1, source_target_pairs={{0,8},{2,10},{4,12},{6,14},{8,0},{10,2},{12,4},{14,6},{1,9},{3,11}... | collective-permute-start | bytes 2064392 | tf_op jit(solution)/shard_map/ppermute | solution.py:201
  155.8 18.4 %copy-start.8 = (bf16[128,2688]{1,0:T(8,128)(2,1)}, bf16[128,2688]{1,0:T(8,128)(2,1)S(1)}, u32[]{:S(2)}) copy-start(bf16[128,2688]{1,0:T(8,128)(2,1)S(1)} %collective-permute-done.7.refs_0_) | copy-start | bytes 2064388
  155.8 44.4 %collective-permute-start.8 = (bf16[128,2688]{1,0:T(8,128)(2,1)S(1)}, bf16[128,2688]{1,0:T(8,128)(2,1)}, u32[]{:S(2)}, u32[]{:S(2)}) collective-permute-start(bf16[128,2688]{1,0:T(8,128)(2,1)S(1)} %collective-permute-done.7.refs_0_), channel_id=1, source_target_pairs={{0,2},{2,0},{4,6},{6,4},{8,10},{10,8},{12,14},{14,12},{1,3},{3,1},... | collective-permute-start | bytes 2064392 | tf_op jit(solution)/shard_map/ppermute | solution.py:193
  156.8 2.4 copy-start.2
  159.2 2.4 copy-start.5
  173.6 27.8 %collective-permute-start.14 = (bf16[128,2688]{1,0:T(8,128)(2,1)}, bf16[128,2688]{1,0:T(8,128)(2,1)}, u32[]{:S(2)}, u32[]{:S(2)}) collective-permute-start(bf16[128,2688]{1,0:T(8,128)(2,1)} %get-tuple-element.36), channel_id=1, source_target_pairs={{0,1},{1,0},{2,3},{3,2},{4,5},{5,4},{6,7},{7,6},{8,9},{9,8},{10,11... | collective-permute-start | bytes 2064392 | tf_op jit(solution)/shard_map/ppermute | solution.py:193
  174.2 29.2 %collective-permute-start.9 = (bf16[128,2688]{1,0:T(8,128)(2,1)S(1)}, bf16[128,2688]{1,0:T(8,128)(2,1)S(1)}, u32[]{:S(2)}, u32[]{:S(2)}) collective-permute-start(bf16[128,2688]{1,0:T(8,128)(2,1)S(1)} %collective-permute-done.7.refs_0_), channel_id=1, source_target_pairs={{0,1},{1,0},{2,3},{3,2},{4,5},{5,4},{6,7},{7,6},{8,9},{9,8},{10,11... | collective-permute-start | bytes 2064392 | tf_op jit(solution)/shard_map/ppermute | solution.py:193
  174.3 29.1 %copy-start.9 = (bf16[128,2688]{1,0:T(8,128)(2,1)S(1)}, bf16[128,2688]{1,0:T(8,128)(2,1)}, u32[]{:S(2)}) copy-start(bf16[128,2688]{1,0:T(8,128)(2,1)} %copy-done.8) | copy-start | bytes 2064388
  174.3 44.6 %collective-permute-start.20 = (bf16[128,2688]{1,0:T(8,128)(2,1)}, bf16[128,2688]{1,0:T(8,128)(2,1)}, u32[]{:S(2)}, u32[]{:S(2)}) collective-permute-start(bf16[128,2688]{1,0:T(8,128)(2,1)} %collective-permute-done.19.refs_0_), channel_id=1, source_target_pairs={{0,2},{2,0},{4,6},{6,4},{8,10},{10,8},{12,14},{14,12},{1,3},{3,1},... | collective-permute-start | bytes 2064392 | tf_op jit(solution)/shard_map/ppermute | solution.py:193
  200.2 19.0 %collective-permute-start.28 = (bf16[128,2688]{1,0:T(8,128)(2,1)}, bf16[128,2688]{1,0:T(8,128)(2,1)}, u32[]{:S(2)}, u32[]{:S(2)}) collective-permute-start(bf16[128,2688]{1,0:T(8,128)(2,1)} %collective-permute-done.27.refs_0_), channel_id=1, source_target_pairs={{0,2},{2,0},{4,6},{6,4},{8,10},{10,8},{12,14},{14,12},{1,3},{3,1},... | collective-permute-start | bytes 2064392 | tf_op jit(solution)/shard_map/ppermute | solution.py:193
  200.3 3.2 collective-permute-start.10
  203.4 2.4 copy-start.3
  205.9 2.4 copy-start.6
  217.8 4.0 %copy-start.16 = (bf16[128,2688]{1,0:T(8,128)(2,1)S(1)}, bf16[128,2688]{1,0:T(8,128)(2,1)}, u32[]{:S(2)}) copy-start(bf16[128,2688]{1,0:T(8,128)(2,1)} %copy-done.15) | copy-start | bytes 2064388
  217.8 2.5 collective-permute-start.16
  218.3 3.4 %collective-permute-start.21 = (bf16[128,2688]{1,0:T(8,128)(2,1)}, bf16[128,2688]{1,0:T(8,128)(2,1)S(1)}, u32[]{:S(2)}, u32[]{:S(2)}) collective-permute-start(bf16[128,2688]{1,0:T(8,128)(2,1)} %collective-permute-done.19.refs_0_), channel_id=1, source_target_pairs={{0,1},{1,0},{2,3},{3,2},{4,5},{5,4},{6,7},{7,6},{8,9},{9,8},{10,11... | collective-permute-start | bytes 2064392 | tf_op jit(solution)/shard_map/ppermute | solution.py:193
  218.6 21.0 %collective-permute-start.29 = (bf16[128,2688]{1,0:T(8,128)(2,1)}, bf16[128,2688]{1,0:T(8,128)(2,1)S(1)}, u32[]{:S(2)}, u32[]{:S(2)}) collective-permute-start(bf16[128,2688]{1,0:T(8,128)(2,1)} %collective-permute-done.27.refs_0_), channel_id=1, source_target_pairs={{0,1},{1,0},{2,3},{3,2},{4,5},{5,4},{6,7},{7,6},{8,9},{9,8},{10,11... | collective-permute-start | bytes 2064392 | tf_op jit(solution)/shard_map/ppermute | solution.py:193
  218.9 18.4 %collective-permute-start.35 = (bf16[128,2688]{1,0:T(8,128)(2,1)}, bf16[128,2688]{1,0:T(8,128)(2,1)S(1)}, u32[]{:S(2)}, u32[]{:S(2)}) collective-permute-start(bf16[128,2688]{1,0:T(8,128)(2,1)} %copy-done.14), channel_id=1, source_target_pairs={{0,1},{1,0},{2,3},{3,2},{4,5},{5,4},{6,7},{7,6},{8,9},{9,8},{10,11... | collective-permute-start | bytes 2064392 | tf_op jit(solution)/shard_map/ppermute | solution.py:193
  219.2 4.9 %collective-permute-start.22 = (bf16[128,2688]{1,0:T(8,128)(2,1)}, bf16[128,2688]{1,0:T(8,128)(2,1)S(1)}, u32[]{:S(2)}, u32[]{:S(2)}) collective-permute-start(bf16[128,2688]{1,0:T(8,128)(2,1)} %collective-permute-done.20.refs_1_), channel_id=1, source_target_pairs={{0,1},{1,0},{2,3},{3,2},{4,5},{5,4},{6,7},{7,6},{8,9},{9,8},{10,11... | collective-permute-start | bytes 2064392 | tf_op jit(solution)/shard_map/ppermute | solution.py:193
  220.2 20.8 %collective-permute-start.30 = (bf16[128,2688]{1,0:T(8,128)(2,1)}, bf16[128,2688]{1,0:T(8,128)(2,1)S(1)}, u32[]{:S(2)}, u32[]{:S(2)}) collective-permute-start(bf16[128,2688]{1,0:T(8,128)(2,1)} %collective-permute-done.28.refs_1_), channel_id=1, source_target_pairs={{0,1},{1,0},{2,3},{3,2},{4,5},{5,4},{6,7},{7,6},{8,9},{9,8},{10,11... | collective-permute-start | bytes 2064392 | tf_op jit(solution)/shard_map/ppermute | solution.py:193
  221.8 28.0 %collective-permute-start.15 = (bf16[128,2688]{1,0:T(8,128)(2,1)S(1)}, bf16[128,2688]{1,0:T(8,128)(2,1)S(1)}, u32[]{:S(2)}, u32[]{:S(2)}) collective-permute-start(bf16[128,2688]{1,0:T(8,128)(2,1)S(1)} %copy-done.16), channel_id=1, source_target_pairs={{0,1},{1,0},{2,3},{3,2},{4,5},{5,4},{6,7},{7,6},{8,9},{9,8},{10,11... | collective-permute-start | bytes 2064392 | tf_op jit(solution)/shard_map/ppermute | solution.py:193
  224.1 2.4 copy-start.4
  226.5 2.4 copy-start.7
  237.0 2.2 collective-permute-start.24
  237.4 16.8 %collective-permute-start.17 = (bf16[128,2688]{1,0:T(8,128)(2,1)S(1)}, bf16[128,2688]{1,0:T(8,128)(2,1)S(1)}, u32[]{:S(2)}, u32[]{:S(2)}) collective-permute-start(bf16[128,2688]{1,0:T(8,128)(2,1)S(1)} %add_convert_fusion.7), channel_id=1, source_target_pairs={{0,2},{2,0},{4,6},{6,4},{8,10},{10,8},{12,14},{14,12},{1,3},{3,1},... | collective-permute-start | bytes 2064392 | tf_op jit(solution)/shard_map/ppermute | solution.py:193
  239.2 19.1 %collective-permute-start.23 = (bf16[128,2688]{1,0:T(8,128)(2,1)S(1)}, bf16[128,2688]{1,0:T(8,128)(2,1)S(1)}, u32[]{:S(2)}, u32[]{:S(2)}) collective-permute-start(bf16[128,2688]{1,0:T(8,128)(2,1)S(1)} %get-tuple-element.50), channel_id=1, source_target_pairs={{0,1},{1,0},{2,3},{3,2},{4,5},{5,4},{6,7},{7,6},{8,9},{9,8},{10,11... | collective-permute-start | bytes 2064392 | tf_op jit(solution)/shard_map/ppermute | solution.py:193
  239.6 29.4 %collective-permute-start.25 = (bf16[128,2688]{1,0:T(8,128)(2,1)S(1)}, bf16[128,2688]{1,0:T(8,128)(2,1)S(1)}, u32[]{:S(2)}, u32[]{:S(2)}) collective-permute-start(bf16[128,2688]{1,0:T(8,128)(2,1)S(1)} %add_convert_fusion.5), channel_id=1, source_target_pairs={{0,2},{2,0},{4,6},{6,4},{8,10},{10,8},{12,14},{14,12},{1,3},{3,1},... | collective-permute-start | bytes 2064392 | tf_op jit(solution)/shard_map/ppermute | solution.py:193
  249.1 7.5 %collective-permute-start.32 = (bf16[128,2688]{1,0:T(8,128)(2,1)S(1)}, bf16[128,2688]{1,0:T(8,128)(2,1)S(1)}, u32[]{:S(2)}, u32[]{:S(2)}) collective-permute-start(bf16[128,2688]{1,0:T(8,128)(2,1)S(1)} %get-tuple-element.60), channel_id=1, source_target_pairs={{0,1},{1,0},{2,3},{3,2},{4,5},{5,4},{6,7},{7,6},{8,9},{9,8},{10,11... | collective-permute-start | bytes 2064392 | tf_op jit(solution)/shard_map/ppermute | solution.py:193
  254.5 34.9 %collective-permute-start.18 = (bf16[128,2688]{1,0:T(8,128)(2,1)S(1)}, bf16[128,2688]{1,0:T(8,128)(2,1)S(1)}, u32[]{:S(2)}, u32[]{:S(2)}) collective-permute-start(bf16[128,2688]{1,0:T(8,128)(2,1)S(1)} %add_convert_fusion.6), channel_id=1, source_target_pairs={{0,12},{2,14},{4,0},{6,2},{8,4},{10,6},{12,8},{14,10},{1,13},{3,15... | collective-permute-start | bytes 2064392 | tf_op jit(solution)/shard_map/ppermute | solution.py:201
  254.6 14.7 %collective-permute-start.31 = (bf16[128,2688]{1,0:T(8,128)(2,1)S(1)}, bf16[128,2688]{1,0:T(8,128)(2,1)S(1)}, u32[]{:S(2)}, u32[]{:S(2)}) collective-permute-start(bf16[128,2688]{1,0:T(8,128)(2,1)S(1)} %get-tuple-element.58), channel_id=1, source_target_pairs={{0,1},{1,0},{2,3},{3,2},{4,5},{5,4},{6,7},{7,6},{8,9},{9,8},{10,11... | collective-permute-start | bytes 2064392 | tf_op jit(solution)/shard_map/ppermute | solution.py:193
  256.8 27.0 %collective-permute-start.33 = (bf16[128,2688]{1,0:T(8,128)(2,1)S(1)}, bf16[128,2688]{1,0:T(8,128)(2,1)S(1)}, u32[]{:S(2)}, u32[]{:S(2)}) collective-permute-start(bf16[128,2688]{1,0:T(8,128)(2,1)S(1)} %add_convert_fusion.3), channel_id=1, source_target_pairs={{0,2},{2,0},{4,6},{6,4},{8,10},{10,8},{12,14},{14,12},{1,3},{3,1},... | collective-permute-start | bytes 2064392 | tf_op jit(solution)/shard_map/ppermute | solution.py:193
  269.3 20.8 %collective-permute-start.26 = (bf16[128,2688]{1,0:T(8,128)(2,1)S(1)}, bf16[128,2688]{1,0:T(8,128)(2,1)S(1)}, u32[]{:S(2)}, u32[]{:S(2)}) collective-permute-start(bf16[128,2688]{1,0:T(8,128)(2,1)S(1)} %add_convert_fusion.4), channel_id=1, source_target_pairs={{0,4},{2,6},{4,8},{6,10},{8,12},{10,14},{12,0},{14,2},{1,5},{3,7},... | collective-permute-start | bytes 2064392 | tf_op jit(solution)/shard_map/ppermute | solution.py:201
  283.7 1.1 copy-start.21
  283.7 34.2 %copy-start.18 = (f32[128,2688]{1,0:T(8,128)S(1)}, f32[128,2688]{1,0:T(8,128)}, u32[]{:S(2)}) copy-start(f32[128,2688]{1,0:T(8,128)} %copy-done.17) | copy-start | bytes 4128772
  284.8 15.8 %collective-permute-start.36 = (bf16[128,2688]{1,0:T(8,128)(2,1)S(1)}, bf16[128,2688]{1,0:T(8,128)(2,1)S(1)}, u32[]{:S(2)}, u32[]{:S(2)}) collective-permute-start(bf16[128,2688]{1,0:T(8,128)(2,1)S(1)} %copy-done.21), channel_id=1, source_target_pairs={{0,2},{2,0},{4,6},{6,4},{8,10},{10,8},{12,14},{14,12},{1,3},{3,1},... | collective-permute-start | bytes 2064392 | tf_op jit(solution)/shard_map/ppermute | solution.py:193
  286.2 31.7 %collective-permute-start.34 = (bf16[128,2688]{1,0:T(8,128)(2,1)S(1)}, bf16[128,2688]{1,0:T(8,128)(2,1)S(1)}, u32[]{:S(2)}, u32[]{:S(2)}) collective-permute-start(bf16[128,2688]{1,0:T(8,128)(2,1)S(1)} %add_convert_fusion.2), channel_id=1, source_target_pairs={{0,8},{2,10},{4,12},{6,14},{8,0},{10,2},{12,4},{14,6},{1,9},{3,11}... | collective-permute-start | bytes 2064392 | tf_op jit(solution)/shard_map/ppermute | solution.py:201
  318.0 1.3 copy-start.1
  (8 other events, 7.4 us)
Sparse Core Ops, SparseCore 0:
  9.6 108.3 all-gather.3

commit v5 on v4

--- a/solution.py
+++ b/solution.py
@@ -147,17 +147,23 @@
 
 def dense_kernel(toks, count, gate_ref, *refs):
     blocks = refs[:count]
-    up_ref, down_ref = refs[count : count + 2]
+    up_hbm, down_hbm = refs[count : count + 2]
     outs = refs[count + 2 : 2 * count + 2]
-    x_ref, y_ref = refs[2 * count + 2 :]
+    x_ref, y_ref, up_ref, down_ref, sems = refs[2 * count + 2 :]
+    up_copy = pltpu.make_async_copy(up_hbm, up_ref, sems.at[0])
+    down_copy = pltpu.make_async_copy(down_hbm, down_ref, sems.at[1])
+    up_copy.start()
+    down_copy.start()
     for j in range(count):
         x_ref[j * toks : (j + 1) * toks, :] = blocks[j][...]
     size = 2 * toks
+    up_copy.wait()
 
     def part(n, carry):
         rows = pl.ds(pl.multiple_of(n * size, size), size)
         inner = dot_t(x_ref[rows, :], up_ref[0])
         inner = jnp.square(jnp.maximum(inner, 0.0)).astype(BF16)
+        pl.when(n == 0)(down_copy.wait)
         answers = jnp.dot(inner, down_ref[0], preferred_element_type=F32)
         y_ref[rows, :] = (answers.astype(BF16).astype(F32) * gate_ref[rows, :]).astype(BF16)
         return carry
@@ -175,13 +181,16 @@
     return pl.pallas_call(
         functools.partial(dense_kernel, toks, count),
         out_shape=(jax.ShapeDtypeStruct((toks, width), BF16),) * count,
-        in_specs=[whole] * (count + 3),
+        in_specs=[whole] * (count + 1) + [pl.BlockSpec(memory_space=pl.ANY)] * 2,
         out_specs=(whole,) * count,
         scratch_shapes=[
             pltpu.VMEM((count * toks, width), BF16),
             pltpu.VMEM((count * toks, width), BF16),
+            pltpu.VMEM((1, hidden, width), BF16),
+            pltpu.VMEM((1, hidden, width), BF16),
+            pltpu.SemaphoreType.DMA((2,)),
         ],
-        compiler_params=pltpu.CompilerParams(vmem_limit_bytes=28 << 20),
+        compiler_params=pltpu.CompilerParams(vmem_limit_bytes=40 << 20),
         cost_estimate=pl.CostEstimate(
             flops=4 * count * toks * width, bytes_accessed=count * toks, transcendentals=0
         ),

time: 331 us -> 329 us (level)
  local copies, waits for them, and re-layouts: 31 us -> 23.6 us
  Pallas kernels: 33.6 us -> 38.2 us
    unnamed x70 -> x64, local copies, waits for them, and re-layouts: 22.4 us -> 15 us
    pallas_call x4, Pallas kernels: 33.6 us -> 38.2 us  [dense_expert(): pl.pallas_call(functools.partial(dense_kernel, toks, count), out_shape=(j...]
  transfers between devices with their start and end apart: 38 -> 38, of which waited for: 16 -> 16; matrix products, arithmetic and copies ran while one was open for 8% -> 8% of each run, Pallas kernels for 10% -> 12%
where the time goes in v5:
time: 329 us; the launch traced here: 324 us
  waiting for transfers between devices  164 us (50%)
  starting transfers between devices  38.7 us (12%)
  Pallas kernels  38.2 us (12%)
  local copies, waits for them, and re-layouts  23.6 us (7%)
  blocking collectives  17.5 us (5%)
  matrix products  16.7 us (5%)
  between operations  14.1 us (4%)
  other arithmetic  11.1 us (3%)
    ppermute x24, waiting for transfers between devices, swap_axis(): return lax.ppermute(array, axis, [(i, i ^ 1) for i in range(count)])  57.6 us
    ppermute x6, waiting for transfers between devices, along_pairs(): return lax.ppermute(array, 'ctx', pairs)  43.9 us
    ppermute x5, waiting for transfers between devices, from_behind(): return lax.ppermute(array, axis, pairs)  43.1 us
    pallas_call x4, Pallas kernels, dense_expert(): pl.pallas_call(functools.partial(dense_kernel, toks, count), out_shape=(j...  38.2 us
    all_gather x1, blocking collectives, per_device(): tables = lax.all_gather(table, ('ctx', 'exp'), axis=0)  17.5 us
    ppermute x24, starting transfers between devices, swap_axis(): return lax.ppermute(array, axis, [(i, i ^ 1) for i in range(count)])  16.3 us
    unnamed x64, local copies, waits for them, and re-layouts  15 us
    ppermute x5, starting transfers between devices, from_behind(): return lax.ppermute(array, axis, pairs)  13.5 us
  transfers between devices with their start and end apart: 38, of which 16 were waited for; matrix products, arithmetic and copies ran while one was open for 8% of the time, Pallas kernels for 12%

profile of v5, /device:TPU:13, one launch (start us, length us, event | category | flops | bytes accessed | tf_op | source)
XLA Modules:
  0.0 324.1 jit_solution(8483301898050875598)
XLA Ops:
  6.6 0.7 all-gather.4.cloned.1.call-update
  7.3 0.7 slice.93
  8.0 3.1 collective-permute-start
  11.2 0.7 slice.102
  12.0 3.1 collective-permute-start.1
  15.2 1.2 reduce-window.6
  16.9 0.7 select_reduce_fusion
  17.7 17.5 %all-gather.1 = f32[16,17,128]{2,1,0:T(8,128)S(1)} all-gather(f32[1,17,128]{2,1,0:T(8,128)S(1)} %fusion.53), channel_id=2, replica_groups=mesh['groups'=2,'ctx'=8,'exp'=2] {'ctx','exp'}, dimensions={0}, use_global_device_ids=true | all-gather | bytes 147968 | tf_op jit(solution)/shard_map/all_gather | solution.py:293
  35.1 0.7 copy-done.22
  36.7 0.8 multiply_convert_fusion.3
  39.5 1.3 collective-permute-start.2
  40.8 1.2 copy.105
  43.1 4.2 %collective-permute-done.2 = bf16[2,8,64,128]{3,2,1,0:T(8,128)(2,1)S(1)} collective-permute-done((bf16[2,8,64,128]{3,2,1,0:T(8,128)(2,1)S(1)}, bf16[2,8,64,128]{3,2,1,0:T(8,128)(2,1)S(1)}, u32[]{:S(2)}, u32[]{:S(2)}) %collective-permute-start.2) | collective-permute-done | bytes 262176 | tf_op jit(solution)/shard_map/ppermute | solution.py:37
  47.5 0.7 collective-permute-start.3
  48.2 4.5 %collective-permute-start.4 = (bf16[2,8,64,128]{3,2,1,0:T(8,128)(2,1)S(1)}, bf16[2,8,64,128]{3,2,1,0:T(8,128)(2,1)S(1)}, u32[]{:S(2)}, u32[]{:S(2)}) collective-permute-start(bf16[2,8,64,128]{3,2,1,0:T(8,128)(2,1)S(1)} %fusion.33), channel_id=1, source_target_pairs={{0,8},{2,10},{4,12},{6,14},{1,9},{3,11},{5,13},{7,15},{16,24},{18,... | collective-permute-start | bytes 786440 | tf_op jit(solution)/shard_map/ppermute | solution.py:24
  52.7 2.1 collective-permute-start.5
  54.8 3.4 %fusion.16 = f32[256,2,8,64]{0,3,2,1:T(8,128)S(1)} fusion(bf16[256,2,8,64]{0,3,2,1:T(8,128)(2,1)S(1)} %bitcast.111, f32[256,256,2]{1,0,2:T(8,128)S(1)} %copy.103, f32[256,2,8]{0,2,1:T(8,128)S(1)} %bitcast.125, f32[256,2,8]{0,2,1:T(8,128)S(1)} %bitcast_bitcast_fusion, pred[256,256]{1,0:T(8,128)(4,1)S(1)} %iota_compare_fusion), kind=kOutput, calls=%fused_computation.29 | convolution fusion | flops 810549248 | bytes 2195456 | tf_op jit(solution)/shard_map/tsgr,sgrp->tgrp/dot_general | solution.py:332
  58.2 24.1 %collective-permute-done.4 = bf16[2,8,64,128]{3,2,1,0:T(8,128)(2,1)S(1)} collective-permute-done((bf16[2,8,64,128]{3,2,1,0:T(8,128)(2,1)S(1)}, bf16[2,8,64,128]{3,2,1,0:T(8,128)(2,1)S(1)}, u32[]{:S(2)}, u32[]{:S(2)}) %collective-permute-start.4) | collective-permute-done | bytes 262176 | tf_op jit(solution)/shard_map/ppermute | solution.py:24
  82.2 19.1 %collective-permute-done.5 = bf16[2,8,64,128]{3,2,1,0:T(8,128)(2,1)S(1)} collective-permute-done((bf16[2,8,64,128]{3,2,1,0:T(8,128)(2,1)S(1)}, bf16[2,8,64,128]{3,2,1,0:T(8,128)(2,1)S(1)}, u32[]{:S(2)}, u32[]{:S(2)}) %collective-permute-start.5) | collective-permute-done | bytes 262176 | tf_op jit(solution)/shard_map/ppermute | solution.py:24
  101.3 2.2 multiply_reduce_fusion.1
  104.2 1.6 copy.104
  106.2 11.7 %all-gather.4.cloned.1.call-done = bf16[2688,1024]{1,0:T(8,128)(2,1)} async-done(((bf16[336,1024]{1,0:T(8,128)(2,1)}), bf16[2688,1024]{1,0:T(8,128)(2,1)}) %all-gather.4.cloned.1.call-update) | async-done | bytes 5505040 | tf_op jit(solution)/shard_map/all_gather | solution.py:279
  117.9 5.5 %fusion.44 = f32[128,2688]{1,0:T(8,128)} fusion(bf16[2688,1024]{1,0:T(8,128)(2,1)} %all-gather.4.cloned.1.call-done, bf16[256,1024]{1,0:T(8,128)(2,1)S(1)} %multiply_convert_fusion.1, s32[]{:T(128)S(6)} %select_n.142), kind=kOutput, calls=%fused_computation.76 | convolution fusion | flops 704643072 | bytes 7143428 | tf_op jit(solution)/shard_map/dot_general | solution.py:348
  123.9 3.0 collective-permute-done.6
  126.9 4.6 %multiply_reduce_fusion = (f32[128]{0:T(128)S(1)}, f32[128,2688]{1,0:T(8,128)S(1)}) fusion(f32[128,2688]{1,0:T(8,128)S(1)} %collective-permute-done.6, bf16[2688,1024]{1,0:T(8,128)(2,1)} %all-gather.4.cloned.1.call-done, bf16[256,1024]{1,0:T(8,128)(2,1)S(1)} %multiply_convert_fusion.1, s32[]{:T(128)S(6)} %select_n.141, bf16[128,2688]{1,0:T(8,128)(2,1)S(1)} %copy-done.19), kind=kOutput, calls=%fused_computation.28 | convolution fusion | flops 707051392 | bytes 9208324 | tf_op jit(solution)/shard_map/dot_general | solution.py:348
  131.9 0.7 collective-permute-start.12
  132.6 15.8 %collective-permute-done.11.refs_1_ = bf16[128,2688]{1,0:T(8,128)(2,1)S(1)} collective-permute-done((bf16[128,2688]{1,0:T(8,128)(2,1)S(1)}, bf16[128,2688]{1,0:T(8,128)(2,1)S(1)}, u32[]{:S(2)}, u32[]{:S(2)}) %collective-permute-start.11) | collective-permute-done | bytes 688160 | tf_op jit(solution)/shard_map/ppermute | solution.py:202
  148.4 1.2 collective-permute-start.13
  149.7 0.8 copy-done.7
  150.7 0.8 constant_dynamic-slice_fusion
  152.5 3.5 %collective-permute-start.27 = (bf16[128,2688]{1,0:T(8,128)(2,1)S(1)}, bf16[128,2688]{1,0:T(8,128)(2,1)}, u32[]{:S(2)}, u32[]{:S(2)}) collective-permute-start(bf16[128,2688]{1,0:T(8,128)(2,1)S(1)} %multiply_convert_fusion.refs_0_), channel_id=1, source_target_pairs={{0,8},{2,10},{4,12},{6,14},{8,0},{10,2},{12,4},{14,6},{1,9},{3,11}... | collective-permute-start | bytes 2064392 | tf_op jit(solution)/shard_map/ppermute | solution.py:210
  156.1 0.9 copy-done.9
  157.1 2.4 copy-done.2
  159.5 1.1 copy-done.8
  160.6 1.1 copy-done.10
  161.7 9.8 %shard_map.163 = (bf16[128,2688]{1,0:T(8,128)(2,1)S(1)}, bf16[128,2688]{1,0:T(8,128)(2,1)S(1)}, bf16[128,2688]{1,0:T(8,128)(2,1)S(1)}, bf16[128,2688]{1,0:T(8,128)(2,1)}) custom-call(f32[512,1]{1,0:T(8,128)S(1)} %copy.107.gate_ref, bf16[128,2688]{1,0:T(8,128)(2,1)S(1)} %multiply_convert_fusion.refs_0_, bf16[128,2688]{1,0:T(8,128)(2,1)S(1)} %copy-done.8, ...), custom_call_target="tpu_custom_call" | custom-call | flops 5505024 | bytes 512 | tf_op jit(solution)/shard_map/pallas_call | solution.py:181
  171.5 0.8 copy-done.11
  173.1 1.5 collective-permute-start.20
  174.6 25.8 %collective-permute-done.27.refs_0_ = bf16[128,2688]{1,0:T(8,128)(2,1)} collective-permute-done((bf16[128,2688]{1,0:T(8,128)(2,1)S(1)}, bf16[128,2688]{1,0:T(8,128)(2,1)}, u32[]{:S(2)}, u32[]{:S(2)}) %collective-permute-start.27) | collective-permute-done | bytes 688160 | tf_op jit(solution)/shard_map/ppermute | solution.py:210
  200.5 1.1 collective-permute-start.10
  201.5 2.1 add_convert_fusion.8
  203.7 2.4 copy-done.3
  206.1 9.8 %shard_map.164 = (bf16[128,2688]{1,0:T(8,128)(2,1)S(1)}, bf16[128,2688]{1,0:T(8,128)(2,1)S(1)}, bf16[128,2688]{1,0:T(8,128)(2,1)S(1)}, bf16[128,2688]{1,0:T(8,128)(2,1)}) custom-call(f32[512,1]{1,0:T(8,128)S(1)} %copy.108.gate_ref, bf16[128,2688]{1,0:T(8,128)(2,1)S(1)} %copy-done.6, bf16[128,2688]{1,0:T(8,128)(2,1)} %collective-permute-done.8.refs_1_, ...), custom_call_target="tpu_custom_call" | custom-call | flops 5505024 | bytes 512 | tf_op jit(solution)/shard_map/pallas_call | solution.py:181
  215.9 0.8 copy-done.12
  218.6 0.7 collective-permute-done.16
  219.5 1.3 add_convert_fusion.7
  221.1 1.9 collective-permute-done.22.refs_3_
  223.1 2.4 copy-done.4
  225.5 9.3 %shard_map.165 = (bf16[128,2688]{1,0:T(8,128)(2,1)S(1)}, bf16[128,2688]{1,0:T(8,128)(2,1)S(1)}, bf16[128,2688]{1,0:T(8,128)(2,1)S(1)}, bf16[128,2688]{1,0:T(8,128)(2,1)S(1)}) custom-call(f32[512,1]{1,0:T(8,128)S(1)} %copy.109.gate_ref, bf16[128,2688]{1,0:T(8,128)(2,1)} %collective-permute-done.19.refs_0_, bf16[128,2688]{1,0:T(8,128)(2,1)} %collective-permute-done.20.refs_1_, ...), custom_call_target="tpu_custom_call" | custom-call | flops 5505024 | bytes 512 | tf_op jit(solution)/shard_map/pallas_call | solution.py:181
  235.3 1.5 collective-permute-start.17
  237.5 1.4 collective-permute-start.25
  238.8 9.3 %shard_map.166 = (bf16[128,2688]{1,0:T(8,128)(2,1)S(1)}, bf16[128,2688]{1,0:T(8,128)(2,1)S(1)}, bf16[128,2688]{1,0:T(8,128)(2,1)S(1)}, bf16[128,2688]{1,0:T(8,128)(2,1)S(1)}) custom-call(f32[512,1]{1,0:T(8,128)S(1)} %copy.110.gate_ref, bf16[128,2688]{1,0:T(8,128)(2,1)} %collective-permute-done.27.refs_0_, bf16[128,2688]{1,0:T(8,128)(2,1)} %collective-permute-done.28.refs_1_, ...), custom_call_target="tpu_custom_call" | custom-call | flops 5505024 | bytes 512 | tf_op jit(solution)/shard_map/pallas_call | solution.py:181
  248.8 3.4 %collective-permute-done.17 = bf16[128,2688]{1,0:T(8,128)(2,1)S(1)} collective-permute-done((bf16[128,2688]{1,0:T(8,128)(2,1)S(1)}, bf16[128,2688]{1,0:T(8,128)(2,1)S(1)}, u32[]{:S(2)}, u32[]{:S(2)}) %collective-permute-start.17) | collective-permute-done | bytes 688160 | tf_op jit(solution)/shard_map/ppermute | solution.py:202
  252.5 2.0 collective-permute-start.31
  254.7 1.4 collective-permute-start.33
  256.2 10.7 %collective-permute-done.25 = bf16[128,2688]{1,0:T(8,128)(2,1)S(1)} collective-permute-done((bf16[128,2688]{1,0:T(8,128)(2,1)S(1)}, bf16[128,2688]{1,0:T(8,128)(2,1)S(1)}, u32[]{:S(2)}, u32[]{:S(2)}) %collective-permute-start.25) | collective-permute-done | bytes 688160 | tf_op jit(solution)/shard_map/ppermute | solution.py:202
  267.2 14.4 %collective-permute-done.33 = bf16[128,2688]{1,0:T(8,128)(2,1)S(1)} collective-permute-done((bf16[128,2688]{1,0:T(8,128)(2,1)S(1)}, bf16[128,2688]{1,0:T(8,128)(2,1)S(1)}, u32[]{:S(2)}, u32[]{:S(2)}) %collective-permute-start.33) | collective-permute-done | bytes 688160 | tf_op jit(solution)/shard_map/ppermute | solution.py:202
  281.9 0.8 copy-done.18
  282.7 1.4 collective-permute-start.36
  284.1 3.2 collective-permute-start.34
  287.3 0.8 collective-permute-done.26
  288.1 10.5 %collective-permute-done.36 = bf16[128,2688]{1,0:T(8,128)(2,1)S(1)} collective-permute-done((bf16[128,2688]{1,0:T(8,128)(2,1)S(1)}, bf16[128,2688]{1,0:T(8,128)(2,1)S(1)}, u32[]{:S(2)}, u32[]{:S(2)}) %collective-permute-start.36) | collective-permute-done | bytes 688160 | tf_op jit(solution)/shard_map/ppermute | solution.py:202
  298.5 17.3 %collective-permute-done.34 = bf16[128,2688]{1,0:T(8,128)(2,1)S(1)} collective-permute-done((bf16[128,2688]{1,0:T(8,128)(2,1)S(1)}, bf16[128,2688]{1,0:T(8,128)(2,1)S(1)}, u32[]{:S(2)}, u32[]{:S(2)}) %collective-permute-start.34) | collective-permute-done | bytes 688160 | tf_op jit(solution)/shard_map/ppermute | solution.py:210
  315.9 1.4 add_convert_fusion
  (159 shorter events, 14.2 us)
Async XLA Ops:
  6.5 8.7 %copy-start = (f32[256,16]{0,1:T(8,128)S(1)}, f32[256,16]{0,1:T(8,128)}, u32[]{:S(2)}) copy-start(f32[256,16]{0,1:T(8,128)} %param.21) | copy-start | bytes 49156
  6.5 29.7 %copy-start.21 = (bf16[256,2,256]{2,1,0:T(2,128)(2,1)S(1)}, bf16[256,2,256]{2,1,0:T(2,128)(2,1)}, u32[]{:S(2)}) copy-start(bf16[256,2,256]{2,1,0:T(2,128)(2,1)} %param.18) | copy-start | bytes 786436
  6.5 29.4 %copy-start.26 = (bf16[4,2,256]{2,1,0:T(2,128)(2,1)S(1)}, bf16[4,2,256]{2,1,0:T(2,128)(2,1)}, u32[]{:S(2)}) copy-start(bf16[4,2,256]{2,1,0:T(2,128)(2,1)} %param.23) | copy-start | bytes 12292
  6.5 29.5 %copy-start.23 = (bf16[4,1024]{1,0:T(4,128)(2,1)S(1)}, bf16[4,1024]{1,0:T(4,128)(2,1)}, u32[]{:S(2)}) copy-start(bf16[4,1024]{1,0:T(4,128)(2,1)} %param.22) | copy-start | bytes 24580
  6.5 29.6 %copy-start.24 = (f32[256,16]{0,1:T(8,128)S(1)}, f32[256,16]{0,1:T(8,128)}, u32[]{:S(2)}) copy-start(f32[256,16]{0,1:T(8,128)} %param.20) | copy-start | bytes 49156
  6.5 111.4 %all-gather.4.cloned.1.call-start = ((), (), s32[]{:S(2)}) async-start(), calls=%async_computation | async-start | bytes 6193152 | tf_op jit(solution)/shard_map/all_gather | solution.py:279
  8.0 29.5 %collective-permute-start = (bf16[3,1024]{1,0:T(4,128)(2,1)S(1)}, bf16[3,1024]{1,0:T(4,128)(2,1)S(1)}, u32[]{:S(2)}, u32[]{:S(2)}) collective-permute-start(bf16[3,1024]{1,0:T(4,128)(2,1)S(1)} %slice.93), channel_id=1, source_target_pairs={{0,2},{2,4},{4,6},{6,8},{8,10},{10,12},{12,14},{1,3},{3,5},{5,7},{... | collective-permute-start | bytes 18440 | tf_op jit(solution)/shard_map/ppermute | solution.py:24
  12.0 24.5 %collective-permute-start.1 = (bf16[3,2,256]{0,2,1:T(8,128)(2,1)S(1)}, bf16[3,2,256]{0,2,1:T(8,128)(2,1)S(1)}, u32[]{:S(2)}, u32[]{:S(2)}) collective-permute-start(bf16[3,2,256]{0,2,1:T(8,128)(2,1)S(1)} %copy.97), channel_id=1, source_target_pairs={{0,2},{2,4},{4,6},{6,8},{8,10},{10,12},{12,14},{1,3},{3,5},{5,7},{... | collective-permute-start | bytes 9224 | tf_op jit(solution)/shard_map/ppermute | solution.py:24
  36.7 1.0 copy-start.20
  38.6 2.2 copy-start.16
  38.8 3.2 copy-start.29
  38.8 3.9 %copy-start.27 = (bf16[1024]{0:T(1024)(128)(2,1)S(1)}, bf16[1024]{0:T(1024)(128)(2,1)}, u32[]{:S(2)}) copy-start(bf16[1024]{0:T(1024)(128)(2,1)} %param.26) | copy-start | bytes 6148
  39.5 7.8 %collective-permute-start.2 = (bf16[2,8,64,128]{3,2,1,0:T(8,128)(2,1)S(1)}, bf16[2,8,64,128]{3,2,1,0:T(8,128)(2,1)S(1)}, u32[]{:S(2)}, u32[]{:S(2)}) collective-permute-start(bf16[2,8,64,128]{3,2,1,0:T(8,128)(2,1)S(1)} %get-tuple-element.86), channel_id=1, source_target_pairs={{0,2},{2,0},{4,6},{6,4},{8,10},{10,8},{12,14},{14,12},{1,3},{3,1},... | collective-permute-start | bytes 786440 | tf_op jit(solution)/shard_map/ppermute | solution.py:37
  47.5 10.7 %collective-permute-start.3 = (bf16[2,8,64,128]{3,2,1,0:T(8,128)(2,1)S(1)}, bf16[2,8,64,128]{3,2,1,0:T(8,128)(2,1)S(1)}, u32[]{:S(2)}, u32[]{:S(2)}) collective-permute-start(bf16[2,8,64,128]{3,2,1,0:T(8,128)(2,1)S(1)} %fusion.33), channel_id=1, source_target_pairs={{0,12},{2,14},{1,13},{3,15},{16,28},{18,30},{17,29},{19,31}} | collective-permute-start | bytes 786440 | tf_op jit(solution)/shard_map/ppermute | solution.py:24
  48.2 34.0 %collective-permute-start.4 = (bf16[2,8,64,128]{3,2,1,0:T(8,128)(2,1)S(1)}, bf16[2,8,64,128]{3,2,1,0:T(8,128)(2,1)S(1)}, u32[]{:S(2)}, u32[]{:S(2)}) collective-permute-start(bf16[2,8,64,128]{3,2,1,0:T(8,128)(2,1)S(1)} %fusion.33), channel_id=1, source_target_pairs={{0,8},{2,10},{4,12},{6,14},{1,9},{3,11},{5,13},{7,15},{16,24},{18,... | collective-permute-start | bytes 786440 | tf_op jit(solution)/shard_map/ppermute | solution.py:24
  52.7 48.7 %collective-permute-start.5 = (bf16[2,8,64,128]{3,2,1,0:T(8,128)(2,1)S(1)}, bf16[2,8,64,128]{3,2,1,0:T(8,128)(2,1)S(1)}, u32[]{:S(2)}, u32[]{:S(2)}) collective-permute-start(bf16[2,8,64,128]{3,2,1,0:T(8,128)(2,1)S(1)} %fusion.33), channel_id=1, source_target_pairs={{0,4},{2,6},{4,8},{6,10},{8,12},{10,14},{1,5},{3,7},{5,9},{7,11},{... | collective-permute-start | bytes 786440 | tf_op jit(solution)/shard_map/ppermute | solution.py:24
  54.8 46.5 %copy-start.17 = (f32[256,1024]{0,1:T(8,128)S(1)}, f32[256,1024]{0,1:T(8,128)}, u32[]{:S(2)}) copy-start(f32[256,1024]{0,1:T(8,128)} %copy.105) | copy-start | bytes 3145732
  54.8 46.5 %copy-start.28 = (bf16[16,64,128]{2,1,0:T(8,128)(2,1)S(1)}, bf16[16,64,128]{2,1,0:T(8,128)(2,1)}, u32[]{:S(2)}) copy-start(bf16[16,64,128]{2,1,0:T(8,128)(2,1)} %param.25) | copy-start | bytes 786436
  54.8 46.5 %copy-start.30 = (f32[2,8]{1,0:T(2,128)S(1)}, f32[2,8]{1,0:T(2,128)}, u32[]{:S(2)}) copy-start(f32[2,8]{1,0:T(2,128)} %mul.362) | copy-start | bytes 196
  106.2 17.7 %copy-start.25 = (bf16[2688]{0:T(1024)(128)(2,1)S(1)}, bf16[2688]{0:T(1024)(128)(2,1)}, u32[]{:S(2)}) copy-start(bf16[2688]{0:T(1024)(128)(2,1)} %param.29) | copy-start | bytes 16132
  106.2 20.7 %copy-start.19 = (bf16[128,2688]{1,0:T(8,128)(2,1)S(1)}, bf16[128,2688]{1,0:T(8,128)(2,1)}, u32[]{:S(2)}) copy-start(bf16[128,2688]{1,0:T(8,128)(2,1)} %param.28) | copy-start | bytes 2064388
  123.5 3.4 %collective-permute-start.6 = (f32[128,2688]{1,0:T(8,128)}, f32[128,2688]{1,0:T(8,128)S(1)}, u32[]{:S(2)}, u32[]{:S(2)}) collective-permute-start(f32[128,2688]{1,0:T(8,128)} %fusion.44), channel_id=1, source_target_pairs={{0,1},{1,0},{2,3},{3,2},{4,5},{5,4},{6,7},{7,6},{8,9},{9,8},{10,11... | collective-permute-start | bytes 4128776 | tf_op jit(solution)/shard_map/ppermute | solution.py:350
  131.5 18.1 %copy-start.14 = (f32[128,2688]{1,0:T(8,128)}, f32[128,2688]{1,0:T(8,128)S(1)}, u32[]{:S(2)}) copy-start(f32[128,2688]{1,0:T(8,128)S(1)} %get-tuple-element.91) | copy-start | bytes 4128772
  131.7 16.7 %collective-permute-start.11 = (bf16[128,2688]{1,0:T(8,128)(2,1)S(1)}, bf16[128,2688]{1,0:T(8,128)(2,1)S(1)}, u32[]{:S(2)}, u32[]{:S(2)}) collective-permute-start(bf16[128,2688]{1,0:T(8,128)(2,1)S(1)} %multiply_convert_fusion.refs_0_), channel_id=1, source_target_pairs={{0,2},{2,0},{4,6},{6,4},{8,10},{10,8},{12,14},{14,12},{1,3},{3,1},... | collective-permute-start | bytes 2064392 | tf_op jit(solution)/shard_map/ppermute | solution.py:202
  131.9 24.2 %collective-permute-start.12 = (bf16[128,2688]{1,0:T(8,128)(2,1)S(1)}, bf16[128,2688]{1,0:T(8,128)(2,1)S(1)}, u32[]{:S(2)}, u32[]{:S(2)}) collective-permute-start(bf16[128,2688]{1,0:T(8,128)(2,1)S(1)} %multiply_convert_fusion.refs_0_), channel_id=1, source_target_pairs={{0,1},{1,0},{2,3},{3,2},{4,5},{5,4},{6,7},{7,6},{8,9},{9,8},{10,11... | collective-permute-start | bytes 2064392 | tf_op jit(solution)/shard_map/ppermute | solution.py:202
  132.6 23.4 %collective-permute-start.7 = (bf16[128,2688]{1,0:T(8,128)(2,1)S(1)}, bf16[128,2688]{1,0:T(8,128)(2,1)S(1)}, u32[]{:S(2)}, u32[]{:S(2)}) collective-permute-start(bf16[128,2688]{1,0:T(8,128)(2,1)S(1)} %multiply_convert_fusion.refs_0_), channel_id=1, source_target_pairs={{0,4},{2,6},{4,8},{6,10},{8,12},{10,14},{12,0},{14,2},{1,5},{3,7},... | collective-permute-start | bytes 2064392 | tf_op jit(solution)/shard_map/ppermute | solution.py:210
  148.4 8.6 %collective-permute-start.13 = (bf16[128,2688]{1,0:T(8,128)(2,1)S(1)}, bf16[128,2688]{1,0:T(8,128)(2,1)}, u32[]{:S(2)}, u32[]{:S(2)}) collective-permute-start(bf16[128,2688]{1,0:T(8,128)(2,1)S(1)} %collective-permute-done.11.refs_1_), channel_id=1, source_target_pairs={{0,1},{1,0},{2,3},{3,2},{4,5},{5,4},{6,7},{7,6},{8,9},{9,8},{10,11... | collective-permute-start | bytes 2064392 | tf_op jit(solution)/shard_map/ppermute | solution.py:202
  152.3 20.8 %collective-permute-start.19 = (bf16[128,2688]{1,0:T(8,128)(2,1)S(1)}, bf16[128,2688]{1,0:T(8,128)(2,1)}, u32[]{:S(2)}, u32[]{:S(2)}) collective-permute-start(bf16[128,2688]{1,0:T(8,128)(2,1)S(1)} %multiply_convert_fusion.refs_0_), channel_id=1, source_target_pairs={{0,12},{2,14},{4,0},{6,2},{8,4},{10,6},{12,8},{14,10},{1,13},{3,15... | collective-permute-start | bytes 2064392 | tf_op jit(solution)/shard_map/ppermute | solution.py:210
  152.5 47.9 %collective-permute-start.27 = (bf16[128,2688]{1,0:T(8,128)(2,1)S(1)}, bf16[128,2688]{1,0:T(8,128)(2,1)}, u32[]{:S(2)}, u32[]{:S(2)}) collective-permute-start(bf16[128,2688]{1,0:T(8,128)(2,1)S(1)} %multiply_convert_fusion.refs_0_), channel_id=1, source_target_pairs={{0,8},{2,10},{4,12},{6,14},{8,0},{10,2},{12,4},{14,6},{1,9},{3,11}... | collective-permute-start | bytes 2064392 | tf_op jit(solution)/shard_map/ppermute | solution.py:210
  156.0 16.9 %copy-start.5 = (bf16[128,2688]{1,0:T(8,128)(2,1)}, bf16[128,2688]{1,0:T(8,128)(2,1)S(1)}, u32[]{:S(2)}) copy-start(bf16[128,2688]{1,0:T(8,128)(2,1)S(1)} %collective-permute-done.7.refs_0_) | copy-start | bytes 2064388
  156.0 44.4 %collective-permute-start.8 = (bf16[128,2688]{1,0:T(8,128)(2,1)S(1)}, bf16[128,2688]{1,0:T(8,128)(2,1)}, u32[]{:S(2)}, u32[]{:S(2)}) collective-permute-start(bf16[128,2688]{1,0:T(8,128)(2,1)S(1)} %collective-permute-done.7.refs_0_), channel_id=1, source_target_pairs={{0,2},{2,0},{4,6},{6,4},{8,10},{10,8},{12,14},{14,12},{1,3},{3,1},... | collective-permute-start | bytes 2064392 | tf_op jit(solution)/shard_map/ppermute | solution.py:202
  157.1 2.4 copy-start.2
  159.5 1.1 copy-start.8
  160.6 1.1 copy-start.10
  172.3 29.2 %collective-permute-start.14 = (bf16[128,2688]{1,0:T(8,128)(2,1)}, bf16[128,2688]{1,0:T(8,128)(2,1)}, u32[]{:S(2)}, u32[]{:S(2)}) collective-permute-start(bf16[128,2688]{1,0:T(8,128)(2,1)} %get-tuple-element.36), channel_id=1, source_target_pairs={{0,1},{1,0},{2,3},{3,2},{4,5},{5,4},{6,7},{7,6},{8,9},{9,8},{10,11... | collective-permute-start | bytes 2064392 | tf_op jit(solution)/shard_map/ppermute | solution.py:202
  173.0 30.7 %collective-permute-start.9 = (bf16[128,2688]{1,0:T(8,128)(2,1)S(1)}, bf16[128,2688]{1,0:T(8,128)(2,1)S(1)}, u32[]{:S(2)}, u32[]{:S(2)}) collective-permute-start(bf16[128,2688]{1,0:T(8,128)(2,1)S(1)} %collective-permute-done.7.refs_0_), channel_id=1, source_target_pairs={{0,1},{1,0},{2,3},{3,2},{4,5},{5,4},{6,7},{7,6},{8,9},{9,8},{10,11... | collective-permute-start | bytes 2064392 | tf_op jit(solution)/shard_map/ppermute | solution.py:202
  173.1 30.6 %copy-start.6 = (bf16[128,2688]{1,0:T(8,128)(2,1)S(1)}, bf16[128,2688]{1,0:T(8,128)(2,1)}, u32[]{:S(2)}) copy-start(bf16[128,2688]{1,0:T(8,128)(2,1)} %copy-done.5) | copy-start | bytes 2064388
  173.1 44.8 %collective-permute-start.20 = (bf16[128,2688]{1,0:T(8,128)(2,1)}, bf16[128,2688]{1,0:T(8,128)(2,1)}, u32[]{:S(2)}, u32[]{:S(2)}) collective-permute-start(bf16[128,2688]{1,0:T(8,128)(2,1)} %collective-permute-done.19.refs_0_), channel_id=1, source_target_pairs={{0,2},{2,0},{4,6},{6,4},{8,10},{10,8},{12,14},{14,12},{1,3},{3,1},... | collective-permute-start | bytes 2064392 | tf_op jit(solution)/shard_map/ppermute | solution.py:202
  200.4 17.8 %collective-permute-start.28 = (bf16[128,2688]{1,0:T(8,128)(2,1)}, bf16[128,2688]{1,0:T(8,128)(2,1)}, u32[]{:S(2)}, u32[]{:S(2)}) collective-permute-start(bf16[128,2688]{1,0:T(8,128)(2,1)} %collective-permute-done.27.refs_0_), channel_id=1, source_target_pairs={{0,2},{2,0},{4,6},{6,4},{8,10},{10,8},{12,14},{14,12},{1,3},{3,1},... | collective-permute-start | bytes 2064392 | tf_op jit(solution)/shard_map/ppermute | solution.py:202
  200.5 3.2 collective-permute-start.10
  203.7 2.4 copy-start.3
  216.8 4.0 %copy-start.13 = (bf16[128,2688]{1,0:T(8,128)(2,1)S(1)}, bf16[128,2688]{1,0:T(8,128)(2,1)}, u32[]{:S(2)}) copy-start(bf16[128,2688]{1,0:T(8,128)(2,1)} %copy-done.12) | copy-start | bytes 2064388
  216.8 2.5 collective-permute-start.16
  217.3 3.4 %collective-permute-start.21 = (bf16[128,2688]{1,0:T(8,128)(2,1)}, bf16[128,2688]{1,0:T(8,128)(2,1)S(1)}, u32[]{:S(2)}, u32[]{:S(2)}) collective-permute-start(bf16[128,2688]{1,0:T(8,128)(2,1)} %collective-permute-done.19.refs_0_), channel_id=1, source_target_pairs={{0,1},{1,0},{2,3},{3,2},{4,5},{5,4},{6,7},{7,6},{8,9},{9,8},{10,11... | collective-permute-start | bytes 2064392 | tf_op jit(solution)/shard_map/ppermute | solution.py:202
  217.7 19.8 %collective-permute-start.29 = (bf16[128,2688]{1,0:T(8,128)(2,1)}, bf16[128,2688]{1,0:T(8,128)(2,1)S(1)}, u32[]{:S(2)}, u32[]{:S(2)}) collective-permute-start(bf16[128,2688]{1,0:T(8,128)(2,1)} %collective-permute-done.27.refs_0_), channel_id=1, source_target_pairs={{0,1},{1,0},{2,3},{3,2},{4,5},{5,4},{6,7},{7,6},{8,9},{9,8},{10,11... | collective-permute-start | bytes 2064392 | tf_op jit(solution)/shard_map/ppermute | solution.py:202
  217.9 17.2 %collective-permute-start.35 = (bf16[128,2688]{1,0:T(8,128)(2,1)}, bf16[128,2688]{1,0:T(8,128)(2,1)S(1)}, u32[]{:S(2)}, u32[]{:S(2)}) collective-permute-start(bf16[128,2688]{1,0:T(8,128)(2,1)} %copy-done.11), channel_id=1, source_target_pairs={{0,1},{1,0},{2,3},{3,2},{4,5},{5,4},{6,7},{7,6},{8,9},{9,8},{10,11... | collective-permute-start | bytes 2064392 | tf_op jit(solution)/shard_map/ppermute | solution.py:202
  218.2 4.9 %collective-permute-start.22 = (bf16[128,2688]{1,0:T(8,128)(2,1)}, bf16[128,2688]{1,0:T(8,128)(2,1)S(1)}, u32[]{:S(2)}, u32[]{:S(2)}) collective-permute-start(bf16[128,2688]{1,0:T(8,128)(2,1)} %collective-permute-done.20.refs_1_), channel_id=1, source_target_pairs={{0,1},{1,0},{2,3},{3,2},{4,5},{5,4},{6,7},{7,6},{8,9},{9,8},{10,11... | collective-permute-start | bytes 2064392 | tf_op jit(solution)/shard_map/ppermute | solution.py:202
  219.3 19.6 %collective-permute-start.30 = (bf16[128,2688]{1,0:T(8,128)(2,1)}, bf16[128,2688]{1,0:T(8,128)(2,1)S(1)}, u32[]{:S(2)}, u32[]{:S(2)}) collective-permute-start(bf16[128,2688]{1,0:T(8,128)(2,1)} %collective-permute-done.28.refs_1_), channel_id=1, source_target_pairs={{0,1},{1,0},{2,3},{3,2},{4,5},{5,4},{6,7},{7,6},{8,9},{9,8},{10,11... | collective-permute-start | bytes 2064392 | tf_op jit(solution)/shard_map/ppermute | solution.py:202
  220.8 28.0 %collective-permute-start.15 = (bf16[128,2688]{1,0:T(8,128)(2,1)S(1)}, bf16[128,2688]{1,0:T(8,128)(2,1)S(1)}, u32[]{:S(2)}, u32[]{:S(2)}) collective-permute-start(bf16[128,2688]{1,0:T(8,128)(2,1)S(1)} %copy-done.13), channel_id=1, source_target_pairs={{0,1},{1,0},{2,3},{3,2},{4,5},{5,4},{6,7},{7,6},{8,9},{9,8},{10,11... | collective-permute-start | bytes 2064392 | tf_op jit(solution)/shard_map/ppermute | solution.py:202
  223.1 2.4 copy-start.4
  234.8 2.2 collective-permute-start.24
  235.3 16.8 %collective-permute-start.17 = (bf16[128,2688]{1,0:T(8,128)(2,1)S(1)}, bf16[128,2688]{1,0:T(8,128)(2,1)S(1)}, u32[]{:S(2)}, u32[]{:S(2)}) collective-permute-start(bf16[128,2688]{1,0:T(8,128)(2,1)S(1)} %add_convert_fusion.7), channel_id=1, source_target_pairs={{0,2},{2,0},{4,6},{6,4},{8,10},{10,8},{12,14},{14,12},{1,3},{3,1},... | collective-permute-start | bytes 2064392 | tf_op jit(solution)/shard_map/ppermute | solution.py:202
  237.0 19.2 %collective-permute-start.23 = (bf16[128,2688]{1,0:T(8,128)(2,1)S(1)}, bf16[128,2688]{1,0:T(8,128)(2,1)S(1)}, u32[]{:S(2)}, u32[]{:S(2)}) collective-permute-start(bf16[128,2688]{1,0:T(8,128)(2,1)S(1)} %get-tuple-element.50), channel_id=1, source_target_pairs={{0,1},{1,0},{2,3},{3,2},{4,5},{5,4},{6,7},{7,6},{8,9},{9,8},{10,11... | collective-permute-start | bytes 2064392 | tf_op jit(solution)/shard_map/ppermute | solution.py:202
  237.5 29.4 %collective-permute-start.25 = (bf16[128,2688]{1,0:T(8,128)(2,1)S(1)}, bf16[128,2688]{1,0:T(8,128)(2,1)S(1)}, u32[]{:S(2)}, u32[]{:S(2)}) collective-permute-start(bf16[128,2688]{1,0:T(8,128)(2,1)S(1)} %add_convert_fusion.5), channel_id=1, source_target_pairs={{0,2},{2,0},{4,6},{6,4},{8,10},{10,8},{12,14},{14,12},{1,3},{3,1},... | collective-permute-start | bytes 2064392 | tf_op jit(solution)/shard_map/ppermute | solution.py:202
  248.1 6.4 %collective-permute-start.32 = (bf16[128,2688]{1,0:T(8,128)(2,1)S(1)}, bf16[128,2688]{1,0:T(8,128)(2,1)S(1)}, u32[]{:S(2)}, u32[]{:S(2)}) collective-permute-start(bf16[128,2688]{1,0:T(8,128)(2,1)S(1)} %get-tuple-element.60), channel_id=1, source_target_pairs={{0,1},{1,0},{2,3},{3,2},{4,5},{5,4},{6,7},{7,6},{8,9},{9,8},{10,11... | collective-permute-start | bytes 2064392 | tf_op jit(solution)/shard_map/ppermute | solution.py:202
  252.4 34.9 %collective-permute-start.18 = (bf16[128,2688]{1,0:T(8,128)(2,1)S(1)}, bf16[128,2688]{1,0:T(8,128)(2,1)S(1)}, u32[]{:S(2)}, u32[]{:S(2)}) collective-permute-start(bf16[128,2688]{1,0:T(8,128)(2,1)S(1)} %add_convert_fusion.6), channel_id=1, source_target_pairs={{0,12},{2,14},{4,0},{6,2},{8,4},{10,6},{12,8},{14,10},{1,13},{3,15... | collective-permute-start | bytes 2064392 | tf_op jit(solution)/shard_map/ppermute | solution.py:210
  252.5 14.7 %collective-permute-start.31 = (bf16[128,2688]{1,0:T(8,128)(2,1)S(1)}, bf16[128,2688]{1,0:T(8,128)(2,1)S(1)}, u32[]{:S(2)}, u32[]{:S(2)}) collective-permute-start(bf16[128,2688]{1,0:T(8,128)(2,1)S(1)} %get-tuple-element.58), channel_id=1, source_target_pairs={{0,1},{1,0},{2,3},{3,2},{4,5},{5,4},{6,7},{7,6},{8,9},{9,8},{10,11... | collective-permute-start | bytes 2064392 | tf_op jit(solution)/shard_map/ppermute | solution.py:202
  254.7 26.9 %collective-permute-start.33 = (bf16[128,2688]{1,0:T(8,128)(2,1)S(1)}, bf16[128,2688]{1,0:T(8,128)(2,1)S(1)}, u32[]{:S(2)}, u32[]{:S(2)}) collective-permute-start(bf16[128,2688]{1,0:T(8,128)(2,1)S(1)} %add_convert_fusion.3), channel_id=1, source_target_pairs={{0,2},{2,0},{4,6},{6,4},{8,10},{10,8},{12,14},{14,12},{1,3},{3,1},... | collective-permute-start | bytes 2064392 | tf_op jit(solution)/shard_map/ppermute | solution.py:202
  267.2 20.9 %collective-permute-start.26 = (bf16[128,2688]{1,0:T(8,128)(2,1)S(1)}, bf16[128,2688]{1,0:T(8,128)(2,1)S(1)}, u32[]{:S(2)}, u32[]{:S(2)}) collective-permute-start(bf16[128,2688]{1,0:T(8,128)(2,1)S(1)} %add_convert_fusion.4), channel_id=1, source_target_pairs={{0,4},{2,6},{4,8},{6,10},{8,12},{10,14},{12,0},{14,2},{1,5},{3,7},... | collective-permute-start | bytes 2064392 | tf_op jit(solution)/shard_map/ppermute | solution.py:210
  281.6 1.1 copy-start.18
  281.6 34.3 %copy-start.15 = (f32[128,2688]{1,0:T(8,128)S(1)}, f32[128,2688]{1,0:T(8,128)}, u32[]{:S(2)}) copy-start(f32[128,2688]{1,0:T(8,128)} %copy-done.14) | copy-start | bytes 4128772
  282.7 15.8 %collective-permute-start.36 = (bf16[128,2688]{1,0:T(8,128)(2,1)S(1)}, bf16[128,2688]{1,0:T(8,128)(2,1)S(1)}, u32[]{:S(2)}, u32[]{:S(2)}) collective-permute-start(bf16[128,2688]{1,0:T(8,128)(2,1)S(1)} %copy-done.18), channel_id=1, source_target_pairs={{0,2},{2,0},{4,6},{6,4},{8,10},{10,8},{12,14},{14,12},{1,3},{3,1},... | collective-permute-start | bytes 2064392 | tf_op jit(solution)/shard_map/ppermute | solution.py:202
  284.1 31.8 %collective-permute-start.34 = (bf16[128,2688]{1,0:T(8,128)(2,1)S(1)}, bf16[128,2688]{1,0:T(8,128)(2,1)S(1)}, u32[]{:S(2)}, u32[]{:S(2)}) collective-permute-start(bf16[128,2688]{1,0:T(8,128)(2,1)S(1)} %add_convert_fusion.2), channel_id=1, source_target_pairs={{0,8},{2,10},{4,12},{6,14},{8,0},{10,2},{12,4},{14,6},{1,9},{3,11}... | collective-permute-start | bytes 2064392 | tf_op jit(solution)/shard_map/ppermute | solution.py:210
  315.9 1.4 copy-start.1
  (5 other events, 4.1 us)
Sparse Core Ops, SparseCore 0:
  9.6 108.3 all-gather.3

commit v6 on v5

--- a/solution.py
+++ b/solution.py
@@ -192,7 +192,9 @@
         ],
         compiler_params=pltpu.CompilerParams(vmem_limit_bytes=40 << 20),
         cost_estimate=pl.CostEstimate(
-            flops=4 * count * toks * width, bytes_accessed=count * toks, transcendentals=0
+            flops=4 * count * toks * width * hidden,
+            bytes_accessed=4 * width * (count * toks + hidden),
+            transcendentals=0,
         ),
     )(gates, *blocks, up_t, down)
 

time: 329 us -> 329 us (level)
    unnamed x64 -> x60, local copies, waits for them, and re-layouts: 15 us -> 15 us
  transfers between devices with their start and end apart: 38 -> 38, of which waited for: 16 -> 17; matrix products, arithmetic and copies ran while one was open for 8% -> 8% of each run, Pallas kernels for 12% -> 12%
where the time goes in v6:
time: 329 us; the launch traced here: 324 us
  waiting for transfers between devices  165 us (50%)
  starting transfers between devices  38.2 us (12%)
  Pallas kernels  38.2 us (12%)
  local copies, waits for them, and re-layouts  23.6 us (7%)
  blocking collectives  17.5 us (5%)
  matrix products  16.7 us (5%)
  between operations  14.1 us (4%)
  other arithmetic  11.1 us (3%)
    ppermute x24, waiting for transfers between devices, swap_axis(): return lax.ppermute(array, axis, [(i, i ^ 1) for i in range(count)])  58.3 us
    ppermute x6, waiting for transfers between devices, along_pairs(): return lax.ppermute(array, 'ctx', pairs)  43.9 us
    ppermute x5, waiting for transfers between devices, from_behind(): return lax.ppermute(array, axis, pairs)  43.1 us
    pallas_call x4, Pallas kernels, dense_expert(): pl.pallas_call(functools.partial(dense_kernel, toks, count), out_shape=(j...  38.2 us
    all_gather x1, blocking collectives, per_device(): tables = lax.all_gather(table, ('ctx', 'exp'), axis=0)  17.5 us
    ppermute x24, starting transfers between devices, swap_axis(): return lax.ppermute(array, axis, [(i, i ^ 1) for i in range(count)])  15.9 us
    unnamed x60, local copies, waits for them, and re-layouts  15 us
    ppermute x5, starting transfers between devices, from_behind(): return lax.ppermute(array, axis, pairs)  13.5 us
  transfers between devices with their start and end apart: 38, of which 17 were waited for; matrix products, arithmetic and copies ran while one was open for 8% of the time, Pallas kernels for 12%

profile of v6, /device:TPU:13, one launch (start us, length us, event | category | flops | bytes accessed | tf_op | source)
XLA Modules:
  0.0 324.3 jit_solution(5077705429867805931)
XLA Ops:
  6.6 0.7 all-gather.4.cloned.1.call-update
  7.3 0.7 slice.93
  8.0 3.1 collective-permute-start
  11.2 0.7 slice.102
  12.0 3.1 collective-permute-start.1
  15.2 1.2 reduce-window.6
  16.9 0.7 select_reduce_fusion
  17.7 17.5 %all-gather.1 = f32[16,17,128]{2,1,0:T(8,128)S(1)} all-gather(f32[1,17,128]{2,1,0:T(8,128)S(1)} %fusion.53), channel_id=2, replica_groups=mesh['groups'=2,'ctx'=8,'exp'=2] {'ctx','exp'}, dimensions={0}, use_global_device_ids=true | all-gather | bytes 147968 | tf_op jit(solution)/shard_map/all_gather | solution.py:295
  35.1 0.7 copy-done.20
  36.7 0.8 multiply_convert_fusion.3
  39.5 1.3 collective-permute-start.2
  40.8 1.2 copy.105
  43.1 4.2 %collective-permute-done.2 = bf16[2,8,64,128]{3,2,1,0:T(8,128)(2,1)S(1)} collective-permute-done((bf16[2,8,64,128]{3,2,1,0:T(8,128)(2,1)S(1)}, bf16[2,8,64,128]{3,2,1,0:T(8,128)(2,1)S(1)}, u32[]{:S(2)}, u32[]{:S(2)}) %collective-permute-start.2) | collective-permute-done | bytes 262176 | tf_op jit(solution)/shard_map/ppermute | solution.py:37
  47.5 0.7 collective-permute-start.3
  48.2 4.4 %collective-permute-start.4 = (bf16[2,8,64,128]{3,2,1,0:T(8,128)(2,1)S(1)}, bf16[2,8,64,128]{3,2,1,0:T(8,128)(2,1)S(1)}, u32[]{:S(2)}, u32[]{:S(2)}) collective-permute-start(bf16[2,8,64,128]{3,2,1,0:T(8,128)(2,1)S(1)} %fusion.33), channel_id=1, source_target_pairs={{0,8},{2,10},{4,12},{6,14},{1,9},{3,11},{5,13},{7,15},{16,24},{18,... | collective-permute-start | bytes 786440 | tf_op jit(solution)/shard_map/ppermute | solution.py:24
  52.6 2.1 collective-permute-start.5
  54.8 3.4 %fusion.16 = f32[256,2,8,64]{0,3,2,1:T(8,128)S(1)} fusion(bf16[256,2,8,64]{0,3,2,1:T(8,128)(2,1)S(1)} %bitcast.111, f32[256,256,2]{1,0,2:T(8,128)S(1)} %copy.103, f32[256,2,8]{0,2,1:T(8,128)S(1)} %bitcast.125, f32[256,2,8]{0,2,1:T(8,128)S(1)} %bitcast_bitcast_fusion, pred[256,256]{1,0:T(8,128)(4,1)S(1)} %iota_compare_fusion), kind=kOutput, calls=%fused_computation.29 | convolution fusion | flops 810549248 | bytes 2195456 | tf_op jit(solution)/shard_map/tsgr,sgrp->tgrp/dot_general | solution.py:334
  58.2 24.1 %collective-permute-done.4 = bf16[2,8,64,128]{3,2,1,0:T(8,128)(2,1)S(1)} collective-permute-done((bf16[2,8,64,128]{3,2,1,0:T(8,128)(2,1)S(1)}, bf16[2,8,64,128]{3,2,1,0:T(8,128)(2,1)S(1)}, u32[]{:S(2)}, u32[]{:S(2)}) %collective-permute-start.4) | collective-permute-done | bytes 262176 | tf_op jit(solution)/shard_map/ppermute | solution.py:24
  82.2 19.0 %collective-permute-done.5 = bf16[2,8,64,128]{3,2,1,0:T(8,128)(2,1)S(1)} collective-permute-done((bf16[2,8,64,128]{3,2,1,0:T(8,128)(2,1)S(1)}, bf16[2,8,64,128]{3,2,1,0:T(8,128)(2,1)S(1)}, u32[]{:S(2)}, u32[]{:S(2)}) %collective-permute-start.5) | collective-permute-done | bytes 262176 | tf_op jit(solution)/shard_map/ppermute | solution.py:24
  101.3 2.2 multiply_reduce_fusion.1
  104.2 1.6 copy.104
  106.2 11.8 %all-gather.4.cloned.1.call-done = bf16[2688,1024]{1,0:T(8,128)(2,1)} async-done(((bf16[336,1024]{1,0:T(8,128)(2,1)}), bf16[2688,1024]{1,0:T(8,128)(2,1)}) %all-gather.4.cloned.1.call-update) | async-done | bytes 5505040 | tf_op jit(solution)/shard_map/all_gather | solution.py:281
  117.9 5.5 %fusion.44 = f32[128,2688]{1,0:T(8,128)} fusion(bf16[2688,1024]{1,0:T(8,128)(2,1)} %all-gather.4.cloned.1.call-done, bf16[256,1024]{1,0:T(8,128)(2,1)S(1)} %multiply_convert_fusion.1, s32[]{:T(128)S(6)} %select_n.142), kind=kOutput, calls=%fused_computation.76 | convolution fusion | flops 704643072 | bytes 7143428 | tf_op jit(solution)/shard_map/dot_general | solution.py:350
  123.9 3.0 collective-permute-done.6
  126.9 4.6 %multiply_reduce_fusion = (f32[128]{0:T(128)S(1)}, f32[128,2688]{1,0:T(8,128)S(1)}) fusion(f32[128,2688]{1,0:T(8,128)S(1)} %collective-permute-done.6, bf16[2688,1024]{1,0:T(8,128)(2,1)} %all-gather.4.cloned.1.call-done, bf16[256,1024]{1,0:T(8,128)(2,1)S(1)} %multiply_convert_fusion.1, s32[]{:T(128)S(6)} %select_n.141, bf16[128,2688]{1,0:T(8,128)(2,1)S(1)} %copy-done.17), kind=kOutput, calls=%fused_computation.28 | convolution fusion | flops 707051392 | bytes 9208324 | tf_op jit(solution)/shard_map/dot_general | solution.py:350
  131.9 0.7 collective-permute-start.12
  132.6 15.9 %collective-permute-done.11.refs_1_ = bf16[128,2688]{1,0:T(8,128)(2,1)S(1)} collective-permute-done((bf16[128,2688]{1,0:T(8,128)(2,1)S(1)}, bf16[128,2688]{1,0:T(8,128)(2,1)S(1)}, u32[]{:S(2)}, u32[]{:S(2)}) %collective-permute-start.11) | collective-permute-done | bytes 688160 | tf_op jit(solution)/shard_map/ppermute | solution.py:204
  148.6 1.1 collective-permute-start.13
  149.7 0.8 copy-done.8
  150.7 0.8 constant_dynamic-slice_fusion
  152.6 3.5 %collective-permute-start.27 = (bf16[128,2688]{1,0:T(8,128)(2,1)S(1)}, bf16[128,2688]{1,0:T(8,128)(2,1)S(1)}, u32[]{:S(2)}, u32[]{:S(2)}) collective-permute-start(bf16[128,2688]{1,0:T(8,128)(2,1)S(1)} %multiply_convert_fusion.refs_0_), channel_id=1, source_target_pairs={{0,8},{2,10},{4,12},{6,14},{8,0},{10,2},{12,4},{14,6},{1,9},{3,11}... | collective-permute-start | bytes 2064392 | tf_op jit(solution)/shard_map/ppermute | solution.py:212
  156.1 0.9 copy-done.10
  157.0 2.4 copy-done.2
  159.4 1.1 copy-done.9
  160.5 1.1 copy-done.11
  161.6 9.8 %shard_map.163 = (bf16[128,2688]{1,0:T(8,128)(2,1)S(1)}, bf16[128,2688]{1,0:T(8,128)(2,1)S(1)}, bf16[128,2688]{1,0:T(8,128)(2,1)S(1)}, bf16[128,2688]{1,0:T(8,128)(2,1)}) custom-call(f32[512,1]{1,0:T(8,128)S(1)} %copy.107.gate_ref, bf16[128,2688]{1,0:T(8,128)(2,1)S(1)} %multiply_convert_fusion.refs_0_, bf16[128,2688]{1,0:T(8,128)(2,1)S(1)} %copy-done.9, ...), custom_call_target="tpu_custom_call" | custom-call | flops 5108662272 | bytes 15482880 | tf_op jit(solution)/shard_map/pallas_call | solution.py:181
  171.4 0.8 copy-done.5
  173.1 1.5 collective-permute-start.20
  174.5 25.9 %collective-permute-done.27.refs_0_ = bf16[128,2688]{1,0:T(8,128)(2,1)S(1)} collective-permute-done((bf16[128,2688]{1,0:T(8,128)(2,1)S(1)}, bf16[128,2688]{1,0:T(8,128)(2,1)S(1)}, u32[]{:S(2)}, u32[]{:S(2)}) %collective-permute-start.27) | collective-permute-done | bytes 688160 | tf_op jit(solution)/shard_map/ppermute | solution.py:212
  200.5 1.1 collective-permute-start.10
  201.6 2.1 add_convert_fusion.8
  203.7 2.4 copy-done.3
  206.1 10.0 %shard_map.164 = (bf16[128,2688]{1,0:T(8,128)(2,1)S(1)}, bf16[128,2688]{1,0:T(8,128)(2,1)S(1)}, bf16[128,2688]{1,0:T(8,128)(2,1)S(1)}, bf16[128,2688]{1,0:T(8,128)(2,1)}) custom-call(f32[512,1]{1,0:T(8,128)S(1)} %copy.108.gate_ref, bf16[128,2688]{1,0:T(8,128)(2,1)} %collective-permute-done.7.refs_0_, bf16[128,2688]{1,0:T(8,128)(2,1)} %collective-permute-done.8.refs_1_, ...), custom_call_target="tpu_custom_call" | custom-call | flops 5108662272 | bytes 15482880 | tf_op jit(solution)/shard_map/pallas_call | solution.py:181
  216.1 0.8 copy-done.6
  218.6 0.8 collective-permute-done.16
  219.7 1.3 add_convert_fusion.7
  221.5 1.7 collective-permute-done.22.refs_3_
  223.3 2.4 copy-done.4
  225.7 9.3 %shard_map.165 = (bf16[128,2688]{1,0:T(8,128)(2,1)S(1)}, bf16[128,2688]{1,0:T(8,128)(2,1)S(1)}, bf16[128,2688]{1,0:T(8,128)(2,1)S(1)}, bf16[128,2688]{1,0:T(8,128)(2,1)S(1)}) custom-call(f32[512,1]{1,0:T(8,128)S(1)} %copy.109.gate_ref, bf16[128,2688]{1,0:T(8,128)(2,1)} %collective-permute-done.19.refs_0_, bf16[128,2688]{1,0:T(8,128)(2,1)} %collective-permute-done.20.refs_1_, ...), custom_call_target="tpu_custom_call" | custom-call | flops 5108662272 | bytes 15482880 | tf_op jit(solution)/shard_map/pallas_call | solution.py:181
  235.5 1.5 collective-permute-start.17
  237.7 1.4 collective-permute-start.25
  239.1 9.1 %shard_map.166 = (bf16[128,2688]{1,0:T(8,128)(2,1)S(1)}, bf16[128,2688]{1,0:T(8,128)(2,1)S(1)}, bf16[128,2688]{1,0:T(8,128)(2,1)S(1)}, bf16[128,2688]{1,0:T(8,128)(2,1)S(1)}) custom-call(f32[512,1]{1,0:T(8,128)S(1)} %copy.110.gate_ref, bf16[128,2688]{1,0:T(8,128)(2,1)S(1)} %collective-permute-done.27.refs_0_, ...), custom_call_target="tpu_custom_call" | custom-call | flops 5108662272 | bytes 15482880 | tf_op jit(solution)/shard_map/pallas_call | solution.py:181
  248.8 3.5 %collective-permute-done.17 = bf16[128,2688]{1,0:T(8,128)(2,1)S(1)} collective-permute-done((bf16[128,2688]{1,0:T(8,128)(2,1)S(1)}, bf16[128,2688]{1,0:T(8,128)(2,1)S(1)}, u32[]{:S(2)}, u32[]{:S(2)}) %collective-permute-start.17) | collective-permute-done | bytes 688160 | tf_op jit(solution)/shard_map/ppermute | solution.py:204
  252.7 1.9 collective-permute-start.31
  254.8 1.4 collective-permute-start.33
  256.3 10.8 %collective-permute-done.25 = bf16[128,2688]{1,0:T(8,128)(2,1)S(1)} collective-permute-done((bf16[128,2688]{1,0:T(8,128)(2,1)S(1)}, bf16[128,2688]{1,0:T(8,128)(2,1)S(1)}, u32[]{:S(2)}, u32[]{:S(2)}) %collective-permute-start.25) | collective-permute-done | bytes 688160 | tf_op jit(solution)/shard_map/ppermute | solution.py:204
  267.4 14.4 %collective-permute-done.33 = bf16[128,2688]{1,0:T(8,128)(2,1)S(1)} collective-permute-done((bf16[128,2688]{1,0:T(8,128)(2,1)S(1)}, bf16[128,2688]{1,0:T(8,128)(2,1)S(1)}, u32[]{:S(2)}, u32[]{:S(2)}) %collective-permute-start.33) | collective-permute-done | bytes 688160 | tf_op jit(solution)/shard_map/ppermute | solution.py:204
  282.1 0.8 copy-done.16
  282.9 1.4 collective-permute-start.36
  284.3 3.1 collective-permute-start.34
  287.4 0.8 collective-permute-done.26
  288.2 10.6 %collective-permute-done.36 = bf16[128,2688]{1,0:T(8,128)(2,1)S(1)} collective-permute-done((bf16[128,2688]{1,0:T(8,128)(2,1)S(1)}, bf16[128,2688]{1,0:T(8,128)(2,1)S(1)}, u32[]{:S(2)}, u32[]{:S(2)}) %collective-permute-start.36) | collective-permute-done | bytes 688160 | tf_op jit(solution)/shard_map/ppermute | solution.py:204
  298.7 17.3 %collective-permute-done.34 = bf16[128,2688]{1,0:T(8,128)(2,1)S(1)} collective-permute-done((bf16[128,2688]{1,0:T(8,128)(2,1)S(1)}, bf16[128,2688]{1,0:T(8,128)(2,1)S(1)}, u32[]{:S(2)}, u32[]{:S(2)}) %collective-permute-start.34) | collective-permute-done | bytes 688160 | tf_op jit(solution)/shard_map/ppermute | solution.py:212
  316.0 1.4 add_convert_fusion
  (155 shorter events, 14.4 us)
Async XLA Ops:
  6.5 8.7 %copy-start = (f32[256,16]{0,1:T(8,128)S(1)}, f32[256,16]{0,1:T(8,128)}, u32[]{:S(2)}) copy-start(f32[256,16]{0,1:T(8,128)} %param.21) | copy-start | bytes 49156
  6.5 29.7 %copy-start.19 = (bf16[256,2,256]{2,1,0:T(2,128)(2,1)S(1)}, bf16[256,2,256]{2,1,0:T(2,128)(2,1)}, u32[]{:S(2)}) copy-start(bf16[256,2,256]{2,1,0:T(2,128)(2,1)} %param.18) | copy-start | bytes 786436
  6.5 29.4 %copy-start.24 = (bf16[4,2,256]{2,1,0:T(2,128)(2,1)S(1)}, bf16[4,2,256]{2,1,0:T(2,128)(2,1)}, u32[]{:S(2)}) copy-start(bf16[4,2,256]{2,1,0:T(2,128)(2,1)} %param.23) | copy-start | bytes 12292
  6.5 29.5 %copy-start.21 = (bf16[4,1024]{1,0:T(4,128)(2,1)S(1)}, bf16[4,1024]{1,0:T(4,128)(2,1)}, u32[]{:S(2)}) copy-start(bf16[4,1024]{1,0:T(4,128)(2,1)} %param.22) | copy-start | bytes 24580
  6.5 29.6 %copy-start.22 = (f32[256,16]{0,1:T(8,128)S(1)}, f32[256,16]{0,1:T(8,128)}, u32[]{:S(2)}) copy-start(f32[256,16]{0,1:T(8,128)} %param.20) | copy-start | bytes 49156
  6.5 111.4 %all-gather.4.cloned.1.call-start = ((), (), s32[]{:S(2)}) async-start(), calls=%async_computation | async-start | bytes 6193152 | tf_op jit(solution)/shard_map/all_gather | solution.py:281
  8.0 29.5 %collective-permute-start = (bf16[3,1024]{1,0:T(4,128)(2,1)S(1)}, bf16[3,1024]{1,0:T(4,128)(2,1)S(1)}, u32[]{:S(2)}, u32[]{:S(2)}) collective-permute-start(bf16[3,1024]{1,0:T(4,128)(2,1)S(1)} %slice.93), channel_id=1, source_target_pairs={{0,2},{2,4},{4,6},{6,8},{8,10},{10,12},{12,14},{1,3},{3,5},{5,7},{... | collective-permute-start | bytes 18440 | tf_op jit(solution)/shard_map/ppermute | solution.py:24
  12.0 24.5 %collective-permute-start.1 = (bf16[3,2,256]{0,2,1:T(8,128)(2,1)S(1)}, bf16[3,2,256]{0,2,1:T(8,128)(2,1)S(1)}, u32[]{:S(2)}, u32[]{:S(2)}) collective-permute-start(bf16[3,2,256]{0,2,1:T(8,128)(2,1)S(1)} %copy.97), channel_id=1, source_target_pairs={{0,2},{2,4},{4,6},{6,8},{8,10},{10,12},{12,14},{1,3},{3,5},{5,7},{... | collective-permute-start | bytes 9224 | tf_op jit(solution)/shard_map/ppermute | solution.py:24
  36.7 1.0 copy-start.18
  38.6 2.2 copy-start.14
  38.8 3.2 copy-start.27
  38.8 3.9 %copy-start.25 = (bf16[1024]{0:T(1024)(128)(2,1)S(1)}, bf16[1024]{0:T(1024)(128)(2,1)}, u32[]{:S(2)}) copy-start(bf16[1024]{0:T(1024)(128)(2,1)} %param.26) | copy-start | bytes 6148
  39.5 7.8 %collective-permute-start.2 = (bf16[2,8,64,128]{3,2,1,0:T(8,128)(2,1)S(1)}, bf16[2,8,64,128]{3,2,1,0:T(8,128)(2,1)S(1)}, u32[]{:S(2)}, u32[]{:S(2)}) collective-permute-start(bf16[2,8,64,128]{3,2,1,0:T(8,128)(2,1)S(1)} %get-tuple-element.86), channel_id=1, source_target_pairs={{0,2},{2,0},{4,6},{6,4},{8,10},{10,8},{12,14},{14,12},{1,3},{3,1},... | collective-permute-start | bytes 786440 | tf_op jit(solution)/shard_map/ppermute | solution.py:37
  47.5 10.7 %collective-permute-start.3 = (bf16[2,8,64,128]{3,2,1,0:T(8,128)(2,1)S(1)}, bf16[2,8,64,128]{3,2,1,0:T(8,128)(2,1)S(1)}, u32[]{:S(2)}, u32[]{:S(2)}) collective-permute-start(bf16[2,8,64,128]{3,2,1,0:T(8,128)(2,1)S(1)} %fusion.33), channel_id=1, source_target_pairs={{0,12},{2,14},{1,13},{3,15},{16,28},{18,30},{17,29},{19,31}} | collective-permute-start | bytes 786440 | tf_op jit(solution)/shard_map/ppermute | solution.py:24
  48.2 34.0 %collective-permute-start.4 = (bf16[2,8,64,128]{3,2,1,0:T(8,128)(2,1)S(1)}, bf16[2,8,64,128]{3,2,1,0:T(8,128)(2,1)S(1)}, u32[]{:S(2)}, u32[]{:S(2)}) collective-permute-start(bf16[2,8,64,128]{3,2,1,0:T(8,128)(2,1)S(1)} %fusion.33), channel_id=1, source_target_pairs={{0,8},{2,10},{4,12},{6,14},{1,9},{3,11},{5,13},{7,15},{16,24},{18,... | collective-permute-start | bytes 786440 | tf_op jit(solution)/shard_map/ppermute | solution.py:24
  52.6 48.6 %collective-permute-start.5 = (bf16[2,8,64,128]{3,2,1,0:T(8,128)(2,1)S(1)}, bf16[2,8,64,128]{3,2,1,0:T(8,128)(2,1)S(1)}, u32[]{:S(2)}, u32[]{:S(2)}) collective-permute-start(bf16[2,8,64,128]{3,2,1,0:T(8,128)(2,1)S(1)} %fusion.33), channel_id=1, source_target_pairs={{0,4},{2,6},{4,8},{6,10},{8,12},{10,14},{1,5},{3,7},{5,9},{7,11},{... | collective-permute-start | bytes 786440 | tf_op jit(solution)/shard_map/ppermute | solution.py:24
  54.8 46.5 %copy-start.15 = (f32[256,1024]{0,1:T(8,128)S(1)}, f32[256,1024]{0,1:T(8,128)}, u32[]{:S(2)}) copy-start(f32[256,1024]{0,1:T(8,128)} %copy.105) | copy-start | bytes 3145732
  54.8 46.5 %copy-start.26 = (bf16[16,64,128]{2,1,0:T(8,128)(2,1)S(1)}, bf16[16,64,128]{2,1,0:T(8,128)(2,1)}, u32[]{:S(2)}) copy-start(bf16[16,64,128]{2,1,0:T(8,128)(2,1)} %param.25) | copy-start | bytes 786436
  54.8 46.5 %copy-start.28 = (f32[2,8]{1,0:T(2,128)S(1)}, f32[2,8]{1,0:T(2,128)}, u32[]{:S(2)}) copy-start(f32[2,8]{1,0:T(2,128)} %mul.362) | copy-start | bytes 196
  106.1 17.8 %copy-start.23 = (bf16[2688]{0:T(1024)(128)(2,1)S(1)}, bf16[2688]{0:T(1024)(128)(2,1)}, u32[]{:S(2)}) copy-start(bf16[2688]{0:T(1024)(128)(2,1)} %param.29) | copy-start | bytes 16132
  106.1 20.7 %copy-start.17 = (bf16[128,2688]{1,0:T(8,128)(2,1)S(1)}, bf16[128,2688]{1,0:T(8,128)(2,1)}, u32[]{:S(2)}) copy-start(bf16[128,2688]{1,0:T(8,128)(2,1)} %param.28) | copy-start | bytes 2064388
  123.5 3.4 %collective-permute-start.6 = (f32[128,2688]{1,0:T(8,128)}, f32[128,2688]{1,0:T(8,128)S(1)}, u32[]{:S(2)}, u32[]{:S(2)}) collective-permute-start(f32[128,2688]{1,0:T(8,128)} %fusion.44), channel_id=1, source_target_pairs={{0,1},{1,0},{2,3},{3,2},{4,5},{5,4},{6,7},{7,6},{8,9},{9,8},{10,11... | collective-permute-start | bytes 4128776 | tf_op jit(solution)/shard_map/ppermute | solution.py:352
  131.5 18.1 %copy-start.12 = (f32[128,2688]{1,0:T(8,128)}, f32[128,2688]{1,0:T(8,128)S(1)}, u32[]{:S(2)}) copy-start(f32[128,2688]{1,0:T(8,128)S(1)} %get-tuple-element.91) | copy-start | bytes 4128772
  131.7 16.8 %collective-permute-start.11 = (bf16[128,2688]{1,0:T(8,128)(2,1)S(1)}, bf16[128,2688]{1,0:T(8,128)(2,1)S(1)}, u32[]{:S(2)}, u32[]{:S(2)}) collective-permute-start(bf16[128,2688]{1,0:T(8,128)(2,1)S(1)} %multiply_convert_fusion.refs_0_), channel_id=1, source_target_pairs={{0,2},{2,0},{4,6},{6,4},{8,10},{10,8},{12,14},{14,12},{1,3},{3,1},... | collective-permute-start | bytes 2064392 | tf_op jit(solution)/shard_map/ppermute | solution.py:204
  131.9 24.2 %collective-permute-start.12 = (bf16[128,2688]{1,0:T(8,128)(2,1)S(1)}, bf16[128,2688]{1,0:T(8,128)(2,1)S(1)}, u32[]{:S(2)}, u32[]{:S(2)}) collective-permute-start(bf16[128,2688]{1,0:T(8,128)(2,1)S(1)} %multiply_convert_fusion.refs_0_), channel_id=1, source_target_pairs={{0,1},{1,0},{2,3},{3,2},{4,5},{5,4},{6,7},{7,6},{8,9},{9,8},{10,11... | collective-permute-start | bytes 2064392 | tf_op jit(solution)/shard_map/ppermute | solution.py:204
  132.6 23.4 %collective-permute-start.7 = (bf16[128,2688]{1,0:T(8,128)(2,1)S(1)}, bf16[128,2688]{1,0:T(8,128)(2,1)}, u32[]{:S(2)}, u32[]{:S(2)}) collective-permute-start(bf16[128,2688]{1,0:T(8,128)(2,1)S(1)} %multiply_convert_fusion.refs_0_), channel_id=1, source_target_pairs={{0,4},{2,6},{4,8},{6,10},{8,12},{10,14},{12,0},{14,2},{1,5},{3,7},... | collective-permute-start | bytes 2064392 | tf_op jit(solution)/shard_map/ppermute | solution.py:212
  148.6 8.4 %collective-permute-start.13 = (bf16[128,2688]{1,0:T(8,128)(2,1)S(1)}, bf16[128,2688]{1,0:T(8,128)(2,1)}, u32[]{:S(2)}, u32[]{:S(2)}) collective-permute-start(bf16[128,2688]{1,0:T(8,128)(2,1)S(1)} %collective-permute-done.11.refs_1_), channel_id=1, source_target_pairs={{0,1},{1,0},{2,3},{3,2},{4,5},{5,4},{6,7},{7,6},{8,9},{9,8},{10,11... | collective-permute-start | bytes 2064392 | tf_op jit(solution)/shard_map/ppermute | solution.py:204
  152.3 20.8 %collective-permute-start.19 = (bf16[128,2688]{1,0:T(8,128)(2,1)S(1)}, bf16[128,2688]{1,0:T(8,128)(2,1)}, u32[]{:S(2)}, u32[]{:S(2)}) collective-permute-start(bf16[128,2688]{1,0:T(8,128)(2,1)S(1)} %multiply_convert_fusion.refs_0_), channel_id=1, source_target_pairs={{0,12},{2,14},{4,0},{6,2},{8,4},{10,6},{12,8},{14,10},{1,13},{3,15... | collective-permute-start | bytes 2064392 | tf_op jit(solution)/shard_map/ppermute | solution.py:212
  152.6 47.9 %collective-permute-start.27 = (bf16[128,2688]{1,0:T(8,128)(2,1)S(1)}, bf16[128,2688]{1,0:T(8,128)(2,1)S(1)}, u32[]{:S(2)}, u32[]{:S(2)}) collective-permute-start(bf16[128,2688]{1,0:T(8,128)(2,1)S(1)} %multiply_convert_fusion.refs_0_), channel_id=1, source_target_pairs={{0,8},{2,10},{4,12},{6,14},{8,0},{10,2},{12,4},{14,6},{1,9},{3,11}... | collective-permute-start | bytes 2064392 | tf_op jit(solution)/shard_map/ppermute | solution.py:212
  156.1 44.4 %collective-permute-start.8 = (bf16[128,2688]{1,0:T(8,128)(2,1)}, bf16[128,2688]{1,0:T(8,128)(2,1)}, u32[]{:S(2)}, u32[]{:S(2)}) collective-permute-start(bf16[128,2688]{1,0:T(8,128)(2,1)} %collective-permute-done.7.refs_0_), channel_id=1, source_target_pairs={{0,2},{2,0},{4,6},{6,4},{8,10},{10,8},{12,14},{14,12},{1,3},{3,1},... | collective-permute-start | bytes 2064392 | tf_op jit(solution)/shard_map/ppermute | solution.py:204
  156.1 0.9 copy-start.10
  157.0 2.4 copy-start.2
  159.4 1.1 copy-start.9
  160.5 1.1 copy-start.11
  172.3 29.3 %collective-permute-start.14 = (bf16[128,2688]{1,0:T(8,128)(2,1)}, bf16[128,2688]{1,0:T(8,128)(2,1)}, u32[]{:S(2)}, u32[]{:S(2)}) collective-permute-start(bf16[128,2688]{1,0:T(8,128)(2,1)} %get-tuple-element.36), channel_id=1, source_target_pairs={{0,1},{1,0},{2,3},{3,2},{4,5},{5,4},{6,7},{7,6},{8,9},{9,8},{10,11... | collective-permute-start | bytes 2064392 | tf_op jit(solution)/shard_map/ppermute | solution.py:204
  173.0 30.7 %collective-permute-start.9 = (bf16[128,2688]{1,0:T(8,128)(2,1)}, bf16[128,2688]{1,0:T(8,128)(2,1)S(1)}, u32[]{:S(2)}, u32[]{:S(2)}) collective-permute-start(bf16[128,2688]{1,0:T(8,128)(2,1)} %collective-permute-done.7.refs_0_), channel_id=1, source_target_pairs={{0,1},{1,0},{2,3},{3,2},{4,5},{5,4},{6,7},{7,6},{8,9},{9,8},{10,11... | collective-permute-start | bytes 2064392 | tf_op jit(solution)/shard_map/ppermute | solution.py:204
  173.1 45.0 %collective-permute-start.20 = (bf16[128,2688]{1,0:T(8,128)(2,1)}, bf16[128,2688]{1,0:T(8,128)(2,1)}, u32[]{:S(2)}, u32[]{:S(2)}) collective-permute-start(bf16[128,2688]{1,0:T(8,128)(2,1)} %collective-permute-done.19.refs_0_), channel_id=1, source_target_pairs={{0,2},{2,0},{4,6},{6,4},{8,10},{10,8},{12,14},{14,12},{1,3},{3,1},... | collective-permute-start | bytes 2064392 | tf_op jit(solution)/shard_map/ppermute | solution.py:204
  200.4 18.0 %collective-permute-start.28 = (bf16[128,2688]{1,0:T(8,128)(2,1)S(1)}, bf16[128,2688]{1,0:T(8,128)(2,1)}, u32[]{:S(2)}, u32[]{:S(2)}) collective-permute-start(bf16[128,2688]{1,0:T(8,128)(2,1)S(1)} %collective-permute-done.27.refs_0_), channel_id=1, source_target_pairs={{0,2},{2,0},{4,6},{6,4},{8,10},{10,8},{12,14},{14,12},{1,3},{3,1},... | collective-permute-start | bytes 2064392 | tf_op jit(solution)/shard_map/ppermute | solution.py:204
  200.5 3.2 collective-permute-start.10
  203.7 2.4 copy-start.3
  216.1 0.9 copy-start.6
  217.0 2.5 collective-permute-start.16
  217.5 3.8 %copy-start.7 = (bf16[128,2688]{1,0:T(8,128)(2,1)S(1)}, bf16[128,2688]{1,0:T(8,128)(2,1)}, u32[]{:S(2)}) copy-start(bf16[128,2688]{1,0:T(8,128)(2,1)} %copy-done.6) | copy-start | bytes 2064388
  217.5 3.8 %collective-permute-start.21 = (bf16[128,2688]{1,0:T(8,128)(2,1)}, bf16[128,2688]{1,0:T(8,128)(2,1)S(1)}, u32[]{:S(2)}, u32[]{:S(2)}) collective-permute-start(bf16[128,2688]{1,0:T(8,128)(2,1)} %collective-permute-done.19.refs_0_), channel_id=1, source_target_pairs={{0,1},{1,0},{2,3},{3,2},{4,5},{5,4},{6,7},{7,6},{8,9},{9,8},{10,11... | collective-permute-start | bytes 2064392 | tf_op jit(solution)/shard_map/ppermute | solution.py:204
  217.9 19.9 %collective-permute-start.29 = (bf16[128,2688]{1,0:T(8,128)(2,1)S(1)}, bf16[128,2688]{1,0:T(8,128)(2,1)S(1)}, u32[]{:S(2)}, u32[]{:S(2)}) collective-permute-start(bf16[128,2688]{1,0:T(8,128)(2,1)S(1)} %collective-permute-done.27.refs_0_), channel_id=1, source_target_pairs={{0,1},{1,0},{2,3},{3,2},{4,5},{5,4},{6,7},{7,6},{8,9},{9,8},{10,11... | collective-permute-start | bytes 2064392 | tf_op jit(solution)/shard_map/ppermute | solution.py:204
  218.1 17.2 %collective-permute-start.35 = (bf16[128,2688]{1,0:T(8,128)(2,1)}, bf16[128,2688]{1,0:T(8,128)(2,1)S(1)}, u32[]{:S(2)}, u32[]{:S(2)}) collective-permute-start(bf16[128,2688]{1,0:T(8,128)(2,1)} %copy-done.5), channel_id=1, source_target_pairs={{0,1},{1,0},{2,3},{3,2},{4,5},{5,4},{6,7},{7,6},{8,9},{9,8},{10,11... | collective-permute-start | bytes 2064392 | tf_op jit(solution)/shard_map/ppermute | solution.py:204
  218.4 4.9 %collective-permute-start.22 = (bf16[128,2688]{1,0:T(8,128)(2,1)}, bf16[128,2688]{1,0:T(8,128)(2,1)S(1)}, u32[]{:S(2)}, u32[]{:S(2)}) collective-permute-start(bf16[128,2688]{1,0:T(8,128)(2,1)} %collective-permute-done.20.refs_1_), channel_id=1, source_target_pairs={{0,1},{1,0},{2,3},{3,2},{4,5},{5,4},{6,7},{7,6},{8,9},{9,8},{10,11... | collective-permute-start | bytes 2064392 | tf_op jit(solution)/shard_map/ppermute | solution.py:204
  219.5 19.6 %collective-permute-start.30 = (bf16[128,2688]{1,0:T(8,128)(2,1)}, bf16[128,2688]{1,0:T(8,128)(2,1)S(1)}, u32[]{:S(2)}, u32[]{:S(2)}) collective-permute-start(bf16[128,2688]{1,0:T(8,128)(2,1)} %collective-permute-done.28.refs_1_), channel_id=1, source_target_pairs={{0,1},{1,0},{2,3},{3,2},{4,5},{5,4},{6,7},{7,6},{8,9},{9,8},{10,11... | collective-permute-start | bytes 2064392 | tf_op jit(solution)/shard_map/ppermute | solution.py:204
  221.3 27.5 %collective-permute-start.15 = (bf16[128,2688]{1,0:T(8,128)(2,1)S(1)}, bf16[128,2688]{1,0:T(8,128)(2,1)S(1)}, u32[]{:S(2)}, u32[]{:S(2)}) collective-permute-start(bf16[128,2688]{1,0:T(8,128)(2,1)S(1)} %copy-done.7), channel_id=1, source_target_pairs={{0,1},{1,0},{2,3},{3,2},{4,5},{5,4},{6,7},{7,6},{8,9},{9,8},{10,11... | collective-permute-start | bytes 2064392 | tf_op jit(solution)/shard_map/ppermute | solution.py:204
  223.3 2.4 copy-start.4
  235.0 2.2 collective-permute-start.24
  235.5 16.8 %collective-permute-start.17 = (bf16[128,2688]{1,0:T(8,128)(2,1)S(1)}, bf16[128,2688]{1,0:T(8,128)(2,1)S(1)}, u32[]{:S(2)}, u32[]{:S(2)}) collective-permute-start(bf16[128,2688]{1,0:T(8,128)(2,1)S(1)} %add_convert_fusion.7), channel_id=1, source_target_pairs={{0,2},{2,0},{4,6},{6,4},{8,10},{10,8},{12,14},{14,12},{1,3},{3,1},... | collective-permute-start | bytes 2064392 | tf_op jit(solution)/shard_map/ppermute | solution.py:204
  237.2 19.1 %collective-permute-start.23 = (bf16[128,2688]{1,0:T(8,128)(2,1)S(1)}, bf16[128,2688]{1,0:T(8,128)(2,1)S(1)}, u32[]{:S(2)}, u32[]{:S(2)}) collective-permute-start(bf16[128,2688]{1,0:T(8,128)(2,1)S(1)} %get-tuple-element.50), channel_id=1, source_target_pairs={{0,1},{1,0},{2,3},{3,2},{4,5},{5,4},{6,7},{7,6},{8,9},{9,8},{10,11... | collective-permute-start | bytes 2064392 | tf_op jit(solution)/shard_map/ppermute | solution.py:204
  237.7 29.3 %collective-permute-start.25 = (bf16[128,2688]{1,0:T(8,128)(2,1)S(1)}, bf16[128,2688]{1,0:T(8,128)(2,1)S(1)}, u32[]{:S(2)}, u32[]{:S(2)}) collective-permute-start(bf16[128,2688]{1,0:T(8,128)(2,1)S(1)} %add_convert_fusion.5), channel_id=1, source_target_pairs={{0,2},{2,0},{4,6},{6,4},{8,10},{10,8},{12,14},{14,12},{1,3},{3,1},... | collective-permute-start | bytes 2064392 | tf_op jit(solution)/shard_map/ppermute | solution.py:204
  248.2 6.4 %collective-permute-start.32 = (bf16[128,2688]{1,0:T(8,128)(2,1)S(1)}, bf16[128,2688]{1,0:T(8,128)(2,1)S(1)}, u32[]{:S(2)}, u32[]{:S(2)}) collective-permute-start(bf16[128,2688]{1,0:T(8,128)(2,1)S(1)} %get-tuple-element.60), channel_id=1, source_target_pairs={{0,1},{1,0},{2,3},{3,2},{4,5},{5,4},{6,7},{7,6},{8,9},{9,8},{10,11... | collective-permute-start | bytes 2064392 | tf_op jit(solution)/shard_map/ppermute | solution.py:204
  252.6 34.8 %collective-permute-start.18 = (bf16[128,2688]{1,0:T(8,128)(2,1)S(1)}, bf16[128,2688]{1,0:T(8,128)(2,1)S(1)}, u32[]{:S(2)}, u32[]{:S(2)}) collective-permute-start(bf16[128,2688]{1,0:T(8,128)(2,1)S(1)} %add_convert_fusion.6), channel_id=1, source_target_pairs={{0,12},{2,14},{4,0},{6,2},{8,4},{10,6},{12,8},{14,10},{1,13},{3,15... | collective-permute-start | bytes 2064392 | tf_op jit(solution)/shard_map/ppermute | solution.py:212
  252.7 14.7 %collective-permute-start.31 = (bf16[128,2688]{1,0:T(8,128)(2,1)S(1)}, bf16[128,2688]{1,0:T(8,128)(2,1)S(1)}, u32[]{:S(2)}, u32[]{:S(2)}) collective-permute-start(bf16[128,2688]{1,0:T(8,128)(2,1)S(1)} %get-tuple-element.58), channel_id=1, source_target_pairs={{0,1},{1,0},{2,3},{3,2},{4,5},{5,4},{6,7},{7,6},{8,9},{9,8},{10,11... | collective-permute-start | bytes 2064392 | tf_op jit(solution)/shard_map/ppermute | solution.py:204
  254.8 27.0 %collective-permute-start.33 = (bf16[128,2688]{1,0:T(8,128)(2,1)S(1)}, bf16[128,2688]{1,0:T(8,128)(2,1)S(1)}, u32[]{:S(2)}, u32[]{:S(2)}) collective-permute-start(bf16[128,2688]{1,0:T(8,128)(2,1)S(1)} %add_convert_fusion.3), channel_id=1, source_target_pairs={{0,2},{2,0},{4,6},{6,4},{8,10},{10,8},{12,14},{14,12},{1,3},{3,1},... | collective-permute-start | bytes 2064392 | tf_op jit(solution)/shard_map/ppermute | solution.py:204
  267.4 20.8 %collective-permute-start.26 = (bf16[128,2688]{1,0:T(8,128)(2,1)S(1)}, bf16[128,2688]{1,0:T(8,128)(2,1)S(1)}, u32[]{:S(2)}, u32[]{:S(2)}) collective-permute-start(bf16[128,2688]{1,0:T(8,128)(2,1)S(1)} %add_convert_fusion.4), channel_id=1, source_target_pairs={{0,4},{2,6},{4,8},{6,10},{8,12},{10,14},{12,0},{14,2},{1,5},{3,7},... | collective-permute-start | bytes 2064392 | tf_op jit(solution)/shard_map/ppermute | solution.py:212
  281.8 1.1 copy-start.16
  281.8 34.2 %copy-start.13 = (f32[128,2688]{1,0:T(8,128)S(1)}, f32[128,2688]{1,0:T(8,128)}, u32[]{:S(2)}) copy-start(f32[128,2688]{1,0:T(8,128)} %copy-done.12) | copy-start | bytes 4128772
  282.9 15.8 %collective-permute-start.36 = (bf16[128,2688]{1,0:T(8,128)(2,1)S(1)}, bf16[128,2688]{1,0:T(8,128)(2,1)S(1)}, u32[]{:S(2)}, u32[]{:S(2)}) collective-permute-start(bf16[128,2688]{1,0:T(8,128)(2,1)S(1)} %copy-done.16), channel_id=1, source_target_pairs={{0,2},{2,0},{4,6},{6,4},{8,10},{10,8},{12,14},{14,12},{1,3},{3,1},... | collective-permute-start | bytes 2064392 | tf_op jit(solution)/shard_map/ppermute | solution.py:204
  284.3 31.7 %collective-permute-start.34 = (bf16[128,2688]{1,0:T(8,128)(2,1)S(1)}, bf16[128,2688]{1,0:T(8,128)(2,1)S(1)}, u32[]{:S(2)}, u32[]{:S(2)}) collective-permute-start(bf16[128,2688]{1,0:T(8,128)(2,1)S(1)} %add_convert_fusion.2), channel_id=1, source_target_pairs={{0,8},{2,10},{4,12},{6,14},{8,0},{10,2},{12,4},{14,6},{1,9},{3,11}... | collective-permute-start | bytes 2064392 | tf_op jit(solution)/shard_map/ppermute | solution.py:212
  316.0 1.4 copy-start.1
  (3 other events, 2.4 us)
Sparse Core Ops, SparseCore 0:
  9.6 108.3 all-gather.3
